TPU v7x, 256 devices: a whole 4x4x8 slice. The times are simulated.
256 devices in a mesh: member: 32 (over z, x_hi, core), row: 4 (over y), col: 2 (over x_lo).
Axes of the slice: x: 4 (x_hi: 2, x_lo: 2; x = x_hi * 2 + x_lo), y: 4, z: 8, core: 2. Of those that a mesh axis runs over, the one named last changes fastest.
Arguments:
- pert: bfloat16 [32, 3, 2, 64, 1024], P('member', None, None, 'row', 'col'), may hold values from -6 to 6
- probes: bfloat16 [32, 3, 2, 64, 1024], P('member', None, None, 'row', 'col'), may hold values from -6 to 6
- diff_class: int32 [64, 1024], P('row', 'col'), may hold values from 0 to 7
- class_rate: float32 [8], replicated, may hold values from 0.03 to 0.24
Outputs:
- cov_probe: float32 [32, 3, 2, 64, 1024], P('member', None, None, 'row', 'col')
All inputs are finite; a program needn't handle non-finite values.
Results may differ from a plain program's by a relative error of at most 0.0018.
Values may be sent and summed in bfloat16 or wider, within the bound.
No kernel may reach another device: no remote copies, remote signals or barrier semaphores. Data moves between devices by JAX's collectives and lax.ppermute only.
A program may use at most 128 MiB of HBM per device.

v0:
```python
import jax
import jax.numpy as jnp
from jax import lax
from jax.sharding import PartitionSpec as P

SWEEPS = 4


def extended(cells, sides, width):
    for axis, dim in sides:
        count = lax.axis_size(axis)
        ends = count - 1
        head = lax.slice_in_dim(cells, 0, width, axis=dim)
        tail = lax.slice_in_dim(cells, cells.shape[dim] - width, cells.shape[dim], axis=dim)
        cells = jnp.concatenate(
            [
                lax.ppermute(tail, axis, [(i, (i + 1) % count) for i in range(ends)]),
                cells,
                lax.ppermute(head, axis, [((i + 1) % count, i) for i in range(ends)]),
            ],
            axis=dim,
        )
    return cells


def class_rates(diff_class, class_rate):
    levels = jnp.arange(class_rate.shape[0], dtype=jnp.int32)
    picked = (diff_class[..., None] == levels).astype(jnp.float32)
    return jnp.sum(picked * class_rate, axis=-1)


def body(pert, probes, diff_class, class_rate):
    cell_rate = class_rates(diff_class, class_rate)
    mem_local = pert.shape[0]
    total_members = mem_local * lax.axis_size("member")
    all_probes = lax.all_gather(probes, "member", axis=0, tiled=True)
    field_now = pert[:, None].astype(jnp.float32) * all_probes[None].astype(jnp.float32)
    for sweep_index in range(SWEEPS):
        padded = extended(field_now.astype(jnp.bfloat16), (("row", 4), ("col", 5)), 1).astype(
            field_now.dtype
        )
        beside_all = (
            padded[..., 2:, 1:-1]
            + padded[..., :-2, 1:-1]
            + padded[..., 1:-1, 2:]
            + padded[..., 1:-1, :-2]
        )
        field_now = field_now + cell_rate * (beside_all - 4.0 * field_now)
    member_terms = jnp.sum(pert[:, None].astype(jnp.float32) * field_now, axis=0)
    summed = lax.psum_scatter(member_terms, "member", scatter_dimension=0, tiled=True)
    return summed / (total_members - 1)


def solution(mesh):
    placed = (
        P("member", None, None, "row", "col"),
        P("member", None, None, "row", "col"),
        P("row", "col"),
        P(),
    )
    return jax.shard_map(
        body,
        mesh=mesh,
        in_specs=placed,
        out_specs=P("member", None, None, "row", "col"),
        check_vma=False,
    )
```

profile of v0, /device:TPU:1, one launch (start us, length us, event | category | flops | bytes accessed | tf_op | source)
XLA Modules:
  0.0 485.1 jit_solution(526615699143542016)
XLA Ops:
  8.2 89.1 %all-gather.2.cloned.1.call-done = bf16[32,3,2,16,512]{4,3,2,1,0:T(8,128)(2,1)} async-done(((bf16[1,3,2,16,512]{4,3,2,1,0:T(8,128)(2,1)}), bf16[32,3,2,16,512]{4,3,2,1,0:T(8,128)(2,1)}) %all-gather.2.cloned.1.call-update) | async-done | bytes 3145744 | tf_op jit(solution)/shard_map/all_gather | solution.py:36
  97.3 2.8 fusion.15
  100.7 3.1 collective-permute-start
  105.2 6.9 %collective-permute-done = bf16[1,32,3,2,1,512]{5,4,3,2,1,0:T(2,128)(2,1)S(1)} collective-permute-done((bf16[1,32,3,2,1,512]{5,4,3,2,1,0:T(2,128)(2,1)S(1)}, bf16[1,32,3,2,1,512]{5,4,3,2,1,0:T(2,128)(2,1)S(1)}, u32[]{:S(2)}, u32[]{:S(2)}) %collective-permute-start) | collective-permute-done | bytes 196640 | tf_op jit(solution)/shard_map/ppermute | solution.py:17
  112.0 3.9 collective-permute-done.1
  115.9 3.0 pad_maximum_fusion.11
  118.9 2.1 copy.21
  121.0 2.1 copy.22
  124.3 4.2 collective-permute-start.2
  129.3 2.0 copy.23
  131.3 2.0 copy.24
  133.3 10.4 %maximum_convert_fusion = f32[1,32,3,2,18,514]{5,4,3,2,1,0:T(8,128)} fusion(bf16[1,32,3,2,18,1]{5,4,3,2,1,0:T(8,128)(2,1)} %copy.24, bf16[1,32,3,2,1,512]{5,4,3,2,1,0:T(2,128)(2,1)} %copy-done.4, bf16[1,32,3,2,16,512]{5,4,3,2,1,0:T(8,128)(2,1)S(1)} %fusion.15, bf16[1,32,3,2,1,512]{5,4,3,2,1,0:T(2,128)(2,1)} %copy-done, bf16[1,32,3,2,18,1]{5,4,3,2,1,0:T(8,128)(2,1)} %copy.23), kind=kLoop, calls=%fused_computation.28 | loop fusion | flops 17763840 | bytes 10658304 | tf_op jit(solution)/shard_map/convert_element_type | solution.py:39
  143.7 19.1 %fusion.20 = (bf16[1,32,3,2,16,512]{5,4,3,2,1,0:T(8,128)(2,1)S(1)}, f32[1,32,3,2,16,512]{5,4,3,2,1,0:T(8,128)}) fusion(f32[1,32,3,2,18,514]{5,4,3,2,1,0:T(8,128)} %maximum_convert_fusion, f32[16,512]{1,0:T(8,128)S(1)} %select_reduce_fusion, bf16[32,3,2,16,512]{4,3,2,1,0:T(8,128)(2,1)} %all-gather.2.cloned.1.call-done, ...), kind=kLoop, calls=%fused_computation.51 | loop fusion | flops 15728640 | bytes 37978112 | tf_op jit(solution)/shard_map/convert_element_type | solution.py:39
  163.5 3.1 collective-permute-start.4
  167.9 4.6 collective-permute-done.4
  172.5 3.9 collective-permute-done.5
  176.3 3.0 pad_maximum_fusion.8
  179.3 2.1 copy.25
  181.4 3.3 collective-permute-start.6
  184.8 2.1 copy.26
  188.3 2.0 copy.27
  191.4 2.0 copy.28
  193.4 10.4 %maximum_convert_fusion.1 = f32[1,32,3,2,18,514]{5,4,3,2,1,0:T(8,128)} fusion(bf16[1,32,3,2,18,1]{5,4,3,2,1,0:T(8,128)(2,1)} %copy.28, bf16[1,32,3,2,1,512]{5,4,3,2,1,0:T(2,128)(2,1)} %copy-done.5, bf16[1,32,3,2,16,512]{5,4,3,2,1,0:T(8,128)(2,1)S(1)} %get-tuple-element.9, bf16[1,32,3,2,1,512]{5,4,3,2,1,0:T(2,128)(2,1)} %copy-done.1, ...), kind=kLoop, calls=%fused_computation.29 | loop fusion | flops 17763840 | bytes 10658304 | tf_op jit(solution)/shard_map/convert_element_type | solution.py:39
  203.8 19.5 %fusion.18 = (bf16[1,32,3,2,16,512]{5,4,3,2,1,0:T(8,128)(2,1)S(1)}, f32[1,32,3,2,16,512]{5,4,3,2,1,0:T(8,128)}) fusion(f32[1,32,3,2,16,512]{5,4,3,2,1,0:T(8,128)} %get-tuple-element.10, f32[1,32,3,2,18,514]{5,4,3,2,1,0:T(8,128)} %maximum_convert_fusion.1, f32[16,512]{1,0:T(8,128)S(1)} %select_reduce_fusion), kind=kLoop, calls=%fused_computation.50 | loop fusion | flops 12582912 | bytes 40927232 | tf_op jit(solution)/shard_map/convert_element_type | solution.py:39
  223.9 2.8 collective-permute-start.8
  228.1 3.4 collective-permute-done.8
  231.4 3.8 collective-permute-done.9
  235.3 3.0 pad_maximum_fusion.5
  238.3 2.1 copy.29
  240.4 2.9 collective-permute-start.10
  243.2 2.1 copy.30
  245.3 1.7 collective-permute-start.11
  247.0 2.0 copy.31
  249.9 2.0 copy.32
  251.9 10.4 %maximum_convert_fusion.2 = f32[1,32,3,2,18,514]{5,4,3,2,1,0:T(8,128)} fusion(bf16[1,32,3,2,18,1]{5,4,3,2,1,0:T(8,128)(2,1)} %copy.32, bf16[1,32,3,2,1,512]{5,4,3,2,1,0:T(2,128)(2,1)} %copy-done.6, bf16[1,32,3,2,16,512]{5,4,3,2,1,0:T(8,128)(2,1)S(1)} %get-tuple-element.7, bf16[1,32,3,2,1,512]{5,4,3,2,1,0:T(2,128)(2,1)} %copy-done.2, ...), kind=kLoop, calls=%fused_computation.30 | loop fusion | flops 17763840 | bytes 10658304 | tf_op jit(solution)/shard_map/convert_element_type | solution.py:39
  262.4 19.7 %fusion.16 = (bf16[1,32,3,2,16,512]{5,4,3,2,1,0:T(8,128)(2,1)S(1)}, f32[1,32,3,2,16,512]{5,4,3,2,1,0:T(8,128)}) fusion(f32[1,32,3,2,16,512]{5,4,3,2,1,0:T(8,128)} %get-tuple-element.8, f32[1,32,3,2,18,514]{5,4,3,2,1,0:T(8,128)} %maximum_convert_fusion.2, f32[16,512]{1,0:T(8,128)S(1)} %select_reduce_fusion), kind=kLoop, calls=%fused_computation.49 | loop fusion | flops 12582912 | bytes 40927232 | tf_op jit(solution)/shard_map/convert_element_type | solution.py:39
  282.7 2.5 collective-permute-start.12
  286.5 3.4 collective-permute-done.12
  289.9 3.8 collective-permute-done.13
  293.7 3.0 pad_maximum_fusion.2
  296.7 2.1 copy.33
  298.8 3.1 collective-permute-start.14
  301.9 2.1 copy.34
  305.4 2.0 copy.35
  308.5 2.0 copy.36
  310.5 10.4 %maximum_convert_fusion.3 = f32[1,32,3,2,18,514]{5,4,3,2,1,0:T(8,128)} fusion(bf16[1,32,3,2,18,1]{5,4,3,2,1,0:T(8,128)(2,1)} %copy.36, bf16[1,32,3,2,1,512]{5,4,3,2,1,0:T(2,128)(2,1)} %copy-done.7, bf16[1,32,3,2,16,512]{5,4,3,2,1,0:T(8,128)(2,1)S(1)} %get-tuple-element.5, bf16[1,32,3,2,1,512]{5,4,3,2,1,0:T(2,128)(2,1)} %copy-done.3, ...), kind=kLoop, calls=%fused_computation.31 | loop fusion | flops 17763840 | bytes 10658304 | tf_op jit(solution)/shard_map/convert_element_type | solution.py:39
  320.9 20.2 %fusion.4 = f32[32,3,2,16,512]{4,3,2,1,0:T(8,128)} fusion(f32[1,32,3,2,16,512]{5,4,3,2,1,0:T(8,128)} %get-tuple-element.6, f32[1,32,3,2,18,514]{5,4,3,2,1,0:T(8,128)} %maximum_convert_fusion.3, f32[16,512]{1,0:T(8,128)S(1)} %select_reduce_fusion, f32[3,2,16,512]{3,2,1,0:T(8,128)S(1)} %bitcast_convert_fusion), kind=kLoop, calls=%fused_computation.5 | loop fusion | flops 12582912 | bytes 37978112 | tf_op jit(solution)/shard_map/reduce_sum | solution.py:49
  341.1 135.4 %reduce-scatter.2.cloned.1.call-done = f32[1,3,2,16,512]{4,3,2,1,0:T(8,128)} async-done(((f32[32,3,2,16,512]{4,3,2,1,0:T(8,128)}), f32[1,3,2,16,512]{4,3,2,1,0:T(8,128)}) %reduce-scatter.2.cloned.1.call-update) | async-done | bytes 196624 | tf_op jit(solution)/shard_map/reduce_scatter | solution.py:50
  (46 shorter events, 19.2 us)
Async XLA Ops:
  6.5 90.8 %all-gather.2.cloned.1.call-start = ((), (), s32[]{:S(2)}) async-start(), calls=%async_computation.1 | async-start | bytes 3244032 | tf_op jit(solution)/shard_map/all_gather | solution.py:36
  7.3 469.2 %reduce-scatter.2.cloned.1.call-start = ((), (), s32[]{:S(2)}) async-start(), calls=%async_computation.2 | async-start | bytes 6488064 | tf_op jit(solution)/shard_map/reduce_scatter | solution.py:50
  100.1 28.4 %copy-start.8 = (s32[16,512]{1,0:T(8,128)S(1)}, s32[16,512]{1,0:T(8,128)}, u32[]{:S(2)}) copy-start(s32[16,512]{1,0:T(8,128)} %param.6) | copy-start | bytes 98308
  100.1 28.4 %copy-start.9 = (f32[8]{0:T(128)S(1)}, f32[8]{0:T(128)}, u32[]{:S(2)}) copy-start(f32[8]{0:T(128)} %param.7) | copy-start | bytes 100
  100.7 11.3 %collective-permute-start = (bf16[1,32,3,2,1,512]{5,4,3,2,1,0:T(2,128)(2,1)S(1)}, bf16[1,32,3,2,1,512]{5,4,3,2,1,0:T(2,128)(2,1)S(1)}, u32[]{:S(2)}, u32[]{:S(2)}) collective-permute-start(bf16[1,32,3,2,1,512]{5,4,3,2,1,0:T(2,128)(2,1)S(1)} %get-tuple-element.25), channel_id=1, source_target_pairs={{0,2},{2,4},{4,6},{1,3},{3,5},{5,7},{8,10},{10,12},{12,14},{9,11},... | collective-permute-start | bytes 589832 | tf_op jit(solution)/shard_map/ppermute | solution.py:17
  103.9 12.0 %collective-permute-start.1 = (bf16[1,32,3,2,1,512]{5,4,3,2,1,0:T(2,128)(2,1)S(1)}, bf16[1,32,3,2,1,512]{5,4,3,2,1,0:T(2,128)(2,1)S(1)}, u32[]{:S(2)}, u32[]{:S(2)}) collective-permute-start(bf16[1,32,3,2,1,512]{5,4,3,2,1,0:T(2,128)(2,1)S(1)} %get-tuple-element.26), channel_id=1, source_target_pairs={{2,0},{4,2},{6,4},{3,1},{5,3},{7,5},{10,8},{12,10},{14,12},{11,9},... | collective-permute-start | bytes 589832 | tf_op jit(solution)/shard_map/ppermute | solution.py:19
  112.0 3.9 copy-start
  115.9 3.0 copy-start.4
  123.0 8.2 %collective-permute-start.3 = (bf16[1,32,3,2,18,1]{1,3,5,4,2,0:T(2,128)(2,1)S(1)}, bf16[1,32,3,2,18,1]{1,3,5,4,2,0:T(2,128)(2,1)S(1)}, u32[]{:S(2)}, u32[]{:S(2)}) collective-permute-start(bf16[1,32,3,2,18,1]{1,3,5,4,2,0:T(2,128)(2,1)S(1)} %copy.22), channel_id=1, source_target_pairs={{1,0},{3,2},{5,4},{7,6},{9,8},{11,10},{13,12},{15,14},{17,16},{19,... | collective-permute-start | bytes 20744 | tf_op jit(solution)/shard_map/ppermute | solution.py:19
  124.3 4.9 %collective-permute-start.2 = (bf16[1,32,3,2,18,1]{1,3,5,4,2,0:T(2,128)(2,1)S(1)}, bf16[1,32,3,2,18,1]{1,3,5,4,2,0:T(2,128)(2,1)S(1)}, u32[]{:S(2)}, u32[]{:S(2)}) collective-permute-start(bf16[1,32,3,2,18,1]{1,3,5,4,2,0:T(2,128)(2,1)S(1)} %copy.21), channel_id=1, source_target_pairs={{0,1},{2,3},{4,5},{6,7},{8,9},{10,11},{12,13},{14,15},{16,17},{18,... | collective-permute-start | bytes 20744 | tf_op jit(solution)/shard_map/ppermute | solution.py:17
  163.5 9.0 %collective-permute-start.4 = (bf16[1,32,3,2,1,512]{5,4,3,2,1,0:T(2,128)(2,1)S(1)}, bf16[1,32,3,2,1,512]{5,4,3,2,1,0:T(2,128)(2,1)S(1)}, u32[]{:S(2)}, u32[]{:S(2)}) collective-permute-start(bf16[1,32,3,2,1,512]{5,4,3,2,1,0:T(2,128)(2,1)S(1)} %get-tuple-element.23), channel_id=1, source_target_pairs={{0,2},{2,4},{4,6},{1,3},{3,5},{5,7},{8,10},{10,12},{12,14},{9,11},... | collective-permute-start | bytes 589832 | tf_op jit(solution)/shard_map/ppermute | solution.py:17
  166.6 9.7 %collective-permute-start.5 = (bf16[1,32,3,2,1,512]{5,4,3,2,1,0:T(2,128)(2,1)S(1)}, bf16[1,32,3,2,1,512]{5,4,3,2,1,0:T(2,128)(2,1)S(1)}, u32[]{:S(2)}, u32[]{:S(2)}) collective-permute-start(bf16[1,32,3,2,1,512]{5,4,3,2,1,0:T(2,128)(2,1)S(1)} %get-tuple-element.24), channel_id=1, source_target_pairs={{2,0},{4,2},{6,4},{3,1},{5,3},{7,5},{10,8},{12,10},{14,12},{11,9},... | collective-permute-start | bytes 589832 | tf_op jit(solution)/shard_map/ppermute | solution.py:19
  172.5 3.9 copy-start.1
  176.3 3.0 copy-start.5
  181.4 6.9 %collective-permute-start.6 = (bf16[1,32,3,2,18,1]{1,3,5,4,2,0:T(2,128)(2,1)S(1)}, bf16[1,32,3,2,18,1]{1,3,5,4,2,0:T(2,128)(2,1)S(1)}, u32[]{:S(2)}, u32[]{:S(2)}) collective-permute-start(bf16[1,32,3,2,18,1]{1,3,5,4,2,0:T(2,128)(2,1)S(1)} %copy.25), channel_id=1, source_target_pairs={{0,1},{2,3},{4,5},{6,7},{8,9},{10,11},{12,13},{14,15},{16,17},{18,... | collective-permute-start | bytes 20744 | tf_op jit(solution)/shard_map/ppermute | solution.py:17
  186.8 4.6 collective-permute-start.7
  223.9 7.5 %collective-permute-start.8 = (bf16[1,32,3,2,1,512]{5,4,3,2,1,0:T(2,128)(2,1)S(1)}, bf16[1,32,3,2,1,512]{5,4,3,2,1,0:T(2,128)(2,1)S(1)}, u32[]{:S(2)}, u32[]{:S(2)}) collective-permute-start(bf16[1,32,3,2,1,512]{5,4,3,2,1,0:T(2,128)(2,1)S(1)} %get-tuple-element.21), channel_id=1, source_target_pairs={{0,2},{2,4},{4,6},{1,3},{3,5},{5,7},{8,10},{10,12},{12,14},{9,11},... | collective-permute-start | bytes 589832 | tf_op jit(solution)/shard_map/ppermute | solution.py:17
  226.8 8.5 %collective-permute-start.9 = (bf16[1,32,3,2,1,512]{5,4,3,2,1,0:T(2,128)(2,1)S(1)}, bf16[1,32,3,2,1,512]{5,4,3,2,1,0:T(2,128)(2,1)S(1)}, u32[]{:S(2)}, u32[]{:S(2)}) collective-permute-start(bf16[1,32,3,2,1,512]{5,4,3,2,1,0:T(2,128)(2,1)S(1)} %get-tuple-element.22), channel_id=1, source_target_pairs={{2,0},{4,2},{6,4},{3,1},{5,3},{7,5},{10,8},{12,10},{14,12},{11,9},... | collective-permute-start | bytes 589832 | tf_op jit(solution)/shard_map/ppermute | solution.py:19
  231.4 3.8 copy-start.2
  235.3 3.0 copy-start.6
  240.4 6.6 %collective-permute-start.10 = (bf16[1,32,3,2,18,1]{1,3,5,4,2,0:T(2,128)(2,1)S(1)}, bf16[1,32,3,2,18,1]{1,3,5,4,2,0:T(2,128)(2,1)S(1)}, u32[]{:S(2)}, u32[]{:S(2)}) collective-permute-start(bf16[1,32,3,2,18,1]{1,3,5,4,2,0:T(2,128)(2,1)S(1)} %copy.29), channel_id=1, source_target_pairs={{0,1},{2,3},{4,5},{6,7},{8,9},{10,11},{12,13},{14,15},{16,17},{18,... | collective-permute-start | bytes 20744 | tf_op jit(solution)/shard_map/ppermute | solution.py:17
  245.3 4.6 collective-permute-start.11
  282.7 7.2 %collective-permute-start.12 = (bf16[1,32,3,2,1,512]{5,4,3,2,1,0:T(2,128)(2,1)S(1)}, bf16[1,32,3,2,1,512]{5,4,3,2,1,0:T(2,128)(2,1)S(1)}, u32[]{:S(2)}, u32[]{:S(2)}) collective-permute-start(bf16[1,32,3,2,1,512]{5,4,3,2,1,0:T(2,128)(2,1)S(1)} %get-tuple-element.19), channel_id=1, source_target_pairs={{0,2},{2,4},{4,6},{1,3},{3,5},{5,7},{8,10},{10,12},{12,14},{9,11},... | collective-permute-start | bytes 589832 | tf_op jit(solution)/shard_map/ppermute | solution.py:17
  285.2 8.5 %collective-permute-start.13 = (bf16[1,32,3,2,1,512]{5,4,3,2,1,0:T(2,128)(2,1)S(1)}, bf16[1,32,3,2,1,512]{5,4,3,2,1,0:T(2,128)(2,1)S(1)}, u32[]{:S(2)}, u32[]{:S(2)}) collective-permute-start(bf16[1,32,3,2,1,512]{5,4,3,2,1,0:T(2,128)(2,1)S(1)} %get-tuple-element.20), channel_id=1, source_target_pairs={{2,0},{4,2},{6,4},{3,1},{5,3},{7,5},{10,8},{12,10},{14,12},{11,9},... | collective-permute-start | bytes 589832 | tf_op jit(solution)/shard_map/ppermute | solution.py:19
  289.9 3.8 copy-start.3
  293.7 3.0 copy-start.7
  298.8 6.6 %collective-permute-start.14 = (bf16[1,32,3,2,18,1]{1,3,5,4,2,0:T(2,128)(2,1)S(1)}, bf16[1,32,3,2,18,1]{1,3,5,4,2,0:T(2,128)(2,1)S(1)}, u32[]{:S(2)}, u32[]{:S(2)}) collective-permute-start(bf16[1,32,3,2,18,1]{1,3,5,4,2,0:T(2,128)(2,1)S(1)} %copy.33), channel_id=1, source_target_pairs={{0,1},{2,3},{4,5},{6,7},{8,9},{10,11},{12,13},{14,15},{16,17},{18,... | collective-permute-start | bytes 20744 | tf_op jit(solution)/shard_map/ppermute | solution.py:17
  303.9 4.6 collective-permute-start.15
Sparse Core Ops, SparseCore 0:
  10.1 87.1 all-gather.1
  341.3 135.1 reduce-scatter.1
where the time goes:
time: 493 us; the launch traced here: 485 us
  waiting for transfers between devices  263 us (53%)
  other arithmetic  138 us (28%)
  starting transfers between devices  36.1 us (7%)
  local copies, waits for them, and re-layouts  34.9 us (7%)
  between operations  13.8 us (3%)
    reduce_scatter x1, waiting for transfers between devices, body(): lax.psum_scatter(member_terms, 'member', scatter_dimension=0, tiled=True)  135 us
    all_gather x1, waiting for transfers between devices, body(): all_probes = lax.all_gather(probes, 'member', axis=0, tiled=True)  89.1 us
    convert_element_type x4, other arithmetic, body(): field_now.astype(jnp.bfloat16)  61 us
    convert_element_type x4, other arithmetic, body(): extended(field_now.astype(jnp.bfloat16), (('row', 4), ('col', 5)), 1)  41.8 us
    ppermute x8, starting transfers between devices, extended(): lax.ppermute(tail, axis, [(i, (i + 1) % count) for i in range(ends)])  25 us
    reduce_sum x1, other arithmetic, body(): jnp.sum(pert[:, None].astype(jnp.float32) * field_now, axis=0)  20.2 us
    ppermute x8, waiting for transfers between devices, extended(): lax.ppermute(tail, axis, [(i, (i + 1) % count) for i in range(ends)])  18.8 us
    ppermute x8, waiting for transfers between devices, extended(): lax.ppermute(head, axis, [((i + 1) % count, i) for i in range(ends)])  18.6 us
  transfers between devices with their start and end apart: 18, of which 14 were waited for; matrix products, arithmetic and copies ran while one was open for 3% of the time, Pallas kernels for 0%

commit v1 on v0

v1 whole, which is shorter than its diff:
```python
import jax
import jax.numpy as jnp
from jax import lax
from jax.experimental import pallas as pl
from jax.experimental.pallas import tpu as pltpu
from jax.sharding import PartitionSpec as P

SWEEPS = 4
VARS = 3
LEV = 2
ROWS = 16
COLS = 512
HALO = 4
STRIP = 32
WIN = STRIP + 2 * HALO
LANES = 128
F32 = jnp.float32
BF16 = jnp.bfloat16


def edge_kernel(col_ref, pert_ref, prob_ref, cls_ref, up_ref, dn_ref, side_ref, sup_ref, sdn_ref):
    last = col_ref[0] == 0
    for plane in range(VARS * LEV + 1):
        if plane < VARS * LEV:
            v, l = plane // LEV, plane % LEV
            a = pert_ref[0, v, l].astype(F32)
            b = prob_ref[0, v, l].astype(F32)
        else:
            a = (cls_ref[...] + 1).astype(F32)
            b = a
        up = jnp.concatenate([a[:HALO], b[:HALO]], axis=0)
        dn = jnp.concatenate([a[ROWS - HALO :], b[ROWS - HALO :]], axis=0)
        up_ref[plane] = up.astype(BF16)
        dn_ref[plane] = dn.astype(BF16)
        sup_ref[plane] = jnp.where(last, up[:, COLS - LANES :], up[:, :LANES]).astype(BF16)
        sdn_ref[plane] = jnp.where(last, dn[:, COLS - LANES :], dn[:, :LANES]).astype(BF16)
        side_ref[0, plane] = jnp.where(last, a[:, COLS - LANES :], a[:, :LANES]).astype(BF16)
        side_ref[1, plane] = jnp.where(last, b[:, COLS - LANES :], b[:, :LANES]).astype(BF16)


def pack_kernel(
    col_ref, pert_ref, prob_ref, cls_ref, below_ref, above_ref, side_ref, sbelow_ref, sabove_ref, out_ref, win_ref
):
    first = col_ref[0] == 0
    blocks = COLS // LANES
    lane = lax.broadcasted_iota(jnp.int32, (ROWS, LANES), 1)

    def block(kind, plane, at):
        inside = 0 <= at < blocks
        span = slice(at * LANES, (at + 1) * LANES)
        v, l = plane // LEV, plane % LEV
        if kind == 2:
            if inside:
                got = jnp.concatenate(
                    [below_ref[plane, :, span].astype(F32), above_ref[plane, :, span].astype(F32)], axis=0
                )
            else:
                got = jnp.concatenate([sbelow_ref[plane].astype(F32), sabove_ref[plane].astype(F32)], axis=0)
        elif not inside:
            got = side_ref[kind, plane].astype(F32)
        elif plane == VARS * LEV:
            got = (cls_ref[:, span] + 1).astype(F32)
        else:
            got = (pert_ref if kind == 0 else prob_ref)[0, v, l, :, span].astype(F32)
        if inside:
            return got
        return jnp.where(first if at == blocks else jnp.logical_not(first), got, 0.0)

    for at in range(-1, blocks + 1):
        span = slice((at + 1) * LANES, (at + 2) * LANES)
        win_ref[:ROWS, span] = block(0, VARS * LEV, at).astype(BF16)
        win_ref[ROWS:, span] = block(2, VARS * LEV, at).astype(BF16)

    for s in range(COLS // STRIP):
        start = s * STRIP - HALO
        at, off = start // LANES, start % LANES
        for l in range(LEV):
            for kind in range(3):
                acc = jnp.zeros((ROWS, LANES), F32)
                for v in range(VARS):
                    shift = (WIN * v - off) % LANES
                    got = block(kind, v * LEV + l, at)
                    got = pltpu.roll(got, shift, 1) if shift else got
                    if off + WIN > LANES:
                        more = block(kind, v * LEV + l, at + 1)
                        more = pltpu.roll(more, shift, 1) if shift else more
                        got = jnp.where(lane < WIN * v + LANES - off, got, more)
                    acc = jnp.where((lane >= WIN * v) & (lane < WIN * (v + 1)), got, acc)
                out_ref[s * LEV + l, kind * ROWS : (kind + 1) * ROWS] = acc.astype(BF16)


TOP = 8
TALL = TOP + ROWS + TOP
FORWARD = [
    (dy, dx)
    for dy in range(HALO + 1)
    for dx in range(-HALO, HALO + 1)
    if dy + abs(dx) <= HALO and (dy > 0 or dx >= 0)
]
EVERY = [(dy, dx) for dx in range(-HALO, HALO + 1) for dy in range(-HALO, HALO + 1) if abs(dy) + abs(dx) <= HALO]
AT = {d: i for i, d in enumerate(EVERY)}


def lanes_by(x, dx):
    return pltpu.roll(x, (-dx) % LANES, 1) if dx else x


def rows_by(x, dy):
    return pltpu.roll(x, (-dy) % x.shape[0], 0) if dy else x


def apply_kernel(strip_ref, rates_ref, got_ref, win_ref, out_ref, pert_ref, prob_ref, gram_ref, weight_ref):
    members = got_ref.shape[0]

    def spread(m, _):
        for ref, own, below, above in (
            (pert_ref, 0, 2 * ROWS, 2 * ROWS + 8),
            (prob_ref, ROWS, 2 * ROWS + 4, 2 * ROWS + 12),
        ):
            tile = got_ref[m].astype(F32)
            ref[m, 0:TOP] = jnp.zeros((TOP, LANES), F32)
            ref[m, TOP + ROWS : TALL] = jnp.zeros((TOP, LANES), F32)
            ref[m, TOP : TOP + ROWS] = tile[own : own + ROWS]
            ref[m, TOP + ROWS : TOP + ROWS + HALO] = tile[below : below + HALO]
            ref[m, TOP - HALO : TOP] = tile[above : above + HALO]
        return 0

    lax.fori_loop(0, members, spread, 0)

    wide = win_ref.shape[1]
    spot = lax.broadcasted_iota(jnp.int32, (wide, LANES), 0)
    lane = lax.broadcasted_iota(jnp.int32, (wide, LANES), 1)
    column = lane - jnp.where(lane >= WIN, WIN, 0) - jnp.where(lane >= 2 * WIN, WIN, 0)
    pick = (spot == LANES - HALO + STRIP * strip_ref[0] + column) & (lane < VARS * WIN)
    cls = jnp.dot(win_ref[...], pick.astype(F32).astype(BF16), preferred_element_type=F32)
    blank = jnp.zeros((TOP - HALO, LANES), F32)
    cls = jnp.concatenate(
        [blank, cls[ROWS + 8 : ROWS + 12], cls[:ROWS], cls[ROWS : ROWS + HALO], blank], axis=0
    )
    rate = jnp.zeros((TALL, LANES), F32)
    for k in range(rates_ref.shape[0]):
        rate = jnp.where(cls == float(k + 1), rates_ref[k], rate)

    steps = ((0, 1), (0, -1), (1, 0), (-1, 0))
    stay = 1.0 - 4.0 * rate
    coef = {(0, 0): stay}
    for e in steps:
        coef[e] = rate
    for sweep in range(1, SWEEPS):
        moved = {}
        for e in steps:
            for d, c in coef.items():
                to = (d[0] + e[0], d[1] + e[1])
                c = lanes_by(rows_by(c, e[0]), e[1])
                moved[to] = moved[to] + c if to in moved else c
        coef = {d: rate * moved[d] + (stay * coef[d] if d in coef else 0.0) for d in moved}
    scale = 1.0 / (members - 1)

    for b in range(3):
        row = TOP + 8 * b

        def products(m, acc):
            low = pert_ref[m, row : row + 8]
            high = [pert_ref[m, row - dy : row - dy + 8] for dy in range(HALO + 1)]
            near = {dx: lanes_by(low, dx) for dx in range(-HALO + 1, HALO + 1)}
            return tuple(a + high[dy] * near[dx] for a, (dy, dx) in zip(acc, FORWARD))

        acc = tuple(jnp.zeros((8, LANES), F32) for _ in FORWARD)
        acc = lax.fori_loop(0, members, products, acc, unroll=4)
        for i, a in enumerate(acc):
            gram_ref[i, 8 * b : 8 * b + 8] = a

    for i, (dy, dx) in enumerate(FORWARD):
        c = coef[(dy, dx)][TOP : TOP + ROWS] * scale
        weight_ref[AT[(dy, dx)]] = lanes_by(c * gram_ref[i, dy : dy + ROWS], -dx)
        if (dy, dx) != (0, 0):
            c = coef[(-dy, -dx)][TOP : TOP + ROWS] * scale
            weight_ref[AT[(-dy, -dx)]] = lanes_by(c, dx) * gram_ref[i, 0:ROWS]

    for b in range(2):

        def one_probe(p, _):
            rows = [prob_ref[p, TOP + 8 * b + dy : TOP + 8 * b + dy + 8] for dy in range(-HALO, HALO + 1)]
            total = None
            for dx in range(-HALO, HALO + 1):
                part = None
                for dy in range(-HALO + abs(dx), HALO - abs(dx) + 1):
                    term = weight_ref[AT[(dy, dx)], 8 * b : 8 * b + 8] * rows[dy + HALO]
                    part = term if part is None else part + term
                part = lanes_by(part, dx)
                total = part if total is None else total + part
            out_ref[p, 8 * b : 8 * b + 8] = total
            return 0

        lax.fori_loop(0, members, one_probe, 0, unroll=4)


def unpack_kernel(got_ref, out_ref):
    lane = lax.broadcasted_iota(jnp.int32, (ROWS, LANES), 1)
    per = LANES // STRIP
    for v in range(VARS):
        for l in range(LEV):
            for at in range(COLS // LANES):
                acc = None
                for q in range(per):
                    got = got_ref[(at * per + q) * LEV + l]
                    shift = (STRIP * q - WIN * v - HALO) % LANES
                    got = pltpu.roll(got, shift, 1) if shift else got
                    acc = got if acc is None else jnp.where(lane >= STRIP * q, got, acc)
                out_ref[0, v, l, :, at * LANES : (at + 1) * LANES] = acc


def body(pert, probes, diff_class, class_rate):
    members = lax.axis_size("member")
    n_row = lax.axis_size("row")
    col = lax.axis_index("col").astype(jnp.int32).reshape(1)
    strip = (lax.axis_index("member") // LEV).astype(jnp.int32).reshape(1)
    vmem = pl.BlockSpec(memory_space=pltpu.VMEM)
    smem = pl.BlockSpec(memory_space=pltpu.SMEM)
    planes = VARS * LEV + 1

    shape = jax.ShapeDtypeStruct
    up, dn, side, sup, sdn = pl.pallas_call(
        edge_kernel,
        in_specs=[smem, vmem, vmem, vmem],
        out_specs=[vmem] * 5,
        out_shape=[
            shape((planes, 2 * HALO, COLS), BF16),
            shape((planes, 2 * HALO, COLS), BF16),
            shape((2, planes, ROWS, LANES), BF16),
            shape((planes, 2 * HALO, LANES), BF16),
            shape((planes, 2 * HALO, LANES), BF16),
        ],
        name="edges",
    )(col, pert, probes, diff_class)

    below = lax.ppermute(up, "row", [(i + 1, i) for i in range(n_row - 1)])
    above = lax.ppermute(dn, "row", [(i, i + 1) for i in range(n_row - 1)])
    beside = lax.ppermute(side, "col", [(0, 1), (1, 0)])
    rc = ("row", "col")
    sbelow = lax.ppermute(sup, rc, [((i + 1) * 2 + c, i * 2 + 1 - c) for i in range(n_row - 1) for c in (0, 1)])
    sabove = lax.ppermute(sdn, rc, [(i * 2 + c, (i + 1) * 2 + 1 - c) for i in range(n_row - 1) for c in (0, 1)])

    chunks, window = pl.pallas_call(
        pack_kernel,
        in_specs=[smem] + [vmem] * 8,
        out_specs=[vmem] * 2,
        out_shape=[shape((members, 3 * ROWS, LANES), BF16), shape((2 * ROWS, COLS + 2 * LANES), BF16)],
        name="pack",
    )(col, pert, probes, diff_class, below, above, beside, sbelow, sabove)

    got = lax.all_to_all(chunks, "member", 0, 0, tiled=True)

    part = pl.pallas_call(
        apply_kernel,
        in_specs=[smem, smem, vmem, vmem],
        out_specs=vmem,
        out_shape=shape((members, ROWS, LANES), F32),
        scratch_shapes=[
            pltpu.VMEM((members, TALL, LANES), F32),
            pltpu.VMEM((members, TALL, LANES), F32),
            pltpu.VMEM((len(FORWARD), 24, LANES), F32),
            pltpu.VMEM((len(EVERY), ROWS, LANES), F32),
        ],
        name="apply",
    )(strip, class_rate, got, window)

    back = lax.all_to_all(part, "member", 0, 0, tiled=True)

    return pl.pallas_call(
        unpack_kernel,
        in_specs=[vmem],
        out_specs=vmem,
        out_shape=shape((1, VARS, LEV, ROWS, COLS), F32),
        name="unpack",
    )(back)


def solution(mesh):
    placed = (
        P("member", None, None, "row", "col"),
        P("member", None, None, "row", "col"),
        P("row", "col"),
        P(),
    )
    return jax.shard_map(
        body,
        mesh=mesh,
        in_specs=placed,
        out_specs=P("member", None, None, "row", "col"),
        check_vma=False,
    )
```

time: 493 us -> 76.4 us (0.15); the launches traced: 485 us -> 75.5 us
  waiting for transfers between devices: 263 us -> 15.2 us
  other arithmetic: 138 us -> 0 us
  local copies, waits for them, and re-layouts: 34.9 us -> 1.98 us
  blocking collectives: 0 us -> 18.7 us
  between operations: 13.8 us -> 0.1 us
  Pallas kernels: 0 us -> 12.5 us
  starting transfers between devices: 36.1 us -> 27 us
    reduce_scatter x1 -> x0, waiting for transfers between devices: 135 us -> none  [body(): lax.psum_scatter(member_terms, 'member', scatter_dimension=0, tiled=True)]
    convert_element_type x9 -> x0, other arithmetic: 104 us -> none  [the longest x4 61 us: body(): field_now.astype(jnp.bfloat16)]
    all_gather x1 -> x0, waiting for transfers between devices: 89.1 us -> none  [body(): all_probes = lax.all_gather(probes, 'member', axis=0, tiled=True)]
    ppermute x16 -> x5, waiting for transfers between devices: 37.4 us -> 1.03 us  [the longest x1 1.02 us: body(): lax.ppermute(sdn, rc, [(i * 2 + c, (i + 1) * 2 + 1 - c) for i in range(n_...]
    ppermute x16 -> x5, starting transfers between devices: 36.1 us -> 13.5 us  [the longest x1 4.88 us: body(): lax.ppermute(sdn, rc, [(i * 2 + c, (i + 1) * 2 + 1 - c) for i in range(n_...]
    reduce_sum x2 -> x0, other arithmetic: 20.3 us -> none  [the longest x1 20.2 us: body(): jnp.sum(pert[:, None].astype(jnp.float32) * field_now, axis=0)]
    slice x12 -> x0, local copies, waits for them, and re-layouts: 19 us -> none  [the longest x8 10.7 us: extended(): lax.slice_in_dim(cells, cells.shape[dim] - width, cells.shape[dim], axis=...]
    all_to_all x0 -> x1, blocking collectives: none -> 18.7 us  [body(): back = lax.all_to_all(part, 'member', 0, 0, tiled=True)]
  transfers between devices with their start and end apart: 18 -> 6, of which waited for: 14 -> 2; matrix products, arithmetic and copies ran while one was open for 3% -> 0% of each run, Pallas kernels for 0% -> 0%
where the time goes in v1:
time: 76.4 us; the launch traced here: 75.5 us
  starting transfers between devices  27 us (35%)
  blocking collectives  18.7 us (24%)
  waiting for transfers between devices  15.2 us (20%)
  Pallas kernels  12.5 us (16%)
  local copies, waits for them, and re-layouts  1.98 us (3%)
    all_to_all x1, blocking collectives, body(): back = lax.all_to_all(part, 'member', 0, 0, tiled=True)  18.7 us
    all_to_all x1, waiting for transfers between devices, body(): got = lax.all_to_all(chunks, 'member', 0, 0, tiled=True)  14.2 us
    all_to_all x1, starting transfers between devices, body(): got = lax.all_to_all(chunks, 'member', 0, 0, tiled=True)  13.4 us
    pallas_call x1, Pallas kernels, body(): pl.pallas_call(apply_kernel, in_specs=[smem, smem, vmem, vmem], out_specs...  6.73 us
    ppermute x1, starting transfers between devices, body(): lax.ppermute(sdn, rc, [(i * 2 + c, (i + 1) * 2 + 1 - c) for i in range(n_...  4.88 us
    ppermute x1, starting transfers between devices, body(): above = lax.ppermute(dn, 'row', [(i, i + 1) for i in range(n_row - 1)])  4.65 us
    pallas_call x1, Pallas kernels, body(): pl.pallas_call(pack_kernel, in_specs=[smem] + [vmem] * 8, out_specs=[vmem...  2.28 us
    unnamed x12, local copies, waits for them, and re-layouts  1.98 us
  transfers between devices with their start and end apart: 6, of which 2 were waited for; matrix products, arithmetic and copies ran while one was open for 0% of the time, Pallas kernels for 0%

profile of v1, /device:TPU:1, one launch (start us, length us, event | category | flops | bytes accessed | tf_op | source)
XLA Modules:
  0.0 75.5 jit_solution(13399738440681334126)
XLA Ops:
  0.0 1.6 %edges.1 = (bf16[7,8,512]{2,1,0:T(8,128)(2,1)}, bf16[7,8,512]{2,1,0:T(8,128)(2,1)}, bf16[2,7,16,128]{3,2,1,0:T(8,128)(2,1)}, bf16[7,8,128]{2,1,0:T(8,128)(2,1)}, bf16[7,8,128]{2,1,0:T(8,128)(2,1)}) custom-call(s32[1]{0:T(128)} %bitcast.1.col_ref, bf16[1,3,2,16,512]{4,3,2,1,0:T(8,128)(2,1)} %pert_ref.3, bf16[1,3,2,16,512]{4,3,2,1,0:T(8,128)(2,1)} %prob_ref.3, ...), custom_call_target="tpu_custom_call" | custom-call | tf_op jit(solution)/shard_map/edges/pallas_call | solution.py:223
  1.6 1.3 %collective-permute-start = (bf16[7,8,512]{2,1,0:T(8,128)(2,1)}, bf16[7,8,512]{2,1,0:T(8,128)(2,1)S(1)}, u32[]{:S(2)}, u32[]{:S(2)}) collective-permute-start(bf16[7,8,512]{2,1,0:T(8,128)(2,1)} %get-tuple-element.12), channel_id=1, source_target_pairs={{2,0},{4,2},{6,4},{3,1},{5,3},{7,5},{10,8},{12,10},{14,12},{11,9},... | collective-permute-start | bytes 172040 | tf_op jit(solution)/shard_map/ppermute | solution.py:237
  2.9 4.6 %collective-permute-start.1 = (bf16[7,8,512]{2,1,0:T(8,128)(2,1)}, bf16[7,8,512]{2,1,0:T(8,128)(2,1)S(1)}, u32[]{:S(2)}, u32[]{:S(2)}) collective-permute-start(bf16[7,8,512]{2,1,0:T(8,128)(2,1)} %get-tuple-element.13), channel_id=1, source_target_pairs={{0,2},{2,4},{4,6},{1,3},{3,5},{5,7},{8,10},{10,12},{12,14},{9,11},... | collective-permute-start | bytes 172040 | tf_op jit(solution)/shard_map/ppermute | solution.py:238
  7.6 1.5 %collective-permute-start.2 = (bf16[2,7,16,128]{3,2,1,0:T(8,128)(2,1)}, bf16[2,7,16,128]{3,2,1,0:T(8,128)(2,1)S(1)}, u32[]{:S(2)}, u32[]{:S(2)}) collective-permute-start(bf16[2,7,16,128]{3,2,1,0:T(8,128)(2,1)} %get-tuple-element.14), channel_id=1, source_target_pairs={{0,1},{1,0},{2,3},{3,2},{4,5},{5,4},{6,7},{7,6},{8,9},{9,8},{10,11... | collective-permute-start | bytes 172040 | tf_op jit(solution)/shard_map/ppermute | solution.py:239
  9.0 1.3 %collective-permute-start.3 = (bf16[7,8,128]{2,1,0:T(8,128)(2,1)}, bf16[7,8,128]{2,1,0:T(8,128)(2,1)S(1)}, u32[]{:S(2)}, u32[]{:S(2)}) collective-permute-start(bf16[7,8,128]{2,1,0:T(8,128)(2,1)} %get-tuple-element.15), channel_id=1, source_target_pairs={{2,1},{3,0},{4,3},{5,2},{6,5},{7,4},{10,9},{11,8},{12,11},{13,10},... | collective-permute-start | bytes 43016 | tf_op jit(solution)/shard_map/ppermute | solution.py:241
  10.3 4.9 %collective-permute-start.4 = (bf16[7,8,128]{2,1,0:T(8,128)(2,1)}, bf16[7,8,128]{2,1,0:T(8,128)(2,1)S(1)}, u32[]{:S(2)}, u32[]{:S(2)}) collective-permute-start(bf16[7,8,128]{2,1,0:T(8,128)(2,1)} %get-tuple-element.16), channel_id=1, source_target_pairs={{0,3},{1,2},{2,5},{3,4},{4,7},{5,6},{8,11},{9,10},{10,13},{11,12},... | collective-permute-start | bytes 43016 | tf_op jit(solution)/shard_map/ppermute | solution.py:242
  15.2 0.0 collective-permute-done.3.sbelow_ref
  15.2 0.0 copy-start.4
  15.2 1.0 %collective-permute-done.4.sabove_ref = bf16[7,8,128]{2,1,0:T(8,128)(2,1)S(1)} collective-permute-done((bf16[7,8,128]{2,1,0:T(8,128)(2,1)}, bf16[7,8,128]{2,1,0:T(8,128)(2,1)S(1)}, u32[]{:S(2)}, u32[]{:S(2)}) %collective-permute-start.4) | collective-permute-done | bytes 14368 | tf_op jit(solution)/shard_map/ppermute | solution.py:242
  16.3 0.0 copy-start.5
  16.3 0.0 collective-permute-done.below_ref
  16.3 0.0 copy-start.1
  16.3 0.0 collective-permute-done.1.above_ref
  16.3 0.0 copy-start.2
  16.3 0.0 collective-permute-done.2.side_ref
  16.3 0.0 copy-done.4
  16.3 0.6 copy-done.5
  16.9 0.0 copy-done.1
  16.9 0.0 copy-done.2
  16.9 0.0 copy-start.3
  16.9 0.6 copy-done.3
  17.5 2.3 %pack.1 = (bf16[32,48,128]{2,1,0:T(8,128)(2,1)}, bf16[32,768]{1,0:T(8,128)(2,1)}) custom-call(s32[1]{0:T(128)} %bitcast.1.col_ref, bf16[1,3,2,16,512]{4,3,2,1,0:T(8,128)(2,1)} %pert_ref.3, bf16[1,3,2,16,512]{4,3,2,1,0:T(8,128)(2,1)} %prob_ref.3, s32[16,512]{1,0:T(8,128)} %cls_ref.3, bf16[7,8,512]{2,1,0:T(8,128)(2,1)} %copy-done.1, ...), custom_call_target="tpu_custom_call" | custom-call | tf_op jit(solution)/shard_map/pack/pallas_call | solution.py:244
  19.8 13.4 %all-to-all-start = ((bf16[32,48,128]{2,1,0:T(8,128)(2,1)}), bf16[32,48,128]{2,1,0:T(8,128)(2,1)S(1)}, u32[]{:S(2)}, u32[]{:S(2)}) async-start(bf16[32,48,128]{2,1,0:T(8,128)(2,1)} %get-tuple-element.17), calls=%async_computation | async-start | bytes 786432 | tf_op jit(solution)/shard_map/all_to_all | solution.py:252
  33.3 14.2 %all-to-all-done.got_ref = bf16[32,48,128]{2,1,0:T(8,128)(2,1)S(1)} async-done(((bf16[32,48,128]{2,1,0:T(8,128)(2,1)}), bf16[32,48,128]{2,1,0:T(8,128)(2,1)S(1)}, u32[]{:S(2)}, u32[]{:S(2)}) %all-to-all-start) | async-done | bytes 393248 | tf_op jit(solution)/shard_map/all_to_all | solution.py:252
  47.5 0.0 copy-start
  47.5 0.7 copy-done
  48.2 6.7 %apply.1 = f32[32,16,128]{2,1,0:T(8,128)} custom-call(s32[1]{0:T(128)} %bitcast.strip_ref, f32[8]{0:T(128)} %rates_ref.1, bf16[32,48,128]{2,1,0:T(8,128)(2,1)} %copy-done, bf16[32,768]{1,0:T(8,128)(2,1)} %get-tuple-element.18.win_ref), custom_call_target="tpu_custom_call" | custom-call | tf_op jit(solution)/shard_map/apply/pallas_call | solution.py:254
  54.9 18.7 %all_to_all.10.got_ref = f32[32,16,128]{2,1,0:T(8,128)} all-to-all(f32[32,16,128]{2,1,0:T(8,128)} %apply.1), channel_id=1, replica_groups=mesh['member'=32,'row'=4,'col'=2] {'member'}, dimensions={0} | all-to-all | bytes 524288 | tf_op jit(solution)/shard_map/all_to_all | solution.py:268
  73.6 1.9 %unpack.1 = f32[1,3,2,16,512]{4,3,2,1,0:T(8,128)} custom-call(f32[32,16,128]{2,1,0:T(8,128)} %all_to_all.10.got_ref), custom_call_target="tpu_custom_call" | custom-call | tf_op jit(solution)/shard_map/unpack/pallas_call | solution.py:270
Async XLA Ops:
  1.6 14.6 %collective-permute-start = (bf16[7,8,512]{2,1,0:T(8,128)(2,1)}, bf16[7,8,512]{2,1,0:T(8,128)(2,1)S(1)}, u32[]{:S(2)}, u32[]{:S(2)}) collective-permute-start(bf16[7,8,512]{2,1,0:T(8,128)(2,1)} %get-tuple-element.12), channel_id=1, source_target_pairs={{2,0},{4,2},{6,4},{3,1},{5,3},{7,5},{10,8},{12,10},{14,12},{11,9},... | collective-permute-start | bytes 172040 | tf_op jit(solution)/shard_map/ppermute | solution.py:237
  2.9 13.3 %collective-permute-start.1 = (bf16[7,8,512]{2,1,0:T(8,128)(2,1)}, bf16[7,8,512]{2,1,0:T(8,128)(2,1)S(1)}, u32[]{:S(2)}, u32[]{:S(2)}) collective-permute-start(bf16[7,8,512]{2,1,0:T(8,128)(2,1)} %get-tuple-element.13), channel_id=1, source_target_pairs={{0,2},{2,4},{4,6},{1,3},{3,5},{5,7},{8,10},{10,12},{12,14},{9,11},... | collective-permute-start | bytes 172040 | tf_op jit(solution)/shard_map/ppermute | solution.py:238
  7.6 8.7 %collective-permute-start.2 = (bf16[2,7,16,128]{3,2,1,0:T(8,128)(2,1)}, bf16[2,7,16,128]{3,2,1,0:T(8,128)(2,1)S(1)}, u32[]{:S(2)}, u32[]{:S(2)}) collective-permute-start(bf16[2,7,16,128]{3,2,1,0:T(8,128)(2,1)} %get-tuple-element.14), channel_id=1, source_target_pairs={{0,1},{1,0},{2,3},{3,2},{4,5},{5,4},{6,7},{7,6},{8,9},{9,8},{10,11... | collective-permute-start | bytes 172040 | tf_op jit(solution)/shard_map/ppermute | solution.py:239
  9.0 6.2 %collective-permute-start.3 = (bf16[7,8,128]{2,1,0:T(8,128)(2,1)}, bf16[7,8,128]{2,1,0:T(8,128)(2,1)S(1)}, u32[]{:S(2)}, u32[]{:S(2)}) collective-permute-start(bf16[7,8,128]{2,1,0:T(8,128)(2,1)} %get-tuple-element.15), channel_id=1, source_target_pairs={{2,1},{3,0},{4,3},{5,2},{6,5},{7,4},{10,9},{11,8},{12,11},{13,10},... | collective-permute-start | bytes 43016 | tf_op jit(solution)/shard_map/ppermute | solution.py:241
  10.3 5.9 %collective-permute-start.4 = (bf16[7,8,128]{2,1,0:T(8,128)(2,1)}, bf16[7,8,128]{2,1,0:T(8,128)(2,1)S(1)}, u32[]{:S(2)}, u32[]{:S(2)}) collective-permute-start(bf16[7,8,128]{2,1,0:T(8,128)(2,1)} %get-tuple-element.16), channel_id=1, source_target_pairs={{0,3},{1,2},{2,5},{3,4},{4,7},{5,6},{8,11},{9,10},{10,13},{11,12},... | collective-permute-start | bytes 43016 | tf_op jit(solution)/shard_map/ppermute | solution.py:242
  15.2 1.1 %copy-start.4 = (bf16[7,8,128]{2,1,0:T(8,128)(2,1)}, bf16[7,8,128]{2,1,0:T(8,128)(2,1)S(1)}, u32[]{:S(2)}) copy-start(bf16[7,8,128]{2,1,0:T(8,128)(2,1)S(1)} %collective-permute-done.3.sbelow_ref) | copy-start | bytes 43012
  16.3 0.6 copy-start.5
  16.3 0.6 copy-start.1
  16.3 0.6 copy-start.2
  16.9 0.6 copy-start.3
  19.8 27.6 %all-to-all-start = ((bf16[32,48,128]{2,1,0:T(8,128)(2,1)}), bf16[32,48,128]{2,1,0:T(8,128)(2,1)S(1)}, u32[]{:S(2)}, u32[]{:S(2)}) async-start(bf16[32,48,128]{2,1,0:T(8,128)(2,1)} %get-tuple-element.17), calls=%async_computation | async-start | bytes 786432 | tf_op jit(solution)/shard_map/all_to_all | solution.py:252
  47.5 0.7 copy-start

commit v2 on v1

v2 whole, which is shorter than its diff:
```python
import jax
import jax.numpy as jnp
from jax import lax
from jax.experimental import pallas as pl
from jax.experimental.pallas import tpu as pltpu
from jax.sharding import PartitionSpec as P

SWEEPS = 4
VARS = 3
LEV = 2
ROWS = 16
COLS = 512
HALO = 4
STRIP = 32
WIN = STRIP + 2 * HALO
LANES = 128
F32 = jnp.float32
BF16 = jnp.bfloat16


def side_kernel(col_ref, pert_ref, prob_ref, cls_ref, side_ref):
    last = col_ref[0] == 0
    for plane in range(2 * VARS * LEV + 1):
        if plane < 2 * VARS * LEV:
            ref = pert_ref if plane < VARS * LEV else prob_ref
            v, l = plane % (VARS * LEV) // LEV, plane % LEV
            head, tail = ref[0, v, l, :, :LANES].astype(F32), ref[0, v, l, :, COLS - LANES :].astype(F32)
        else:
            head, tail = (cls_ref[:, :LANES] + 1).astype(F32), (cls_ref[:, COLS - LANES :] + 1).astype(F32)
        side_ref[plane] = jnp.where(last, tail, head).astype(BF16)


def pack_kernel(col_ref, strip_ref, pert_ref, prob_ref, cls_ref, side_ref, out_ref, cls_out_ref, wide_ref):
    first = col_ref[0] == 0
    blocks = COLS // LANES
    lane = lax.broadcasted_iota(jnp.int32, (ROWS, LANES), 1)
    upper = lax.broadcasted_iota(jnp.int32, (8, LANES), 0) < HALO

    def block(plane, at):
        if 0 <= at < blocks:
            span = slice(at * LANES, (at + 1) * LANES)
            if plane == 2 * VARS * LEV:
                return (cls_ref[:, span] + 1).astype(F32)
            ref = pert_ref if plane < VARS * LEV else prob_ref
            return ref[0, plane % (VARS * LEV) // LEV, plane % LEV, :, span].astype(F32)
        got = side_ref[plane].astype(F32)
        return jnp.where(first if at == blocks else jnp.logical_not(first), got, 0.0)

    for s in range(COLS // STRIP):
        start = s * STRIP - HALO
        at, off = start // LANES, start % LANES
        for l in range(LEV):
            both = []
            for kind in range(2):
                acc = jnp.zeros((ROWS, LANES), F32)
                for v in range(VARS):
                    plane = (kind * VARS + v) * LEV + l
                    shift = (WIN * v - off) % LANES
                    got = block(plane, at)
                    got = pltpu.roll(got, shift, 1) if shift else got
                    if off + WIN > LANES:
                        more = block(plane, at + 1)
                        more = pltpu.roll(more, shift, 1) if shift else more
                        got = jnp.where(lane < WIN * v + LANES - off, got, more)
                    acc = jnp.where((lane >= WIN * v) & (lane < WIN * (v + 1)), got, acc)
                both.append(acc)
            a, b = both
            groups = [
                jnp.where(upper, a[:8], pltpu.roll(b[:8], HALO, 0)),
                jnp.where(upper, pltpu.roll(a[8:], HALO, 0), b[8:]),
                jnp.where(upper, pltpu.roll(a[:8], HALO, 0), b[:8]),
                jnp.where(upper, a[8:], pltpu.roll(b[8:], HALO, 0)),
            ]
            for pair in range(2):
                out_ref[s * LEV + l, pair * ROWS : (pair + 1) * ROWS] = jnp.concatenate(
                    groups[2 * pair : 2 * pair + 2], axis=0
                ).astype(BF16)

    for at in range(-1, blocks + 1):
        wide_ref[:, (at + 1) * LANES : (at + 2) * LANES] = block(2 * VARS * LEV, at).astype(BF16)
    wide = wide_ref.shape[1]
    spot = lax.broadcasted_iota(jnp.int32, (wide, LANES), 0)
    lane = lax.broadcasted_iota(jnp.int32, (wide, LANES), 1)
    column = lane - jnp.where(lane >= WIN, WIN, 0) - jnp.where(lane >= 2 * WIN, WIN, 0)
    pick = (spot == LANES - HALO + STRIP * strip_ref[0] + column) & (lane < VARS * WIN)
    cls_out_ref[...] = jnp.dot(wide_ref[...], pick.astype(F32).astype(BF16), preferred_element_type=F32)


def edge_kernel(got_ref, cls_ref, up_ref, dn_ref):
    members = got_ref.shape[0]
    up_ref[:members] = got_ref[:, :8]
    dn_ref[:members] = got_ref[:, 8:16]
    up_ref[members] = cls_ref[:8].astype(BF16)
    dn_ref[members] = pltpu.roll(cls_ref[8:], HALO, 0).astype(BF16)


TOP = 8
TALL = TOP + ROWS + TOP
FORWARD = [
    (dy, dx)
    for dy in range(HALO + 1)
    for dx in range(-HALO, HALO + 1)
    if dy + abs(dx) <= HALO and (dy > 0 or dx >= 0)
]
EVERY = [(dy, dx) for dx in range(-HALO, HALO + 1) for dy in range(-HALO, HALO + 1) if abs(dy) + abs(dx) <= HALO]
AT = {d: i for i, d in enumerate(EVERY)}


def lanes_by(x, dx):
    return pltpu.roll(x, (-dx) % LANES, 1) if dx else x


def rows_by(x, dy):
    return pltpu.roll(x, (-dy) % x.shape[0], 0) if dy else x


def apply_kernel(
    row_ref, rates_ref, got_ref, cls_ref, below_ref, above_ref, out_ref, pert_ref, prob_ref, gram_ref, weight_ref
):
    members = got_ref.shape[0]
    has_below = row_ref[0] != row_ref[1] - 1
    has_above = row_ref[0] != 0
    blank = jnp.zeros((HALO, LANES), F32)

    def spread(m, _):
        tile = got_ref[m].astype(F32)
        below = jnp.where(has_below, below_ref[m].astype(F32), 0.0)
        above = jnp.where(has_above, above_ref[m].astype(F32), 0.0)
        for ref, at in ((pert_ref, 0), (prob_ref, HALO)):
            ref[m, 0 : TOP - HALO] = blank
            ref[m, TOP - HALO : TOP] = above[at : at + HALO]
            for group, to in enumerate((0, 12, 4, 8)):
                ref[m, TOP + to : TOP + to + HALO] = tile[8 * group + at : 8 * group + at + HALO]
            ref[m, TOP + ROWS : TOP + ROWS + HALO] = below[at : at + HALO]
            ref[m, TOP + ROWS + HALO : TALL] = blank
        return 0

    lax.fori_loop(0, members, spread, 0, unroll=2)

    cls = jnp.concatenate(
        [
            blank,
            jnp.where(has_above, above_ref[members, :HALO].astype(F32), 0.0),
            cls_ref[...],
            jnp.where(has_below, below_ref[members, :HALO].astype(F32), 0.0),
            blank,
        ],
        axis=0,
    )
    rate = jnp.zeros((TALL, LANES), F32)
    for k in range(rates_ref.shape[0]):
        rate = jnp.where(cls == float(k + 1), rates_ref[k], rate)

    steps = ((0, 1), (0, -1), (1, 0), (-1, 0))
    stay = 1.0 - 4.0 * rate
    coef = {(0, 0): stay}
    for e in steps:
        coef[e] = rate
    for sweep in range(1, SWEEPS):
        moved = {}
        for e in steps:
            for d, c in coef.items():
                to = (d[0] + e[0], d[1] + e[1])
                c = lanes_by(rows_by(c, e[0]), e[1])
                moved[to] = moved[to] + c if to in moved else c
        coef = {d: rate * moved[d] + (stay * coef[d] if d in coef else 0.0) for d in moved}
    scale = 1.0 / (members - 1)

    for b in range(3):
        row = TOP + 8 * b

        def products(m, acc):
            low = pert_ref[m, row : row + 8]
            high = [pert_ref[m, row - dy : row - dy + 8] for dy in range(HALO + 1)]
            near = {dx: lanes_by(low, dx) for dx in range(-HALO + 1, HALO + 1)}
            return tuple(a + high[dy] * near[dx] for a, (dy, dx) in zip(acc, FORWARD))

        acc = tuple(jnp.zeros((8, LANES), F32) for _ in FORWARD)
        acc = lax.fori_loop(0, members, products, acc, unroll=4)
        for i, a in enumerate(acc):
            gram_ref[i, 8 * b : 8 * b + 8] = a

    for i, (dy, dx) in enumerate(FORWARD):
        c = coef[(dy, dx)][TOP : TOP + ROWS] * scale
        weight_ref[AT[(dy, dx)]] = lanes_by(c * gram_ref[i, dy : dy + ROWS], -dx)
        if (dy, dx) != (0, 0):
            c = coef[(-dy, -dx)][TOP : TOP + ROWS] * scale
            weight_ref[AT[(-dy, -dx)]] = lanes_by(c, dx) * gram_ref[i, 0:ROWS]

    for b in range(2):

        def one_probe(p, _):
            rows = [prob_ref[p, TOP + 8 * b + dy : TOP + 8 * b + dy + 8] for dy in range(-HALO, HALO + 1)]
            total = None
            for dx in range(-HALO, HALO + 1):
                part = None
                for dy in range(-HALO + abs(dx), HALO - abs(dx) + 1):
                    term = weight_ref[AT[(dy, dx)], 8 * b : 8 * b + 8] * rows[dy + HALO]
                    part = term if part is None else part + term
                part = lanes_by(part, dx)
                total = part if total is None else total + part
            out_ref[p, 8 * b : 8 * b + 8] = total
            return 0

        lax.fori_loop(0, members, one_probe, 0, unroll=4)


def unpack_kernel(got_ref, out_ref):
    lane = lax.broadcasted_iota(jnp.int32, (ROWS, LANES), 1)
    per = LANES // STRIP
    for v in range(VARS):
        for l in range(LEV):
            for at in range(COLS // LANES):
                acc = None
                for q in range(per):
                    got = got_ref[(at * per + q) * LEV + l]
                    shift = (STRIP * q - WIN * v - HALO) % LANES
                    got = pltpu.roll(got, shift, 1) if shift else got
                    acc = got if acc is None else jnp.where(lane >= STRIP * q, got, acc)
                out_ref[0, v, l, :, at * LANES : (at + 1) * LANES] = acc


def body(pert, probes, diff_class, class_rate):
    members = lax.axis_size("member")
    n_row = lax.axis_size("row")
    col = lax.axis_index("col").astype(jnp.int32).reshape(1)
    strip = (lax.axis_index("member") // LEV).astype(jnp.int32).reshape(1)
    vmem = pl.BlockSpec(memory_space=pltpu.VMEM)
    smem = pl.BlockSpec(memory_space=pltpu.SMEM)
    row = jnp.stack([lax.axis_index("row").astype(jnp.int32), jnp.int32(n_row)])
    planes = 2 * VARS * LEV + 1

    shape = pltpu.VMEM

    def near(x):
        return pltpu.with_memory_space_constraint(x, pltpu.VMEM)

    side = pl.pallas_call(
        side_kernel,
        in_specs=[smem, vmem, vmem, vmem],
        out_specs=vmem,
        out_shape=shape((planes, ROWS, LANES), BF16),
        name="side",
    )(col, pert, probes, diff_class)
    beside = lax.ppermute(side, "col", [(0, 1), (1, 0)])

    chunks, cls = pl.pallas_call(
        pack_kernel,
        in_specs=[smem] * 2 + [vmem] * 4,
        out_specs=[vmem] * 2,
        out_shape=[shape((members, 2 * ROWS, LANES), BF16), shape((ROWS, LANES), F32)],
        scratch_shapes=[pltpu.VMEM((ROWS, COLS + 2 * LANES), BF16)],
        name="pack",
    )(col, strip, pert, probes, diff_class, near(beside))

    got = lax.all_to_all(chunks, "member", 0, 0, tiled=True)

    edge = shape((members + 1, 8, LANES), BF16)
    up, dn = pl.pallas_call(
        edge_kernel,
        in_specs=[vmem] * 2,
        out_specs=[vmem] * 2,
        out_shape=[edge, edge],
        name="edges",
    )(near(got), near(cls))
    below = lax.ppermute(up, "row", [(i, (i - 1) % n_row) for i in range(n_row)])
    above = lax.ppermute(dn, "row", [(i, (i + 1) % n_row) for i in range(n_row)])

    part = pl.pallas_call(
        apply_kernel,
        in_specs=[smem, smem] + [vmem] * 4,
        out_specs=vmem,
        out_shape=shape((members, ROWS, LANES), F32),
        scratch_shapes=[
            pltpu.VMEM((members, TALL, LANES), F32),
            pltpu.VMEM((members, TALL, LANES), F32),
            pltpu.VMEM((len(FORWARD), 24, LANES), F32),
            pltpu.VMEM((len(EVERY), ROWS, LANES), F32),
        ],
        name="apply",
    )(row, class_rate, near(got), near(cls), near(below), near(above))

    back = lax.all_to_all(part, "member", 0, 0, tiled=True)

    return pl.pallas_call(
        unpack_kernel,
        in_specs=[vmem],
        out_specs=vmem,
        out_shape=jax.ShapeDtypeStruct((1, VARS, LEV, ROWS, COLS), F32),
        name="unpack",
    )(near(back))


def solution(mesh):
    placed = (
        P("member", None, None, "row", "col"),
        P("member", None, None, "row", "col"),
        P("row", "col"),
        P(),
    )
    return jax.shard_map(
        body,
        mesh=mesh,
        in_specs=placed,
        out_specs=P("member", None, None, "row", "col"),
        check_vma=False,
    )
```

time: 76.4 us -> 65 us (0.85)
  starting transfers between devices: 27 us -> 18.1 us
  Pallas kernels: 12.5 us -> 9.51 us
  waiting for transfers between devices: 15.2 us -> 18.1 us
  local copies, waits for them, and re-layouts: 1.98 us -> 0 us
    ppermute x4 -> x2, starting transfers between devices: 12.1 us -> 2.81 us  [the longest x1 2.81 us: body(): lax.ppermute(up, 'row', [(i, (i - 1) % n_row) for i in range(n_row)])]
    ppermute x4 -> x2, waiting for transfers between devices: 1.03 us -> 3.68 us  [the longest x1 3 us: body(): lax.ppermute(dn, 'row', [(i, (i + 1) % n_row) for i in range(n_row)])]
    pallas_call x3 -> x4, Pallas kernels: 10.7 us -> 8.56 us  [the longest x1 5.55 us: body(): pl.pallas_call(apply_kernel, in_specs=[smem, smem] + [vmem] * 4, out_spec...]
    unnamed x12 -> x0, local copies, waits for them, and re-layouts: 1.98 us -> none
    ppermute x1, waiting for transfers between devices: 0.01 us -> 1.52 us  [body(): beside = lax.ppermute(side, 'col', [(0, 1), (1, 0)])]
    all_to_all x1, waiting for transfers between devices: 14.2 us -> 12.9 us  [body(): got = lax.all_to_all(chunks, 'member', 0, 0, tiled=True)]
    pallas_call x1, Pallas kernels: 1.9 us -> 0.95 us  [body(): pl.pallas_call(unpack_kernel, in_specs=[vmem], out_specs=vmem, out_shape=...]
  transfers between devices with their start and end apart: 6 -> 4, of which waited for: 2 -> 4; matrix products, arithmetic and copies ran while one was open for 0% -> 1% of each run, Pallas kernels for 0% -> 0%
where the time goes in v2:
time: 65 us; the launch traced here: 64.7 us
  blocking collectives  18.3 us (28%)
  starting transfers between devices  18.1 us (28%)
  waiting for transfers between devices  18.1 us (28%)
  Pallas kernels  9.51 us (15%)
  other arithmetic  0.66 us (1%)
    all_to_all x1, blocking collectives, body(): back = lax.all_to_all(part, 'member', 0, 0, tiled=True)  18.3 us
    all_to_all x1, starting transfers between devices, body(): got = lax.all_to_all(chunks, 'member', 0, 0, tiled=True)  13.2 us
    all_to_all x1, waiting for transfers between devices, body(): got = lax.all_to_all(chunks, 'member', 0, 0, tiled=True)  12.9 us
    pallas_call x1, Pallas kernels, body(): pl.pallas_call(apply_kernel, in_specs=[smem, smem] + [vmem] * 4, out_spec...  5.55 us
    ppermute x1, waiting for transfers between devices, body(): lax.ppermute(dn, 'row', [(i, (i + 1) % n_row) for i in range(n_row)])  3 us
    ppermute x1, starting transfers between devices, body(): lax.ppermute(up, 'row', [(i, (i - 1) % n_row) for i in range(n_row)])  2.81 us
    ppermute x1, starting transfers between devices, body(): beside = lax.ppermute(side, 'col', [(0, 1), (1, 0)])  2.12 us
    pallas_call x1, Pallas kernels, body(): pl.pallas_call(pack_kernel, in_specs=[smem] * 2 + [vmem] * 4, out_specs=[...  2.04 us
  transfers between devices with their start and end apart: 4, of which 4 were waited for; matrix products, arithmetic and copies ran while one was open for 1% of the time, Pallas kernels for 0%

profile of v2, /device:TPU:1, one launch (start us, length us, event | category | flops | bytes accessed | tf_op | source)
XLA Modules:
  0.0 64.7 jit_solution(13059903225672181952)
XLA Ops:
  0.0 1.0 %side.1 = bf16[13,16,128]{2,1,0:T(8,128)(2,1)S(1)} custom-call(s32[1]{0:T(128)} %bitcast.1.col_ref, bf16[1,3,2,16,512]{4,3,2,1,0:T(8,128)(2,1)} %pert_ref.3, bf16[1,3,2,16,512]{4,3,2,1,0:T(8,128)(2,1)} %prob_ref.3, s32[16,512]{1,0:T(8,128)} %cls_ref.3), custom_call_target="tpu_custom_call" | custom-call | tf_op jit(solution)/shard_map/side/pallas_call | solution.py:238
  1.0 2.1 %collective-permute-start = (bf16[13,16,128]{2,1,0:T(8,128)(2,1)S(1)}, bf16[13,16,128]{2,1,0:T(8,128)(2,1)S(1)}, u32[]{:S(2)}, u32[]{:S(2)}) collective-permute-start(bf16[13,16,128]{2,1,0:T(8,128)(2,1)S(1)} %side.1), channel_id=1, source_target_pairs={{0,1},{1,0},{2,3},{3,2},{4,5},{5,4},{6,7},{7,6},{8,9},{9,8},{10,11... | collective-permute-start | bytes 159752 | tf_op jit(solution)/shard_map/ppermute | solution.py:245
  3.1 1.5 %collective-permute-done.side_ref = bf16[13,16,128]{2,1,0:T(8,128)(2,1)S(1)} collective-permute-done((bf16[13,16,128]{2,1,0:T(8,128)(2,1)S(1)}, bf16[13,16,128]{2,1,0:T(8,128)(2,1)S(1)}, u32[]{:S(2)}, u32[]{:S(2)}) %collective-permute-start) | collective-permute-done | bytes 53280 | tf_op jit(solution)/shard_map/ppermute | solution.py:245
  4.6 2.0 %pack.1 = (bf16[32,32,128]{2,1,0:T(8,128)(2,1)}, f32[16,128]{1,0:T(8,128)S(1)}) custom-call(s32[1]{0:T(128)} %bitcast.1.col_ref, s32[1]{0:T(128)} %bitcast.2.strip_ref, bf16[1,3,2,16,512]{4,3,2,1,0:T(8,128)(2,1)} %pert_ref.3, bf16[1,3,2,16,512]{4,3,2,1,0:T(8,128)(2,1)} %prob_ref.3, s32[16,512]{1,0:T(8,128)} %cls_ref.3, ...), custom_call_target="tpu_custom_call" | custom-call | tf_op jit(solution)/shard_map/pack/pallas_call | solution.py:247
  6.6 13.2 %all-to-all-start = ((bf16[32,32,128]{2,1,0:T(8,128)(2,1)}), bf16[32,32,128]{2,1,0:T(8,128)(2,1)S(1)}, u32[]{:S(2)}, u32[]{:S(2)}) async-start(bf16[32,32,128]{2,1,0:T(8,128)(2,1)} %get-tuple-element.9), calls=%async_computation | async-start | bytes 524288 | tf_op jit(solution)/shard_map/all_to_all | solution.py:256
  19.8 12.9 %all-to-all-done.got_ref = bf16[32,32,128]{2,1,0:T(8,128)(2,1)S(1)} async-done(((bf16[32,32,128]{2,1,0:T(8,128)(2,1)}), bf16[32,32,128]{2,1,0:T(8,128)(2,1)S(1)}, u32[]{:S(2)}, u32[]{:S(2)}) %all-to-all-start) | async-done | bytes 262176 | tf_op jit(solution)/shard_map/all_to_all | solution.py:256
  32.8 2.8 %collective-permute-start.1 = (bf16[33,8,128]{2,1,0:T(8,128)(2,1)S(1)}, bf16[33,8,128]{2,1,0:T(8,128)(2,1)S(1)}, u32[]{:S(2)}, u32[]{:S(2)}) collective-permute-start(bf16[33,8,128]{2,1,0:T(8,128)(2,1)S(1)} %get-tuple-element.11), channel_id=1, source_target_pairs={{0,6},{2,0},{4,2},{6,4},{1,7},{3,1},{5,3},{7,5},{8,14},{10,8},{12,... | collective-permute-start | bytes 202760 | tf_op jit(solution)/shard_map/ppermute | solution.py:266
  35.6 0.0 collective-permute-start.2
  35.6 0.7 %pad_add_fusion.row_ref = s32[2]{0:T(128)} fusion(s32[1]{0:T(128)} %constant.24.clone.1, s32[1]{0:T(128)} %bitcast), kind=kLoop, calls=%fused_computation | loop fusion | flops 2 | bytes 16 | tf_op jit(solution)/shard_map/stack | solution.py:230
  36.2 0.7 %collective-permute-done.1.below_ref = bf16[33,8,128]{2,1,0:T(8,128)(2,1)S(1)} collective-permute-done((bf16[33,8,128]{2,1,0:T(8,128)(2,1)S(1)}, bf16[33,8,128]{2,1,0:T(8,128)(2,1)S(1)}, u32[]{:S(2)}, u32[]{:S(2)}) %collective-permute-start.1) | collective-permute-done | bytes 67616 | tf_op jit(solution)/shard_map/ppermute | solution.py:266
  36.9 3.0 %collective-permute-done.2.above_ref = bf16[33,8,128]{2,1,0:T(8,128)(2,1)S(1)} collective-permute-done((bf16[33,8,128]{2,1,0:T(8,128)(2,1)S(1)}, bf16[33,8,128]{2,1,0:T(8,128)(2,1)S(1)}, u32[]{:S(2)}, u32[]{:S(2)}) %collective-permute-start.2) | collective-permute-done | bytes 67616 | tf_op jit(solution)/shard_map/ppermute | solution.py:267
  39.9 5.5 %apply.1 = f32[32,16,128]{2,1,0:T(8,128)S(1)} custom-call(s32[2]{0:T(128)} %pad_add_fusion.row_ref, f32[8]{0:T(128)} %rates_ref.1, bf16[32,32,128]{2,1,0:T(8,128)(2,1)S(1)} %all-to-all-done.got_ref, f32[16,128]{1,0:T(8,128)S(1)} %get-tuple-element.10.cls_ref, bf16[33,8,128]{2,1,0:T(8,128)(2,1)S(1)} %collective-permute-done.1.below_ref, ...), custom_call_target="tpu_custom_call" | custom-call | tf_op jit(solution)/shard_map/apply/pallas_call | solution.py:269
  45.5 18.3 %all_to_all.10.got_ref = f32[32,16,128]{2,1,0:T(8,128)S(1)} all-to-all(f32[32,16,128]{2,1,0:T(8,128)S(1)} %apply.1), channel_id=1, replica_groups=mesh['member'=32,'row'=4,'col'=2] {'member'}, dimensions={0} | all-to-all | bytes 524288 | tf_op jit(solution)/shard_map/all_to_all | solution.py:283
  63.7 0.9 %unpack.1 = f32[1,3,2,16,512]{4,3,2,1,0:T(8,128)} custom-call(f32[32,16,128]{2,1,0:T(8,128)S(1)} %all_to_all.10.got_ref), custom_call_target="tpu_custom_call" | custom-call | tf_op jit(solution)/shard_map/unpack/pallas_call | solution.py:285
  (1 shorter events, 0.0 us)
Async XLA Ops:
  1.0 3.6 %collective-permute-start = (bf16[13,16,128]{2,1,0:T(8,128)(2,1)S(1)}, bf16[13,16,128]{2,1,0:T(8,128)(2,1)S(1)}, u32[]{:S(2)}, u32[]{:S(2)}) collective-permute-start(bf16[13,16,128]{2,1,0:T(8,128)(2,1)S(1)} %side.1), channel_id=1, source_target_pairs={{0,1},{1,0},{2,3},{3,2},{4,5},{5,4},{6,7},{7,6},{8,9},{9,8},{10,11... | collective-permute-start | bytes 159752 | tf_op jit(solution)/shard_map/ppermute | solution.py:245
  6.6 26.1 %all-to-all-start = ((bf16[32,32,128]{2,1,0:T(8,128)(2,1)}), bf16[32,32,128]{2,1,0:T(8,128)(2,1)S(1)}, u32[]{:S(2)}, u32[]{:S(2)}) async-start(bf16[32,32,128]{2,1,0:T(8,128)(2,1)} %get-tuple-element.9), calls=%async_computation | async-start | bytes 524288 | tf_op jit(solution)/shard_map/all_to_all | solution.py:256
  32.8 4.2 %collective-permute-start.1 = (bf16[33,8,128]{2,1,0:T(8,128)(2,1)S(1)}, bf16[33,8,128]{2,1,0:T(8,128)(2,1)S(1)}, u32[]{:S(2)}, u32[]{:S(2)}) collective-permute-start(bf16[33,8,128]{2,1,0:T(8,128)(2,1)S(1)} %get-tuple-element.11), channel_id=1, source_target_pairs={{0,6},{2,0},{4,2},{6,4},{1,7},{3,1},{5,3},{7,5},{8,14},{10,8},{12,... | collective-permute-start | bytes 202760 | tf_op jit(solution)/shard_map/ppermute | solution.py:266
  35.6 4.3 %collective-permute-start.2 = (bf16[33,8,128]{2,1,0:T(8,128)(2,1)S(1)}, bf16[33,8,128]{2,1,0:T(8,128)(2,1)S(1)}, u32[]{:S(2)}, u32[]{:S(2)}) collective-permute-start(bf16[33,8,128]{2,1,0:T(8,128)(2,1)S(1)} %get-tuple-element.12), channel_id=1, source_target_pairs={{0,2},{2,4},{4,6},{6,0},{1,3},{3,5},{5,7},{7,1},{8,10},{10,12},{12... | collective-permute-start | bytes 202760 | tf_op jit(solution)/shard_map/ppermute | solution.py:267

commit v3 on v2

v3 whole, which is shorter than its diff:
```python
import functools

import jax
import jax.numpy as jnp
from jax import lax
from jax.experimental import pallas as pl
from jax.experimental.pallas import tpu as pltpu
from jax.sharding import PartitionSpec as P

SWEEPS = 4
VARS = 3
LEV = 2
ROWS = 16
COLS = 512
HALO = 4
STRIP = 32
WIN = STRIP + 2 * HALO
LANES = 128
F32 = jnp.float32
BF16 = jnp.bfloat16


def side_kernel(col_ref, pert_ref, prob_ref, cls_ref, side_ref):
    last = col_ref[0] == 0
    for plane in range(2 * VARS * LEV + 1):
        if plane < 2 * VARS * LEV:
            ref = pert_ref if plane < VARS * LEV else prob_ref
            v, l = plane % (VARS * LEV) // LEV, plane % LEV
            head, tail = ref[0, v, l, :, :LANES].astype(F32), ref[0, v, l, :, COLS - LANES :].astype(F32)
        else:
            head, tail = (cls_ref[:, :LANES] + 1).astype(F32), (cls_ref[:, COLS - LANES :] + 1).astype(F32)
        side_ref[plane] = jnp.where(last, tail, head).astype(BF16)


def shared(strips, planes_at, out):
    lane = lax.broadcasted_iota(jnp.int32, (ROWS, LANES), 1)
    upper = lax.broadcasted_iota(jnp.int32, (8, LANES), 0) < HALO
    for s in strips:
        start = s * STRIP - HALO
        at, off = start // LANES, start % LANES
        for l in range(LEV):
            both = []
            for kind in range(2):
                acc = jnp.zeros((ROWS, LANES), F32)
                for v in range(VARS):
                    plane = (kind * VARS + v) * LEV + l
                    shift = (WIN * v - off) % LANES
                    got = planes_at(plane, at)
                    got = pltpu.roll(got, shift, 1) if shift else got
                    if off + WIN > LANES:
                        more = planes_at(plane, at + 1)
                        more = pltpu.roll(more, shift, 1) if shift else more
                        got = jnp.where(lane < WIN * v + LANES - off, got, more)
                    acc = jnp.where((lane >= WIN * v) & (lane < WIN * (v + 1)), got, acc)
                both.append(acc)
            a, b = both
            groups = [
                jnp.where(upper, a[:8], pltpu.roll(b[:8], HALO, 0)),
                jnp.where(upper, pltpu.roll(a[8:], HALO, 0), b[8:]),
                jnp.where(upper, pltpu.roll(a[:8], HALO, 0), b[:8]),
                jnp.where(upper, a[8:], pltpu.roll(b[8:], HALO, 0)),
            ]
            for pair in range(2):
                rows = jnp.concatenate(groups[2 * pair : 2 * pair + 2], axis=0)
                out(s * LEV + l, pair, rows.astype(BF16))


def pack_kernel(pert_ref, prob_ref, out_ref):
    def block(plane, at):
        ref = pert_ref if plane < VARS * LEV else prob_ref
        span = slice(at * LANES, (at + 1) * LANES)
        return ref[0, plane % (VARS * LEV) // LEV, plane % LEV, :, span].astype(F32)

    def out(owner, pair, rows):
        out_ref[owner, pair * ROWS : (pair + 1) * ROWS] = rows

    shared(range(1, COLS // STRIP - 1), block, out)


def patch_kernel(col_ref, pert0_ref, prob0_ref, pert1_ref, prob1_ref, side_ref, all_ref, out_ref, new_ref, sems):
    first = col_ref[0] == 0
    blocks = COLS // LANES
    owners = LEV * COLS // STRIP

    def block(plane, at):
        if at in (-1, blocks):
            got = side_ref[plane].astype(F32)
            return jnp.where(first if at == blocks else jnp.logical_not(first), got, 0.0)
        refs = (pert0_ref, prob0_ref) if at == 0 else (pert1_ref, prob1_ref)
        ref = refs[0] if plane < VARS * LEV else refs[1]
        return ref[0, plane % (VARS * LEV) // LEV, plane % LEV].astype(F32)

    def out(owner, pair, rows):
        slot = owner if owner < LEV else owner - owners + 2 * LEV
        new_ref[slot, pair * ROWS : (pair + 1) * ROWS] = rows

    shared((0, COLS // STRIP - 1), block, out)
    head = pltpu.make_async_copy(new_ref.at[0:LEV], out_ref.at[0:LEV], sems.at[0])
    tail = pltpu.make_async_copy(new_ref.at[LEV : 2 * LEV], out_ref.at[owners - LEV : owners], sems.at[1])
    head.start()
    tail.start()
    head.wait()
    tail.wait()


def class_kernel(col_ref, strip_ref, cls_ref, side_ref, cls_out_ref, wide_ref):
    first = col_ref[0] == 0
    got = side_ref[2 * VARS * LEV].astype(F32)
    wide_ref[:, :LANES] = jnp.where(jnp.logical_not(first), got, 0.0).astype(BF16)
    wide_ref[:, LANES : LANES + COLS] = (cls_ref[...] + 1).astype(F32).astype(BF16)
    wide_ref[:, LANES + COLS :] = jnp.where(first, got, 0.0).astype(BF16)
    wide = wide_ref.shape[1]
    spot = lax.broadcasted_iota(jnp.int32, (wide, LANES), 0)
    lane = lax.broadcasted_iota(jnp.int32, (wide, LANES), 1)
    column = lane - jnp.where(lane >= WIN, WIN, 0) - jnp.where(lane >= 2 * WIN, WIN, 0)
    pick = (spot == LANES - HALO + STRIP * strip_ref[0] + column) & (lane < VARS * WIN)
    cls_out_ref[...] = jnp.dot(wide_ref[...], pick.astype(F32).astype(BF16), preferred_element_type=F32)


def edge_kernel(got_ref, cls_ref, up_ref, dn_ref):
    members = got_ref.shape[0]
    up_ref[:members] = got_ref[:, :8]
    dn_ref[:members] = got_ref[:, 8:16]
    up_ref[members] = cls_ref[:8].astype(BF16)
    dn_ref[members] = pltpu.roll(cls_ref[8:], HALO, 0).astype(BF16)


TOP = 8
TALL = TOP + ROWS + TOP
FORWARD = [
    (dy, dx)
    for dy in range(HALO + 1)
    for dx in range(-HALO, HALO + 1)
    if dy + abs(dx) <= HALO and (dy > 0 or dx >= 0)
]
EVERY = [(dy, dx) for dx in range(-HALO, HALO + 1) for dy in range(-HALO, HALO + 1) if abs(dy) + abs(dx) <= HALO]
AT = {d: i for i, d in enumerate(EVERY)}


def lanes_by(x, dx):
    return pltpu.roll(x, (-dx) % LANES, 1) if dx else x


def own_kernel(got_ref, gram_ref, pert_ref):
    members = got_ref.shape[0]
    blank = jnp.zeros((TOP, LANES), F32)

    def spread(m, _):
        tile = got_ref[m].astype(F32)
        pert_ref[m, 0:TOP] = blank
        for group, to in enumerate((0, 12, 4, 8)):
            pert_ref[m, TOP + to : TOP + to + HALO] = tile[8 * group : 8 * group + HALO]
        return 0

    lax.fori_loop(0, members, spread, 0, unroll=4)
    for b in range(2):
        row = TOP + 8 * b

        def products(m, acc):
            low = pert_ref[m, row : row + 8]
            high = [pert_ref[m, row - dy : row - dy + 8] for dy in range(HALO + 1)]
            near = {dx: lanes_by(low, dx) for dx in range(-HALO + 1, HALO + 1)}
            return tuple(a + high[dy] * near[dx] for a, (dy, dx) in zip(acc, FORWARD))

        acc = tuple(jnp.zeros((8, LANES), F32) for _ in FORWARD)
        acc = lax.fori_loop(0, members, products, acc, unroll=4)
        for i, a in enumerate(acc):
            gram_ref[i, 8 * b : 8 * b + 8] = a


def apply_kernel(
    n_row, row_ref, rates_ref, got_ref, cls_ref, below_ref, above_ref, own_ref, out_ref,
    prob_ref, gram_ref, weight_ref, rate_ref,
):
    members = got_ref.shape[0]
    has_below = row_ref[0] != n_row - 1
    has_above = row_ref[0] != 0
    blank = jnp.zeros((HALO, LANES), F32)
    sub = lax.broadcasted_iota(jnp.int32, (8, LANES), 0)
    lane = lax.broadcasted_iota(jnp.int32, (8, LANES), 1)
    upper = sub < HALO
    crossing = [d for d in FORWARD if d[0] > 0]

    def spread(m, acc):
        tile = got_ref[m].astype(F32)
        below = jnp.where(has_below, below_ref[m].astype(F32), 0.0)
        above = jnp.where(has_above, above_ref[m].astype(F32), 0.0)
        prob_ref[m, 0 : TOP - HALO] = blank
        prob_ref[m, TOP - HALO : TOP] = above[HALO:]
        for group, to in enumerate((0, 12, 4, 8)):
            prob_ref[m, TOP + to : TOP + to + HALO] = tile[8 * group + HALO : 8 * group + 8]
        prob_ref[m, TOP + ROWS : TOP + ROWS + HALO] = below[HALO:]
        prob_ref[m, TOP + ROWS + HALO : TALL] = blank
        low = jnp.where(upper, tile[0:8], pltpu.roll(below, HALO, 0))
        high = jnp.where(upper, above, pltpu.roll(tile[8:16], HALO, 0))
        high = {dy: pltpu.roll(high, HALO + dy, 0) if dy < HALO else high for dy in range(1, HALO + 1)}
        near = {dx: lanes_by(low, dx) for dx in range(-HALO + 1, HALO)}
        return tuple(a + high[dy] * near[dx] for a, (dy, dx) in zip(acc, crossing))

    acc = tuple(jnp.zeros((8, LANES), F32) for _ in crossing)
    acc = dict(zip(crossing, lax.fori_loop(0, members, spread, acc, unroll=4)))
    for i, d in enumerate(FORWARD):
        gram_ref[i, 8:16] = own_ref[i, 8:16]
        if d in acc:
            gram_ref[i, 0:8] = own_ref[i, 0:8] + jnp.where(sub < d[0], acc[d], 0.0)
            gram_ref[i, 16:24] = pltpu.roll(acc[d], HALO, 0)
        else:
            gram_ref[i, 0:8] = own_ref[i, 0:8]

    cls = jnp.concatenate(
        [
            blank,
            jnp.where(has_above, above_ref[members, :HALO].astype(F32), 0.0),
            cls_ref[...],
            jnp.where(has_below, below_ref[members, :HALO].astype(F32), 0.0),
            blank,
        ],
        axis=0,
    )
    rate = jnp.zeros((TALL, LANES), F32)
    for k in range(rates_ref.shape[0]):
        rate = jnp.where(cls == float(k + 1), rates_ref[k], rate)
    rate_ref[...] = rate

    steps = ((0, 1), (0, -1), (1, 0), (-1, 0))
    at = {
        (dy, dx): lanes_by(rate_ref[TOP + dy : TOP + dy + ROWS], dx)
        for dy, dx in EVERY
        if abs(dy) + abs(dx) < HALO
    }
    coef = {(0, 0): 1.0 - 4.0 * at[(0, 0)]}
    for e in steps:
        coef[e] = at[(0, 0)]
    for sweep in range(1, SWEEPS):
        flow = {d: c * at[d] for d, c in coef.items()}
        to = {(d[0] + e[0], d[1] + e[1]) for d in flow for e in steps}
        new = {}
        for d in EVERY:
            if d not in to:
                continue
            terms = [flow[(d[0] - e[0], d[1] - e[1])] for e in steps if (d[0] - e[0], d[1] - e[1]) in flow]
            if d in coef:
                terms.append(coef[d] - 4.0 * flow[d])
            total = terms[0]
            for t in terms[1:]:
                total = total + t
            new[d] = total
        coef = new
    scale = 1.0 / (members - 1)

    for i, (dy, dx) in enumerate(FORWARD):
        weight_ref[AT[(dy, dx)]] = lanes_by(coef[(dy, dx)] * scale * gram_ref[i, dy : dy + ROWS], -dx)
        if (dy, dx) != (0, 0):
            weight_ref[AT[(-dy, -dx)]] = lanes_by(coef[(-dy, -dx)] * scale, dx) * gram_ref[i, 0:ROWS]

    def one_probe(p, _):
        both = []
        for b in range(2):
            rows = [prob_ref[p, TOP + 8 * b + dy : TOP + 8 * b + dy + 8] for dy in range(-HALO, HALO + 1)]
            total = None
            for dx in range(-HALO, HALO + 1):
                part = None
                for dy in range(-HALO + abs(dx), HALO - abs(dx) + 1):
                    term = weight_ref[AT[(dy, dx)], 8 * b : 8 * b + 8] * rows[dy + HALO]
                    part = term if part is None else part + term
                part = lanes_by(part, dx)
                total = part if total is None else total + part
            both.append(total)
        a, b = both
        first = jnp.where(lane < STRIP, lanes_by(a, HALO), lanes_by(a, HALO + 8))
        first = jnp.where(lane < 2 * STRIP, first, lanes_by(a, HALO + 16))
        first = jnp.where(lane < 3 * STRIP, first, lanes_by(b, HALO - 3 * STRIP))
        rest = jnp.where(lane < STRIP, lanes_by(b, WIN + HALO), lanes_by(b, 2 * WIN + HALO - STRIP))
        rest = jnp.where(lane < 2 * STRIP, rest, pltpu.roll(lanes_by(rest, 2 * STRIP), HALO, 0))
        out_ref[p, 0] = first[:HALO]
        out_ref[p, 1] = first[HALO:]
        out_ref[p, 2] = rest[:HALO]
        return 0

    lax.fori_loop(0, members, one_probe, 0, unroll=4)


def unpack_kernel(got_ref, out_ref):
    lane = lax.broadcasted_iota(jnp.int32, (ROWS, LANES), 1)
    per = LANES // STRIP

    def moved(x, shift):
        shift %= LANES
        return pltpu.roll(x, shift, 1) if shift else x

    for l in range(LEV):
        for at in range(COLS // LANES):
            acc = [None] * VARS
            for q in range(per):
                got = got_ref[(at * per + q) * LEV + l]
                top = jnp.concatenate([got[0], got[1]], axis=0)
                low = jnp.concatenate([got[2], moved(got[2], 2 * STRIP)], axis=0)
                for v in range(VARS):
                    under = moved(top, STRIP * (q - VARS)) if v == 0 else moved(low, STRIP * (q - v + 1))
                    piece = jnp.concatenate([moved(top, STRIP * (q - v)), under], axis=0)
                    acc[v] = piece if acc[v] is None else jnp.where(lane >= STRIP * q, piece, acc[v])
            for v in range(VARS):
                out_ref[0, v, l, :, at * LANES : (at + 1) * LANES] = acc[v]


def body(pert, probes, diff_class, class_rate):
    members = lax.axis_size("member")
    n_row = lax.axis_size("row")
    col = lax.axis_index("col").astype(jnp.int32).reshape(1)
    strip = (lax.axis_index("member") // LEV).astype(jnp.int32).reshape(1)
    vmem = pl.BlockSpec(memory_space=pltpu.VMEM)
    smem = pl.BlockSpec(memory_space=pltpu.SMEM)
    row = lax.axis_index("row").astype(jnp.int32).reshape(1)
    planes = 2 * VARS * LEV + 1

    shape = pltpu.VMEM

    def near(x):
        return pltpu.with_memory_space_constraint(x, pltpu.VMEM)

    side = pl.pallas_call(
        side_kernel,
        in_specs=[smem, vmem, vmem, vmem],
        out_specs=vmem,
        out_shape=shape((planes, ROWS, LANES), BF16),
        name="side",
    )(col, pert, probes, diff_class)
    beside = lax.ppermute(side, "col", [(0, 1), (1, 0)])

    chunk = jax.ShapeDtypeStruct((members, 2 * ROWS, LANES), BF16)
    inner = pl.pallas_call(pack_kernel, in_specs=[vmem] * 2, out_specs=vmem, out_shape=chunk, name="pack")(pert, probes)
    ends = [
        pl.BlockSpec((1, VARS, LEV, ROWS, LANES), lambda i: (0, 0, 0, 0, 0)),
        pl.BlockSpec((1, VARS, LEV, ROWS, LANES), lambda i: (0, 0, 0, 0, COLS // LANES - 1)),
    ]
    chunks = pl.pallas_call(
        patch_kernel,
        grid=(1,),
        in_specs=[smem, ends[0], ends[0], ends[1], ends[1], vmem, pl.BlockSpec(memory_space=pl.ANY)],
        out_specs=pl.BlockSpec(memory_space=pl.ANY),
        out_shape=chunk,
        scratch_shapes=[pltpu.VMEM((2 * LEV, 2 * ROWS, LANES), BF16), pltpu.SemaphoreType.DMA((2,))],
        input_output_aliases={6: 0},
        name="patch",
    )(col, pert, probes, pert, probes, near(beside), inner)
    cls = pl.pallas_call(
        class_kernel,
        in_specs=[smem] * 2 + [vmem] * 2,
        out_specs=vmem,
        out_shape=shape((ROWS, LANES), F32),
        scratch_shapes=[pltpu.VMEM((ROWS, COLS + 2 * LANES), BF16)],
        name="classes",
    )(col, strip, diff_class, near(beside))

    got = lax.all_to_all(chunks, "member", 0, 0, tiled=True)

    edge = shape((members + 1, 8, LANES), BF16)
    up, dn = pl.pallas_call(
        edge_kernel,
        in_specs=[vmem] * 2,
        out_specs=[vmem] * 2,
        out_shape=[edge, edge],
        name="edges",
    )(near(got), near(cls))
    below = lax.ppermute(up, "row", [(i, (i - 1) % n_row) for i in range(n_row)])
    above = lax.ppermute(dn, "row", [(i, (i + 1) % n_row) for i in range(n_row)])

    own = pl.pallas_call(
        own_kernel,
        in_specs=[vmem],
        out_specs=vmem,
        out_shape=shape((len(FORWARD), ROWS, LANES), F32),
        scratch_shapes=[pltpu.VMEM((members, TOP + ROWS, LANES), F32)],
        name="own",
    )(near(got))

    part = pl.pallas_call(
        functools.partial(apply_kernel, n_row),
        in_specs=[smem, smem] + [vmem] * 5,
        out_specs=vmem,
        out_shape=shape((members, VARS, HALO, LANES), F32),
        scratch_shapes=[
            pltpu.VMEM((members, TALL, LANES), F32),
            pltpu.VMEM((len(FORWARD), 24, LANES), F32),
            pltpu.VMEM((len(EVERY), ROWS, LANES), F32),
            pltpu.VMEM((TALL, LANES), F32),
        ],
        name="apply",
    )(row, class_rate, near(got), near(cls), near(below), near(above), near(own))

    back = lax.all_to_all(part, "member", 0, 0, tiled=True)

    return pl.pallas_call(
        unpack_kernel,
        in_specs=[vmem],
        out_specs=vmem,
        out_shape=jax.ShapeDtypeStruct((1, VARS, LEV, ROWS, COLS), F32),
        name="unpack",
    )(near(back))


def solution(mesh):
    placed = (
        P("member", None, None, "row", "col"),
        P("member", None, None, "row", "col"),
        P("row", "col"),
        P(),
    )
    return jax.shard_map(
        body,
        mesh=mesh,
        in_specs=placed,
        out_specs=P("member", None, None, "row", "col"),
        check_vma=False,
    )
```

time: 65 us -> 62.1 us (0.955)
  waiting for transfers between devices: 18.1 us -> 14.7 us
  Pallas kernels: 9.51 us -> 12.1 us
  blocking collectives: 18.3 us -> 17.2 us
  other arithmetic: 0.66 us -> 0 us
    pallas_call x2 -> x5, Pallas kernels: 7.58 us -> 9.8 us  [the longest x1 3.73 us: body(): pl.pallas_call(functools.partial(apply_kernel, n_row), in_specs=[smem, sm...]
    ppermute x1, waiting for transfers between devices: 1.52 us -> 0.01 us  [body(): beside = lax.ppermute(side, 'col', [(0, 1), (1, 0)])]
    all_to_all x1, blocking collectives: 18.3 us -> 17.2 us  [body(): back = lax.all_to_all(part, 'member', 0, 0, tiled=True)]
    all_to_all x1, waiting for transfers between devices: 12.9 us -> 12 us  [body(): got = lax.all_to_all(chunks, 'member', 0, 0, tiled=True)]
    ppermute x1, waiting for transfers between devices: 0.68 us -> 0.01 us  [body(): lax.ppermute(up, 'row', [(i, (i - 1) % n_row) for i in range(n_row)])]
    another operation x1 -> x0, other arithmetic: 0.66 us -> none  [body(): row = jnp.stack([lax.axis_index('row').astype(jnp.int32), jnp.int32(n_row)])]
  transfers between devices with their start and end apart: 4 -> 4, of which waited for: 4 -> 2; matrix products, arithmetic and copies ran while one was open for 1% -> 0% of each run, Pallas kernels for 0% -> 7%
where the time goes in v3:
time: 62.1 us; the launch traced here: 61.7 us
  starting transfers between devices  17.7 us (29%)
  blocking collectives  17.2 us (28%)
  waiting for transfers between devices  14.7 us (24%)
  Pallas kernels  12.1 us (19%)
    all_to_all x1, blocking collectives, body(): back = lax.all_to_all(part, 'member', 0, 0, tiled=True)  17.2 us
    all_to_all x1, starting transfers between devices, body(): got = lax.all_to_all(chunks, 'member', 0, 0, tiled=True)  12.7 us
    all_to_all x1, waiting for transfers between devices, body(): got = lax.all_to_all(chunks, 'member', 0, 0, tiled=True)  12 us
    pallas_call x1, Pallas kernels, body(): pl.pallas_call(functools.partial(apply_kernel, n_row), in_specs=[smem, sm...  3.73 us
    ppermute x1, starting transfers between devices, body(): lax.ppermute(up, 'row', [(i, (i - 1) % n_row) for i in range(n_row)])  2.81 us
    ppermute x1, waiting for transfers between devices, body(): lax.ppermute(dn, 'row', [(i, (i + 1) % n_row) for i in range(n_row)])  2.69 us
    ppermute x1, starting transfers between devices, body(): beside = lax.ppermute(side, 'col', [(0, 1), (1, 0)])  2.12 us
    pallas_call x1, Pallas kernels, body(): pl.pallas_call(pack_kernel, in_specs=[vmem] * 2, out_specs=vmem, out_shap...  1.96 us
  transfers between devices with their start and end apart: 4, of which 2 were waited for; matrix products, arithmetic and copies ran while one was open for 0% of the time, Pallas kernels for 7%

profile of v3, /device:TPU:1, one launch (start us, length us, event | category | flops | bytes accessed | tf_op | source)
XLA Modules:
  0.0 61.7 jit_solution(8123850749917969949)
XLA Ops:
  0.0 1.0 %side.1 = bf16[13,16,128]{2,1,0:T(8,128)(2,1)S(1)} custom-call(s32[1]{0:T(128)} %bitcast.1.col_ref, bf16[1,3,2,16,512]{4,3,2,1,0:T(8,128)(2,1)} %pert1_ref.1, bf16[1,3,2,16,512]{4,3,2,1,0:T(8,128)(2,1)} %prob1_ref.1, s32[16,512]{1,0:T(8,128)} %cls_ref.3), custom_call_target="tpu_custom_call" | custom-call | tf_op jit(solution)/shard_map/side/pallas_call | solution.py:321
  1.0 2.1 %collective-permute-start = (bf16[13,16,128]{2,1,0:T(8,128)(2,1)S(1)}, bf16[13,16,128]{2,1,0:T(8,128)(2,1)S(1)}, u32[]{:S(2)}, u32[]{:S(2)}) collective-permute-start(bf16[13,16,128]{2,1,0:T(8,128)(2,1)S(1)} %side.1), channel_id=1, source_target_pairs={{0,1},{1,0},{2,3},{3,2},{4,5},{5,4},{6,7},{7,6},{8,9},{9,8},{10,11... | collective-permute-start | bytes 159752 | tf_op jit(solution)/shard_map/ppermute | solution.py:328
  3.1 2.0 %pack.1.all_ref = bf16[32,32,128]{2,1,0:T(8,128)(2,1)} custom-call(bf16[1,3,2,16,512]{4,3,2,1,0:T(8,128)(2,1)} %pert1_ref.1, bf16[1,3,2,16,512]{4,3,2,1,0:T(8,128)(2,1)} %prob1_ref.1), custom_call_target="tpu_custom_call" | custom-call | tf_op jit(solution)/shard_map/pack/pallas_call | solution.py:331
  5.0 0.0 collective-permute-done.side_ref
  5.0 1.6 %patch.1 = bf16[32,32,128]{2,1,0:T(8,128)(2,1)} custom-call(s32[1]{0:T(128)} %bitcast.1.col_ref, bf16[1,3,2,16,512]{4,3,2,1,0:T(8,128)(2,1)} %pert1_ref.1, bf16[1,3,2,16,512]{4,3,2,1,0:T(8,128)(2,1)} %prob1_ref.1, bf16[1,3,2,16,512]{4,3,2,1,0:T(8,128)(2,1)} %pert1_ref.1, bf16[1,3,2,16,512]{4,3,2,1,0:T(8,128)(2,1)} %prob1_ref.1, ...), custom_call_target="tpu_custom_call", output_to_operand_aliasing={{}: (6, {})} | custom-call | tf_op jit(solution)/shard_map/patch/pallas_call | solution.py:336
  6.6 12.7 %all-to-all-start = ((bf16[32,32,128]{2,1,0:T(8,128)(2,1)}), bf16[32,32,128]{2,1,0:T(8,128)(2,1)S(1)}, u32[]{:S(2)}, u32[]{:S(2)}) async-start(bf16[32,32,128]{2,1,0:T(8,128)(2,1)} %patch.1), calls=%async_computation | async-start | bytes 524288 | tf_op jit(solution)/shard_map/all_to_all | solution.py:355
  19.3 0.9 %classes.1.cls_ref = f32[16,128]{1,0:T(8,128)S(1)} custom-call(s32[1]{0:T(128)} %bitcast.1.col_ref, s32[1]{0:T(128)} %bitcast.2.strip_ref, s32[16,512]{1,0:T(8,128)} %cls_ref.3, bf16[13,16,128]{2,1,0:T(8,128)(2,1)S(1)} %collective-permute-done.side_ref), custom_call_target="tpu_custom_call" | custom-call | tf_op jit(solution)/shard_map/classes/pallas_call | solution.py:346
  20.3 12.0 %all-to-all-done.got_ref = bf16[32,32,128]{2,1,0:T(8,128)(2,1)S(1)} async-done(((bf16[32,32,128]{2,1,0:T(8,128)(2,1)}), bf16[32,32,128]{2,1,0:T(8,128)(2,1)S(1)}, u32[]{:S(2)}, u32[]{:S(2)}) %all-to-all-start) | async-done | bytes 262176 | tf_op jit(solution)/shard_map/all_to_all | solution.py:355
  32.3 2.8 %collective-permute-start.1 = (bf16[33,8,128]{2,1,0:T(8,128)(2,1)S(1)}, bf16[33,8,128]{2,1,0:T(8,128)(2,1)S(1)}, u32[]{:S(2)}, u32[]{:S(2)}) collective-permute-start(bf16[33,8,128]{2,1,0:T(8,128)(2,1)S(1)} %get-tuple-element.7), channel_id=1, source_target_pairs={{0,6},{2,0},{4,2},{6,4},{1,7},{3,1},{5,3},{7,5},{8,14},{10,8},{12,... | collective-permute-start | bytes 202760 | tf_op jit(solution)/shard_map/ppermute | solution.py:365
  35.1 0.0 collective-permute-start.2
  35.1 1.6 %own.1.own_ref = f32[21,16,128]{2,1,0:T(8,128)S(1)} custom-call(bf16[32,32,128]{2,1,0:T(8,128)(2,1)S(1)} %all-to-all-done.got_ref), custom_call_target="tpu_custom_call" | custom-call | tf_op jit(solution)/shard_map/own/pallas_call | solution.py:368
  36.8 0.0 collective-permute-done.1.below_ref
  36.8 2.7 %collective-permute-done.2.above_ref = bf16[33,8,128]{2,1,0:T(8,128)(2,1)S(1)} collective-permute-done((bf16[33,8,128]{2,1,0:T(8,128)(2,1)S(1)}, bf16[33,8,128]{2,1,0:T(8,128)(2,1)S(1)}, u32[]{:S(2)}, u32[]{:S(2)}) %collective-permute-start.2) | collective-permute-done | bytes 67616 | tf_op jit(solution)/shard_map/ppermute | solution.py:366
  39.5 3.7 %apply.1 = f32[32,3,4,128]{3,2,1,0:T(4,128)S(1)} custom-call(s32[1]{0:T(128)} %bitcast.row_ref, f32[8]{0:T(128)} %rates_ref.1, bf16[32,32,128]{2,1,0:T(8,128)(2,1)S(1)} %all-to-all-done.got_ref, f32[16,128]{1,0:T(8,128)S(1)} %classes.1.cls_ref, bf16[33,8,128]{2,1,0:T(8,128)(2,1)S(1)} %collective-permute-done.1.below_ref, ...), custom_call_target="tpu_custom_call" | custom-call | tf_op jit(solution)/shard_map/apply/pallas_call | solution.py:377
  43.2 17.2 %all_to_all.10.got_ref = f32[32,3,4,128]{3,2,1,0:T(4,128)S(1)} all-to-all(f32[32,3,4,128]{3,2,1,0:T(4,128)S(1)} %apply.1), channel_id=1, replica_groups=mesh['member'=32,'row'=4,'col'=2] {'member'}, dimensions={0} | all-to-all | bytes 393216 | tf_op jit(solution)/shard_map/all_to_all | solution.py:391
  60.3 1.4 %unpack.1 = f32[1,3,2,16,512]{4,3,2,1,0:T(8,128)} custom-call(f32[32,3,4,128]{3,2,1,0:T(4,128)S(1)} %all_to_all.10.got_ref), custom_call_target="tpu_custom_call" | custom-call | tf_op jit(solution)/shard_map/unpack/pallas_call | solution.py:393
  (1 shorter events, 0.0 us)
Async XLA Ops:
  1.0 4.1 %collective-permute-start = (bf16[13,16,128]{2,1,0:T(8,128)(2,1)S(1)}, bf16[13,16,128]{2,1,0:T(8,128)(2,1)S(1)}, u32[]{:S(2)}, u32[]{:S(2)}) collective-permute-start(bf16[13,16,128]{2,1,0:T(8,128)(2,1)S(1)} %side.1), channel_id=1, source_target_pairs={{0,1},{1,0},{2,3},{3,2},{4,5},{5,4},{6,7},{7,6},{8,9},{9,8},{10,11... | collective-permute-start | bytes 159752 | tf_op jit(solution)/shard_map/ppermute | solution.py:328
  6.6 25.7 %all-to-all-start = ((bf16[32,32,128]{2,1,0:T(8,128)(2,1)}), bf16[32,32,128]{2,1,0:T(8,128)(2,1)S(1)}, u32[]{:S(2)}, u32[]{:S(2)}) async-start(bf16[32,32,128]{2,1,0:T(8,128)(2,1)} %patch.1), calls=%async_computation | async-start | bytes 524288 | tf_op jit(solution)/shard_map/all_to_all | solution.py:355
  32.3 4.5 %collective-permute-start.1 = (bf16[33,8,128]{2,1,0:T(8,128)(2,1)S(1)}, bf16[33,8,128]{2,1,0:T(8,128)(2,1)S(1)}, u32[]{:S(2)}, u32[]{:S(2)}) collective-permute-start(bf16[33,8,128]{2,1,0:T(8,128)(2,1)S(1)} %get-tuple-element.7), channel_id=1, source_target_pairs={{0,6},{2,0},{4,2},{6,4},{1,7},{3,1},{5,3},{7,5},{8,14},{10,8},{12,... | collective-permute-start | bytes 202760 | tf_op jit(solution)/shard_map/ppermute | solution.py:365
  35.1 4.3 %collective-permute-start.2 = (bf16[33,8,128]{2,1,0:T(8,128)(2,1)S(1)}, bf16[33,8,128]{2,1,0:T(8,128)(2,1)S(1)}, u32[]{:S(2)}, u32[]{:S(2)}) collective-permute-start(bf16[33,8,128]{2,1,0:T(8,128)(2,1)S(1)} %get-tuple-element.8), channel_id=1, source_target_pairs={{0,2},{2,4},{4,6},{6,0},{1,3},{3,5},{5,7},{7,1},{8,10},{10,12},{12... | collective-permute-start | bytes 202760 | tf_op jit(solution)/shard_map/ppermute | solution.py:366

commit v4 on v3

v4 whole, which is shorter than its diff:
```python
import functools

import jax
import jax.numpy as jnp
from jax import lax
from jax.experimental import pallas as pl
from jax.experimental.pallas import tpu as pltpu
from jax.sharding import PartitionSpec as P

SWEEPS = 4
VARS = 3
LEV = 2
ROWS = 16
COLS = 512
HALO = 4
STRIP = 32
WIN = STRIP + 2 * HALO
LANES = 128
F32 = jnp.float32
BF16 = jnp.bfloat16


def grouped(a, b):
    upper = lax.broadcasted_iota(jnp.int32, (8, LANES), 0) < HALO
    groups = [
        jnp.where(upper, a[:8], pltpu.roll(b[:8], HALO, 0)),
        jnp.where(upper, pltpu.roll(a[8:], HALO, 0), b[8:]),
        jnp.where(upper, pltpu.roll(a[:8], HALO, 0), b[:8]),
        jnp.where(upper, a[8:], pltpu.roll(b[8:], HALO, 0)),
    ]
    return jnp.concatenate(groups, axis=0).astype(BF16)


def side_kernel(pert_ref, prob_ref, cls_ref, side_ref):
    last = lax.axis_index("col") == 0
    lane = lax.broadcasted_iota(jnp.int32, (ROWS, LANES), 1)
    use = [
        (lane >= WIN * v + jnp.where(last, 0, WIN - HALO)) & (lane < WIN * v + jnp.where(last, HALO, WIN))
        for v in range(VARS)
    ]

    def placed(blocks):
        acc = jnp.zeros((ROWS, LANES), F32)
        for v, (head, tail) in enumerate(blocks):
            tail = pltpu.roll(tail, (WIN * v + HALO) % LANES, 1)
            head = pltpu.roll(head, (WIN * v + WIN - HALO) % LANES, 1)
            acc = jnp.where(use[v], jnp.where(last, tail, head), acc)
        return acc

    def ends(ref, v, l):
        return ref[0, v, l, :, :LANES].astype(F32), ref[0, v, l, :, COLS - LANES :].astype(F32)

    for l in range(LEV):
        a, b = (placed([ends(ref, v, l) for v in range(VARS)]) for ref in (pert_ref, prob_ref))
        side_ref[l * 2 * ROWS : (l + 1) * 2 * ROWS] = grouped(a, b)
    cls = ((cls_ref[:, :LANES] + 1).astype(F32), (cls_ref[:, COLS - LANES :] + 1).astype(F32))
    side_ref[LEV * 2 * ROWS :] = placed([cls] * VARS).astype(BF16)


def pack_kernel(pert_ref, prob_ref, cls_ref, out_ref, cls_out_ref, wide_ref):
    lane = lax.broadcasted_iota(jnp.int32, (ROWS, LANES), 1)
    blocks = COLS // LANES

    def block(ref, v, l, at, shift):
        got = ref[0, v, l, :, at * LANES : (at + 1) * LANES].astype(F32)
        return pltpu.roll(got, shift, 1) if shift else got

    for s in range(COLS // STRIP):
        start = s * STRIP - HALO
        at, off = start // LANES, start % LANES
        for l in range(LEV):
            both = []
            for ref in (pert_ref, prob_ref):
                acc = jnp.zeros((ROWS, LANES), F32)
                for v in range(VARS):
                    shift = (WIN * v - off) % LANES
                    low, high = WIN * v, WIN * (v + 1)
                    split = low + LANES - off
                    if at >= 0:
                        use = (lane >= low) & (lane < min(high, split))
                        acc = jnp.where(use, block(ref, v, l, at, shift), acc)
                    if split < high and at + 1 < blocks:
                        use = (lane >= split) & (lane < high)
                        acc = jnp.where(use, block(ref, v, l, at + 1, shift), acc)
                both.append(acc)
            out_ref[s * LEV + l] = grouped(*both)

    zero = jnp.zeros((ROWS, LANES), BF16)
    wide_ref[:, :LANES] = zero
    wide_ref[:, LANES : LANES + COLS] = (cls_ref[...] + 1).astype(F32).astype(BF16)
    wide_ref[:, LANES + COLS :] = zero
    strip = lax.axis_index("member") // LEV
    wide = wide_ref.shape[1]
    spot = lax.broadcasted_iota(jnp.int32, (wide, LANES), 0)
    lane = lax.broadcasted_iota(jnp.int32, (wide, LANES), 1)
    column = lane - jnp.where(lane >= WIN, WIN, 0) - jnp.where(lane >= 2 * WIN, WIN, 0)
    pick = (spot == LANES - HALO + STRIP * strip + column) & (lane < VARS * WIN)
    cls_out_ref[...] = jnp.dot(wide_ref[...], pick.astype(F32).astype(BF16), preferred_element_type=F32)


def patch_kernel(side_ref, inner_ref, cls_ref, out_ref, cls_out_ref):
    first = lax.axis_index("col") == 0
    strip = lax.axis_index("member") // LEV
    end = COLS // STRIP - 1
    for l in range(LEV):
        side = side_ref[l * 2 * ROWS : (l + 1) * 2 * ROWS].astype(F32)
        for s, here in ((0, jnp.logical_not(first)), (end, first)):
            at = s * LEV + l
            out_ref[at] = (inner_ref[at].astype(F32) + jnp.where(here, side, 0.0)).astype(BF16)
    mine = strip == jnp.where(first, end, 0)
    cls_out_ref[...] = cls_ref[...] + jnp.where(mine, side_ref[LEV * 2 * ROWS :].astype(F32), 0.0)


def edge_kernel(got_ref, cls_ref, up_ref, dn_ref):
    members = got_ref.shape[0]
    up_ref[:members] = got_ref[:, :8]
    dn_ref[:members] = got_ref[:, 8:16]
    up_ref[members] = cls_ref[:8].astype(BF16)
    dn_ref[members] = pltpu.roll(cls_ref[8:], HALO, 0).astype(BF16)


TOP = 8
TALL = TOP + ROWS + TOP
FORWARD = [
    (dy, dx)
    for dy in range(HALO + 1)
    for dx in range(-HALO, HALO + 1)
    if dy + abs(dx) <= HALO and (dy > 0 or dx >= 0)
]
EVERY = [(dy, dx) for dx in range(-HALO, HALO + 1) for dy in range(-HALO, HALO + 1) if abs(dy) + abs(dx) <= HALO]
AT = {d: i for i, d in enumerate(EVERY)}


def lanes_by(x, dx):
    return pltpu.roll(x, (-dx) % LANES, 1) if dx else x


def own_kernel(got_ref, gram_ref, prob_ref, pert_ref):
    members = got_ref.shape[0]
    blank = jnp.zeros((TOP, LANES), F32)

    def spread(m, _):
        tile = got_ref[m].astype(F32)
        pert_ref[m, 0:TOP] = blank
        for group, to in enumerate((0, 12, 4, 8)):
            pert_ref[m, TOP + to : TOP + to + HALO] = tile[8 * group : 8 * group + HALO]
            prob_ref[m, TOP + to : TOP + to + HALO] = tile[8 * group + HALO : 8 * group + 8]
        return 0

    lax.fori_loop(0, members, spread, 0, unroll=4)
    for b in range(2):
        row = TOP + 8 * b

        def products(m, acc):
            low = pert_ref[m, row : row + 8]
            high = [pert_ref[m, row - dy : row - dy + 8] for dy in range(HALO + 1)]
            near = {dx: lanes_by(low, dx) for dx in range(-HALO + 1, HALO + 1)}
            return tuple(a + high[dy] * near[dx] for a, (dy, dx) in zip(acc, FORWARD))

        acc = tuple(jnp.zeros((8, LANES), F32) for _ in FORWARD)
        acc = lax.fori_loop(0, members, products, acc, unroll=4)
        for i, a in enumerate(acc):
            gram_ref[i, 8 * b : 8 * b + 8] = a


def apply_kernel(
    n_row, rates_ref, got_ref, cls_ref, below_ref, above_ref, own_ref, part_ref, out_ref,
    prob_ref, gram_ref, weight_ref, rate_ref,
):
    members = got_ref.shape[0]
    has_below = lax.axis_index("row") != n_row - 1
    has_above = lax.axis_index("row") != 0
    blank = jnp.zeros((HALO, LANES), F32)
    sub = lax.broadcasted_iota(jnp.int32, (8, LANES), 0)
    lane = lax.broadcasted_iota(jnp.int32, (8, LANES), 1)
    upper = sub < HALO
    crossing = [d for d in FORWARD if d[0] > 0]

    def spread(m, acc):
        tile = got_ref[m, :ROWS].astype(F32)
        below = jnp.where(has_below, below_ref[m].astype(F32), 0.0)
        above = jnp.where(has_above, above_ref[m].astype(F32), 0.0)
        prob_ref[m, TOP - HALO : TOP] = above[HALO:]
        prob_ref[m, TOP + ROWS : TOP + ROWS + HALO] = below[HALO:]
        low = jnp.where(upper, tile[0:8], pltpu.roll(below, HALO, 0))
        high = jnp.where(upper, above, pltpu.roll(tile[8:16], HALO, 0))
        high = {dy: pltpu.roll(high, HALO + dy, 0) if dy < HALO else high for dy in range(1, HALO + 1)}
        near = {dx: lanes_by(low, dx) for dx in range(-HALO + 1, HALO)}
        return tuple(a + high[dy] * near[dx] for a, (dy, dx) in zip(acc, crossing))

    acc = tuple(jnp.zeros((8, LANES), F32) for _ in crossing)
    acc = dict(zip(crossing, lax.fori_loop(0, members, spread, acc, unroll=4)))
    for i, d in enumerate(FORWARD):
        gram_ref[i, 8:16] = own_ref[i, 8:16]
        if d in acc:
            gram_ref[i, 0:8] = own_ref[i, 0:8] + jnp.where(sub < d[0], acc[d], 0.0)
            gram_ref[i, 16:24] = pltpu.roll(acc[d], HALO, 0)
        else:
            gram_ref[i, 0:8] = own_ref[i, 0:8]

    cls = jnp.concatenate(
        [
            blank,
            jnp.where(has_above, above_ref[members, :HALO].astype(F32), 0.0),
            cls_ref[...],
            jnp.where(has_below, below_ref[members, :HALO].astype(F32), 0.0),
            blank,
        ],
        axis=0,
    )
    rate = jnp.zeros((TALL, LANES), F32)
    for k in range(rates_ref.shape[0]):
        rate = jnp.where(cls == float(k + 1), rates_ref[k], rate)
    rate_ref[...] = rate

    steps = ((0, 1), (0, -1), (1, 0), (-1, 0))
    at = {
        (dy, dx): lanes_by(rate_ref[TOP + dy : TOP + dy + ROWS], dx)
        for dy, dx in EVERY
        if abs(dy) + abs(dx) < HALO
    }
    coef = {(0, 0): 1.0 - 4.0 * at[(0, 0)]}
    for e in steps:
        coef[e] = at[(0, 0)]
    for sweep in range(1, SWEEPS):
        flow = {d: c * at[d] for d, c in coef.items()}
        to = {(d[0] + e[0], d[1] + e[1]) for d in flow for e in steps}
        new = {}
        for d in EVERY:
            if d not in to:
                continue
            terms = [flow[(d[0] - e[0], d[1] - e[1])] for e in steps if (d[0] - e[0], d[1] - e[1]) in flow]
            if d in coef:
                terms.append(coef[d] - 4.0 * flow[d])
            total = terms[0]
            for t in terms[1:]:
                total = total + t
            new[d] = total
        coef = new
    scale = 1.0 / (members - 1)

    for i, (dy, dx) in enumerate(FORWARD):
        weight_ref[AT[(dy, dx)]] = lanes_by(coef[(dy, dx)] * scale * gram_ref[i, dy : dy + ROWS], -dx)
        if (dy, dx) != (0, 0):
            weight_ref[AT[(-dy, -dx)]] = lanes_by(coef[(-dy, -dx)] * scale, dx) * gram_ref[i, 0:ROWS]

    def probe_pair(i, _):
        pair = (2 * i, 2 * i + 1)
        both = [[], []]
        for b in range(2):
            rows = [
                [prob_ref[p, TOP + 8 * b + dy : TOP + 8 * b + dy + 8] for dy in range(-HALO, HALO + 1)] for p in pair
            ]
            total = [None, None]
            for dx in range(-HALO, HALO + 1):
                part = [None, None]
                for dy in range(-HALO + abs(dx), HALO - abs(dx) + 1):
                    weight = weight_ref[AT[(dy, dx)], 8 * b : 8 * b + 8]
                    for j in range(2):
                        term = weight * rows[j][dy + HALO]
                        part[j] = term if part[j] is None else part[j] + term
                for j in range(2):
                    moved = lanes_by(part[j], dx)
                    total[j] = moved if total[j] is None else total[j] + moved
            for j in range(2):
                both[j].append(total[j])
        for p, (a, b) in zip(pair, both):
            first = jnp.where(lane < STRIP, lanes_by(a, HALO), lanes_by(a, HALO + 8))
            first = jnp.where(lane < 2 * STRIP, first, lanes_by(a, HALO + 16))
            first = jnp.where(lane < 3 * STRIP, first, lanes_by(b, HALO - 3 * STRIP))
            rest = jnp.where(lane < STRIP, lanes_by(b, WIN + HALO), lanes_by(b, 2 * WIN + HALO - STRIP))
            rest = jnp.where(lane < 2 * STRIP, rest, pltpu.roll(lanes_by(rest, 2 * STRIP), HALO, 0))
            out_ref[p, 0] = first[:HALO]
            out_ref[p, 1] = first[HALO:]
            out_ref[p, 2] = rest[:HALO]
        return 0

    lax.fori_loop(0, members // 2, probe_pair, 0, unroll=2)


def unpack_kernel(got_ref, out_ref):
    lane = lax.broadcasted_iota(jnp.int32, (ROWS, LANES), 1)
    per = LANES // STRIP

    def moved(x, shift):
        shift %= LANES
        return pltpu.roll(x, shift, 1) if shift else x

    for l in range(LEV):
        for at in range(COLS // LANES):
            acc = [None] * VARS
            for q in range(per):
                got = got_ref[(at * per + q) * LEV + l]
                top = jnp.concatenate([got[0], got[1]], axis=0)
                low = jnp.concatenate([got[2], moved(got[2], 2 * STRIP)], axis=0)
                for v in range(VARS):
                    under = moved(top, STRIP * (q - VARS)) if v == 0 else moved(low, STRIP * (q - v + 1))
                    piece = jnp.concatenate([moved(top, STRIP * (q - v)), under], axis=0)
                    acc[v] = piece if acc[v] is None else jnp.where(lane >= STRIP * q, piece, acc[v])
            for v in range(VARS):
                out_ref[0, v, l, :, at * LANES : (at + 1) * LANES] = acc[v]


def body(pert, probes, diff_class, class_rate):
    members = lax.axis_size("member")
    n_row = lax.axis_size("row")
    vmem = pl.BlockSpec(memory_space=pltpu.VMEM)
    smem = pl.BlockSpec(memory_space=pltpu.SMEM)
    shape = pltpu.VMEM

    def near(x):
        return pltpu.with_memory_space_constraint(x, pltpu.VMEM)

    side = pl.pallas_call(
        side_kernel,
        in_specs=[vmem] * 3,
        out_specs=vmem,
        out_shape=shape(((2 * LEV + 1) * ROWS, LANES), BF16),
        name="side",
    )(pert, probes, diff_class)
    beside = lax.ppermute(side, "col", [(0, 1), (1, 0)])

    chunk, classes = shape((members, 2 * ROWS, LANES), BF16), shape((ROWS, LANES), F32)
    inner, cls = pl.pallas_call(
        pack_kernel,
        in_specs=[vmem] * 3,
        out_specs=[vmem] * 2,
        out_shape=[chunk, classes],
        scratch_shapes=[pltpu.VMEM((ROWS, COLS + 2 * LANES), BF16)],
        name="pack",
    )(pert, probes, diff_class)
    chunks, cls = pl.pallas_call(
        patch_kernel,
        in_specs=[vmem] * 3,
        out_specs=[vmem] * 2,
        out_shape=[chunk, classes],
        input_output_aliases={1: 0},
        name="patch",
    )(near(beside), near(inner), near(cls))

    got = lax.all_to_all(chunks, "member", 0, 0, tiled=True)

    edge = shape((members + 1, 8, LANES), BF16)
    up, dn = pl.pallas_call(
        edge_kernel,
        in_specs=[vmem] * 2,
        out_specs=[vmem] * 2,
        out_shape=[edge, edge],
        name="edges",
    )(near(got), near(cls))
    below = lax.ppermute(up, "row", [(i, (i - 1) % n_row) for i in range(n_row)])
    above = lax.ppermute(dn, "row", [(i, (i + 1) % n_row) for i in range(n_row)])

    tall = shape((members, TALL, LANES), F32)
    own, spread = pl.pallas_call(
        own_kernel,
        in_specs=[vmem],
        out_specs=[vmem] * 2,
        out_shape=[shape((len(FORWARD), ROWS, LANES), F32), tall],
        scratch_shapes=[pltpu.VMEM((members, TOP + ROWS, LANES), F32)],
        name="own",
    )(near(got))

    part, spread = pl.pallas_call(
        functools.partial(apply_kernel, n_row),
        in_specs=[smem] + [vmem] * 6,
        out_specs=[vmem] * 2,
        out_shape=[shape((members, VARS, HALO, LANES), F32), tall],
        input_output_aliases={6: 1},
        scratch_shapes=[
            pltpu.VMEM((len(FORWARD), 24, LANES), F32),
            pltpu.VMEM((len(EVERY), ROWS, LANES), F32),
            pltpu.VMEM((TALL, LANES), F32),
        ],
        name="apply",
    )(class_rate, near(got), near(cls), near(below), near(above), near(own), near(spread))

    back = lax.all_to_all(part, "member", 0, 0, tiled=True)

    return pl.pallas_call(
        unpack_kernel,
        in_specs=[vmem],
        out_specs=vmem,
        out_shape=jax.ShapeDtypeStruct((1, VARS, LEV, ROWS, COLS), F32),
        name="unpack",
    )(near(back))


def solution(mesh):
    placed = (
        P("member", None, None, "row", "col"),
        P("member", None, None, "row", "col"),
        P("row", "col"),
        P(),
    )
    return jax.shard_map(
        body,
        mesh=mesh,
        in_specs=placed,
        out_specs=P("member", None, None, "row", "col"),
        check_vma=False,
    )
```

time: 62.1 us -> 59.9 us (0.965)
  blocking collectives: 17.2 us -> 42.9 us
  starting transfers between devices: 17.7 us -> 4.93 us
  waiting for transfers between devices: 14.7 us -> 2.67 us
  Pallas kernels: 12.1 us -> 9.13 us
    all_to_all x0 -> x1, blocking collectives: none -> 25.7 us  [body(): got = lax.all_to_all(chunks, 'member', 0, 0, tiled=True)]
    all_to_all x1 -> x0, starting transfers between devices: 12.7 us -> none  [body(): got = lax.all_to_all(chunks, 'member', 0, 0, tiled=True)]
    all_to_all x1 -> x0, waiting for transfers between devices: 12 us -> none  [body(): got = lax.all_to_all(chunks, 'member', 0, 0, tiled=True)]
    pallas_call x6 -> x5, Pallas kernels: 10.8 us -> 7.74 us  [the longest x1 3.71 us: body(): pl.pallas_call(functools.partial(apply_kernel, n_row), in_specs=[smem] +...]
  transfers between devices with their start and end apart: 4 -> 3, of which waited for: 2 -> 1; matrix products, arithmetic and copies ran while one was open for 0% -> 0% of each run, Pallas kernels for 7% -> 5%
where the time goes in v4:
time: 59.9 us; the launch traced here: 59.7 us
  blocking collectives  42.9 us (72%)
  Pallas kernels  9.13 us (15%)
  starting transfers between devices  4.93 us (8%)
  waiting for transfers between devices  2.67 us (4%)
    all_to_all x1, blocking collectives, body(): got = lax.all_to_all(chunks, 'member', 0, 0, tiled=True)  25.7 us
    all_to_all x1, blocking collectives, body(): back = lax.all_to_all(part, 'member', 0, 0, tiled=True)  17.2 us
    pallas_call x1, Pallas kernels, body(): pl.pallas_call(functools.partial(apply_kernel, n_row), in_specs=[smem] +...  3.71 us
    ppermute x1, starting transfers between devices, body(): lax.ppermute(up, 'row', [(i, (i - 1) % n_row) for i in range(n_row)])  2.81 us
    ppermute x1, waiting for transfers between devices, body(): lax.ppermute(dn, 'row', [(i, (i + 1) % n_row) for i in range(n_row)])  2.66 us
    ppermute x1, starting transfers between devices, body(): beside = lax.ppermute(side, 'col', [(0, 1), (1, 0)])  2.12 us
    pallas_call x1, Pallas kernels, body(): pl.pallas_call(own_kernel, in_specs=[vmem], out_specs=[vmem] * 2, out_sha...  1.66 us
    pallas_call x1, Pallas kernels, body(): pl.pallas_call(unpack_kernel, in_specs=[vmem], out_specs=vmem, out_shape=...  1.36 us
  transfers between devices with their start and end apart: 3, of which 1 were waited for; matrix products, arithmetic and copies ran while one was open for 0% of the time, Pallas kernels for 5%

profile of v4, /device:TPU:1, one launch (start us, length us, event | category | flops | bytes accessed | tf_op | source)
XLA Modules:
  0.0 59.7 jit_solution(13913570755517108521)
XLA Ops:
  0.0 1.0 %side.1 = bf16[80,128]{1,0:T(8,128)(2,1)S(1)} custom-call(bf16[1,3,2,16,512]{4,3,2,1,0:T(8,128)(2,1)} %pert_ref.3, bf16[1,3,2,16,512]{4,3,2,1,0:T(8,128)(2,1)} %prob_ref.3, s32[16,512]{1,0:T(8,128)} %cls_ref.3), custom_call_target="tpu_custom_call" | custom-call | tf_op jit(solution)/shard_map/side/pallas_call | solution.py:314
  1.0 2.1 %collective-permute-start = (bf16[80,128]{1,0:T(8,128)(2,1)S(1)}, bf16[80,128]{1,0:T(8,128)(2,1)S(1)}, u32[]{:S(2)}, u32[]{:S(2)}) collective-permute-start(bf16[80,128]{1,0:T(8,128)(2,1)S(1)} %side.1), channel_id=1, source_target_pairs={{0,1},{1,0},{2,3},{3,2},{4,5},{5,4},{6,7},{7,6},{8,9},{9,8},{10,11... | collective-permute-start | bytes 61448 | tf_op jit(solution)/shard_map/ppermute | solution.py:321
  3.2 1.3 %pack.1 = (bf16[32,32,128]{2,1,0:T(8,128)(2,1)S(1)}, f32[16,128]{1,0:T(8,128)S(1)}) custom-call(bf16[1,3,2,16,512]{4,3,2,1,0:T(8,128)(2,1)} %pert_ref.3, bf16[1,3,2,16,512]{4,3,2,1,0:T(8,128)(2,1)} %prob_ref.3, s32[16,512]{1,0:T(8,128)} %cls_ref.3), custom_call_target="tpu_custom_call" | custom-call | tf_op jit(solution)/shard_map/pack/pallas_call | solution.py:324
  4.5 0.0 collective-permute-done.side_ref
  4.5 25.7 %all_to_all.10.got_ref = bf16[32,32,128]{2,1,0:T(8,128)(2,1)S(1)} all-to-all(bf16[32,32,128]{2,1,0:T(8,128)(2,1)S(1)} %get-tuple-element.16), channel_id=1, replica_groups=mesh['member'=32,'row'=4,'col'=2] {'member'}, dimensions={0} | all-to-all | bytes 524288 | tf_op jit(solution)/shard_map/all_to_all | solution.py:341
  30.3 2.8 %collective-permute-start.1 = (bf16[33,8,128]{2,1,0:T(8,128)(2,1)S(1)}, bf16[33,8,128]{2,1,0:T(8,128)(2,1)S(1)}, u32[]{:S(2)}, u32[]{:S(2)}) collective-permute-start(bf16[33,8,128]{2,1,0:T(8,128)(2,1)S(1)} %get-tuple-element.18), channel_id=1, source_target_pairs={{0,6},{2,0},{4,2},{6,4},{1,7},{3,1},{5,3},{7,5},{8,14},{10,8},{12,... | collective-permute-start | bytes 202760 | tf_op jit(solution)/shard_map/ppermute | solution.py:351
  33.1 0.0 collective-permute-start.2
  33.1 1.7 %own.1 = (f32[21,16,128]{2,1,0:T(8,128)S(1)}, f32[32,32,128]{2,1,0:T(8,128)S(1)}) custom-call(bf16[32,32,128]{2,1,0:T(8,128)(2,1)S(1)} %all_to_all.10.got_ref), custom_call_target="tpu_custom_call" | custom-call | tf_op jit(solution)/shard_map/own/pallas_call | solution.py:355
  34.8 0.0 collective-permute-done.1.below_ref
  34.8 2.7 %collective-permute-done.2.above_ref = bf16[33,8,128]{2,1,0:T(8,128)(2,1)S(1)} collective-permute-done((bf16[33,8,128]{2,1,0:T(8,128)(2,1)S(1)}, bf16[33,8,128]{2,1,0:T(8,128)(2,1)S(1)}, u32[]{:S(2)}, u32[]{:S(2)}) %collective-permute-start.2) | collective-permute-done | bytes 67616 | tf_op jit(solution)/shard_map/ppermute | solution.py:352
  37.4 3.7 %apply.1 = (f32[32,3,4,128]{3,2,1,0:T(4,128)S(1)}, f32[32,32,128]{2,1,0:T(8,128)S(1)}) custom-call(f32[8]{0:T(128)} %rates_ref.1, bf16[32,32,128]{2,1,0:T(8,128)(2,1)S(1)} %all_to_all.10.got_ref, f32[16,128]{1,0:T(8,128)S(1)} %get-tuple-element.17.cls_ref, bf16[33,8,128]{2,1,0:T(8,128)(2,1)S(1)} %collective-permute-done.1.below_ref, ...), custom_call_target="tpu_custom_call", output_to_operand_aliasing={{1}: (6, {})} | custom-call | tf_op jit(solution)/shard_map/apply/pallas_call | solution.py:364
  41.1 17.2 %all_to_all.11.got_ref = f32[32,3,4,128]{3,2,1,0:T(4,128)S(1)} all-to-all(f32[32,3,4,128]{3,2,1,0:T(4,128)S(1)} %get-tuple-element.22), channel_id=1, replica_groups=mesh['member'=32,'row'=4,'col'=2] {'member'}, dimensions={0} | all-to-all | bytes 393216 | tf_op jit(solution)/shard_map/all_to_all | solution.py:378
  58.3 1.4 %unpack.1 = f32[1,3,2,16,512]{4,3,2,1,0:T(8,128)} custom-call(f32[32,3,4,128]{3,2,1,0:T(4,128)S(1)} %all_to_all.11.got_ref), custom_call_target="tpu_custom_call" | custom-call | tf_op jit(solution)/shard_map/unpack/pallas_call | solution.py:380
  (2 shorter events, 0.0 us)
Async XLA Ops:
  1.0 3.4 %collective-permute-start = (bf16[80,128]{1,0:T(8,128)(2,1)S(1)}, bf16[80,128]{1,0:T(8,128)(2,1)S(1)}, u32[]{:S(2)}, u32[]{:S(2)}) collective-permute-start(bf16[80,128]{1,0:T(8,128)(2,1)S(1)} %side.1), channel_id=1, source_target_pairs={{0,1},{1,0},{2,3},{3,2},{4,5},{5,4},{6,7},{7,6},{8,9},{9,8},{10,11... | collective-permute-start | bytes 61448 | tf_op jit(solution)/shard_map/ppermute | solution.py:321
  30.3 4.5 %collective-permute-start.1 = (bf16[33,8,128]{2,1,0:T(8,128)(2,1)S(1)}, bf16[33,8,128]{2,1,0:T(8,128)(2,1)S(1)}, u32[]{:S(2)}, u32[]{:S(2)}) collective-permute-start(bf16[33,8,128]{2,1,0:T(8,128)(2,1)S(1)} %get-tuple-element.18), channel_id=1, source_target_pairs={{0,6},{2,0},{4,2},{6,4},{1,7},{3,1},{5,3},{7,5},{8,14},{10,8},{12,... | collective-permute-start | bytes 202760 | tf_op jit(solution)/shard_map/ppermute | solution.py:351
  33.1 4.3 %collective-permute-start.2 = (bf16[33,8,128]{2,1,0:T(8,128)(2,1)S(1)}, bf16[33,8,128]{2,1,0:T(8,128)(2,1)S(1)}, u32[]{:S(2)}, u32[]{:S(2)}) collective-permute-start(bf16[33,8,128]{2,1,0:T(8,128)(2,1)S(1)} %get-tuple-element.19), channel_id=1, source_target_pairs={{0,2},{2,4},{4,6},{6,0},{1,3},{3,5},{5,7},{7,1},{8,10},{10,12},{12... | collective-permute-start | bytes 202760 | tf_op jit(solution)/shard_map/ppermute | solution.py:352

commit v5 on v4

--- a/solution.py
+++ b/solution.py
@@ -31,7 +31,7 @@
     return jnp.concatenate(groups, axis=0).astype(BF16)
 
 
-def side_kernel(pert_ref, prob_ref, cls_ref, side_ref):
+def side_kernel(pert0_ref, pert1_ref, prob0_ref, prob1_ref, cls0_ref, cls1_ref, side_ref):
     last = lax.axis_index("col") == 0
     lane = lax.broadcasted_iota(jnp.int32, (ROWS, LANES), 1)
     use = [
@@ -47,13 +47,13 @@
             acc = jnp.where(use[v], jnp.where(last, tail, head), acc)
         return acc
 
-    def ends(ref, v, l):
-        return ref[0, v, l, :, :LANES].astype(F32), ref[0, v, l, :, COLS - LANES :].astype(F32)
-
     for l in range(LEV):
-        a, b = (placed([ends(ref, v, l) for v in range(VARS)]) for ref in (pert_ref, prob_ref))
+        a, b = (
+            placed([(head[0, v, l].astype(F32), tail[0, v, l].astype(F32)) for v in range(VARS)])
+            for head, tail in ((pert0_ref, pert1_ref), (prob0_ref, prob1_ref))
+        )
         side_ref[l * 2 * ROWS : (l + 1) * 2 * ROWS] = grouped(a, b)
-    cls = ((cls_ref[:, :LANES] + 1).astype(F32), (cls_ref[:, COLS - LANES :] + 1).astype(F32))
+    cls = ((cls0_ref[...] + 1).astype(F32), (cls1_ref[...] + 1).astype(F32))
     side_ref[LEV * 2 * ROWS :] = placed([cls] * VARS).astype(BF16)
 
 
@@ -178,8 +178,7 @@
 
     def spread(m, acc):
         tile = got_ref[m, :ROWS].astype(F32)
-        below = jnp.where(has_below, below_ref[m].astype(F32), 0.0)
-        above = jnp.where(has_above, above_ref[m].astype(F32), 0.0)
+        below, above = below_ref[m].astype(F32), above_ref[m].astype(F32)
         prob_ref[m, TOP - HALO : TOP] = above[HALO:]
         prob_ref[m, TOP + ROWS : TOP + ROWS + HALO] = below[HALO:]
         low = jnp.where(upper, tile[0:8], pltpu.roll(below, HALO, 0))
@@ -189,7 +188,9 @@
         return tuple(a + high[dy] * near[dx] for a, (dy, dx) in zip(acc, crossing))
 
     acc = tuple(jnp.zeros((8, LANES), F32) for _ in crossing)
-    acc = dict(zip(crossing, lax.fori_loop(0, members, spread, acc, unroll=4)))
+    acc = lax.fori_loop(0, members, spread, acc, unroll=4)
+    inside = (upper & has_above) | (jnp.logical_not(upper) & has_below)
+    acc = {d: jnp.where(inside, a, 0.0) for d, a in zip(crossing, acc)}
     for i, d in enumerate(FORWARD):
         gram_ref[i, 8:16] = own_ref[i, 8:16]
         if d in acc:
@@ -214,38 +215,39 @@
     rate_ref[...] = rate
 
     steps = ((0, 1), (0, -1), (1, 0), (-1, 0))
-    at = {
-        (dy, dx): lanes_by(rate_ref[TOP + dy : TOP + dy + ROWS], dx)
-        for dy, dx in EVERY
-        if abs(dy) + abs(dx) < HALO
-    }
-    coef = {(0, 0): 1.0 - 4.0 * at[(0, 0)]}
-    for e in steps:
-        coef[e] = at[(0, 0)]
-    for sweep in range(1, SWEEPS):
-        flow = {d: c * at[d] for d, c in coef.items()}
-        to = {(d[0] + e[0], d[1] + e[1]) for d in flow for e in steps}
-        new = {}
-        for d in EVERY:
-            if d not in to:
-                continue
-            terms = [flow[(d[0] - e[0], d[1] - e[1])] for e in steps if (d[0] - e[0], d[1] - e[1]) in flow]
-            if d in coef:
-                terms.append(coef[d] - 4.0 * flow[d])
-            total = terms[0]
-            for t in terms[1:]:
-                total = total + t
-            new[d] = total
-        coef = new
     scale = 1.0 / (members - 1)
-
-    for i, (dy, dx) in enumerate(FORWARD):
-        weight_ref[AT[(dy, dx)]] = lanes_by(coef[(dy, dx)] * scale * gram_ref[i, dy : dy + ROWS], -dx)
-        if (dy, dx) != (0, 0):
-            weight_ref[AT[(-dy, -dx)]] = lanes_by(coef[(-dy, -dx)] * scale, dx) * gram_ref[i, 0:ROWS]
-
-    def probe_pair(i, _):
-        pair = (2 * i, 2 * i + 1)
+    for b in range(2):
+        at = {
+            (dy, dx): lanes_by(rate_ref[TOP + 8 * b + dy : TOP + 8 * b + dy + 8], dx)
+            for dy, dx in EVERY
+            if abs(dy) + abs(dx) < HALO
+        }
+        coef = {(0, 0): 1.0 - 4.0 * at[(0, 0)]}
+        for e in steps:
+            coef[e] = at[(0, 0)]
+        for sweep in range(1, SWEEPS):
+            flow = {d: c * at[d] for d, c in coef.items()}
+            to = {(d[0] + e[0], d[1] + e[1]) for d in flow for e in steps}
+            new = {}
+            for d in EVERY:
+                if d not in to:
+                    continue
+                terms = [flow[(d[0] - e[0], d[1] - e[1])] for e in steps if (d[0] - e[0], d[1] - e[1]) in flow]
+                if d in coef:
+                    terms.append(coef[d] - 4.0 * flow[d])
+                total = terms[0]
+                for t in terms[1:]:
+                    total = total + t
+                new[d] = total
+            coef = new
+        rows = slice(8 * b, 8 * b + 8)
+        for i, (dy, dx) in enumerate(FORWARD):
+            gram = gram_ref[i, 8 * b + dy : 8 * b + dy + 8]
+            weight_ref[AT[(dy, dx)], rows] = lanes_by(coef[(dy, dx)] * scale * gram, -dx)
+            if (dy, dx) != (0, 0):
+                weight_ref[AT[(-dy, -dx)], rows] = lanes_by(coef[(-dy, -dx)] * scale, dx) * gram_ref[i, rows]
+
+    def sums(pair):
         both = [[], []]
         for b in range(2):
             rows = [
@@ -264,7 +266,10 @@
                     total[j] = moved if total[j] is None else total[j] + moved
             for j in range(2):
                 both[j].append(total[j])
-        for p, (a, b) in zip(pair, both):
+        return tuple(both[0] + both[1])
+
+    def store(pair, done):
+        for p, a, b in ((pair[0], done[0], done[1]), (pair[1], done[2], done[3])):
             first = jnp.where(lane < STRIP, lanes_by(a, HALO), lanes_by(a, HALO + 8))
             first = jnp.where(lane < 2 * STRIP, first, lanes_by(a, HALO + 16))
             first = jnp.where(lane < 3 * STRIP, first, lanes_by(b, HALO - 3 * STRIP))
@@ -273,9 +278,13 @@
             out_ref[p, 0] = first[:HALO]
             out_ref[p, 1] = first[HALO:]
             out_ref[p, 2] = rest[:HALO]
+
+    def step(i, _):
+        pair = (2 * i, 2 * i + 1)
+        store(pair, sums(pair))
         return 0
 
-    lax.fori_loop(0, members // 2, probe_pair, 0, unroll=2)
+    lax.fori_loop(0, members // 2, step, 0, unroll=4)
 
 
 def unpack_kernel(got_ref, out_ref):
@@ -311,13 +320,17 @@
     def near(x):
         return pltpu.with_memory_space_constraint(x, pltpu.VMEM)
 
+    ends = (0, COLS // LANES - 1)
+    tile = [pl.BlockSpec((1, VARS, LEV, ROWS, LANES), functools.partial(lambda at, i: (0, 0, 0, 0, at), at)) for at in ends]
+    plane = [pl.BlockSpec((ROWS, LANES), functools.partial(lambda at, i: (0, at), at)) for at in ends]
     side = pl.pallas_call(
         side_kernel,
-        in_specs=[vmem] * 3,
+        grid=(1,),
+        in_specs=tile + tile + plane,
         out_specs=vmem,
         out_shape=shape(((2 * LEV + 1) * ROWS, LANES), BF16),
         name="side",
-    )(pert, probes, diff_class)
+    )(pert, pert, probes, probes, diff_class, diff_class)
     beside = lax.ppermute(side, "col", [(0, 1), (1, 0)])
 
     chunk, classes = shape((members, 2 * ROWS, LANES), BF16), shape((ROWS, LANES), F32)

time: 59.9 us -> 59.3 us (0.990)
  Pallas kernels: 9.13 us -> 8.46 us
where the time goes in v5:
time: 59.3 us; the launch traced here: 59 us
  blocking collectives  42.9 us (72%)
  Pallas kernels  8.46 us (14%)
  starting transfers between devices  4.93 us (8%)
  waiting for transfers between devices  2.67 us (5%)
    all_to_all x1, blocking collectives, body(): got = lax.all_to_all(chunks, 'member', 0, 0, tiled=True)  25.7 us
    all_to_all x1, blocking collectives, body(): back = lax.all_to_all(part, 'member', 0, 0, tiled=True)  17.2 us
    pallas_call x1, Pallas kernels, body(): pl.pallas_call(functools.partial(apply_kernel, n_row), in_specs=[smem] +...  3.17 us
    ppermute x1, starting transfers between devices, body(): lax.ppermute(up, 'row', [(i, (i - 1) % n_row) for i in range(n_row)])  2.81 us
    ppermute x1, waiting for transfers between devices, body(): lax.ppermute(dn, 'row', [(i, (i + 1) % n_row) for i in range(n_row)])  2.66 us
    ppermute x1, starting transfers between devices, body(): beside = lax.ppermute(side, 'col', [(0, 1), (1, 0)])  2.12 us
    pallas_call x1, Pallas kernels, body(): pl.pallas_call(own_kernel, in_specs=[vmem], out_specs=[vmem] * 2, out_sha...  1.66 us
    pallas_call x1, Pallas kernels, body(): pl.pallas_call(unpack_kernel, in_specs=[vmem], out_specs=vmem, out_shape=...  1.36 us
  transfers between devices with their start and end apart: 3, of which 1 were waited for; matrix products, arithmetic and copies ran while one was open for 0% of the time, Pallas kernels for 5%

profile of v5, /device:TPU:1, one launch (start us, length us, event | category | flops | bytes accessed | tf_op | source)
XLA Modules:
  0.0 59.0 jit_solution(9051775006089921119)
XLA Ops:
  0.0 0.9 %side.1 = bf16[80,128]{1,0:T(8,128)(2,1)S(1)} custom-call(bf16[1,3,2,16,512]{4,3,2,1,0:T(8,128)(2,1)} %pert_ref.1, bf16[1,3,2,16,512]{4,3,2,1,0:T(8,128)(2,1)} %pert_ref.1, bf16[1,3,2,16,512]{4,3,2,1,0:T(8,128)(2,1)} %prob_ref.1, bf16[1,3,2,16,512]{4,3,2,1,0:T(8,128)(2,1)} %prob_ref.1, s32[16,512]{1,0:T(8,128)} %cls_ref.1, s32[16,512]{1,0:T(8,128)} %cls_ref.1), custom_call_target="tpu_custom_call" | custom-call | tf_op jit(solution)/shard_map/side/pallas_call | solution.py:326
  0.9 2.1 %collective-permute-start = (bf16[80,128]{1,0:T(8,128)(2,1)S(1)}, bf16[80,128]{1,0:T(8,128)(2,1)S(1)}, u32[]{:S(2)}, u32[]{:S(2)}) collective-permute-start(bf16[80,128]{1,0:T(8,128)(2,1)S(1)} %side.1), channel_id=1, source_target_pairs={{0,1},{1,0},{2,3},{3,2},{4,5},{5,4},{6,7},{7,6},{8,9},{9,8},{10,11... | collective-permute-start | bytes 61448 | tf_op jit(solution)/shard_map/ppermute | solution.py:334
  3.0 1.3 %pack.1 = (bf16[32,32,128]{2,1,0:T(8,128)(2,1)S(1)}, f32[16,128]{1,0:T(8,128)S(1)}) custom-call(bf16[1,3,2,16,512]{4,3,2,1,0:T(8,128)(2,1)} %pert_ref.1, bf16[1,3,2,16,512]{4,3,2,1,0:T(8,128)(2,1)} %prob_ref.1, s32[16,512]{1,0:T(8,128)} %cls_ref.1), custom_call_target="tpu_custom_call" | custom-call | tf_op jit(solution)/shard_map/pack/pallas_call | solution.py:337
  4.3 0.0 collective-permute-done.side_ref
  4.4 25.7 %all_to_all.10.got_ref = bf16[32,32,128]{2,1,0:T(8,128)(2,1)S(1)} all-to-all(bf16[32,32,128]{2,1,0:T(8,128)(2,1)S(1)} %get-tuple-element.16), channel_id=1, replica_groups=mesh['member'=32,'row'=4,'col'=2] {'member'}, dimensions={0} | all-to-all | bytes 524288 | tf_op jit(solution)/shard_map/all_to_all | solution.py:354
  30.1 2.8 %collective-permute-start.1 = (bf16[33,8,128]{2,1,0:T(8,128)(2,1)S(1)}, bf16[33,8,128]{2,1,0:T(8,128)(2,1)S(1)}, u32[]{:S(2)}, u32[]{:S(2)}) collective-permute-start(bf16[33,8,128]{2,1,0:T(8,128)(2,1)S(1)} %get-tuple-element.18), channel_id=1, source_target_pairs={{0,6},{2,0},{4,2},{6,4},{1,7},{3,1},{5,3},{7,5},{8,14},{10,8},{12,... | collective-permute-start | bytes 202760 | tf_op jit(solution)/shard_map/ppermute | solution.py:364
  33.0 0.0 collective-permute-start.2
  33.0 1.7 %own.1 = (f32[21,16,128]{2,1,0:T(8,128)S(1)}, f32[32,32,128]{2,1,0:T(8,128)S(1)}) custom-call(bf16[32,32,128]{2,1,0:T(8,128)(2,1)S(1)} %all_to_all.10.got_ref), custom_call_target="tpu_custom_call" | custom-call | tf_op jit(solution)/shard_map/own/pallas_call | solution.py:368
  34.6 0.0 collective-permute-done.1.below_ref
  34.6 2.7 %collective-permute-done.2.above_ref = bf16[33,8,128]{2,1,0:T(8,128)(2,1)S(1)} collective-permute-done((bf16[33,8,128]{2,1,0:T(8,128)(2,1)S(1)}, bf16[33,8,128]{2,1,0:T(8,128)(2,1)S(1)}, u32[]{:S(2)}, u32[]{:S(2)}) %collective-permute-start.2) | collective-permute-done | bytes 67616 | tf_op jit(solution)/shard_map/ppermute | solution.py:365
  37.3 3.2 %apply.1 = (f32[32,3,4,128]{3,2,1,0:T(4,128)S(1)}, f32[32,32,128]{2,1,0:T(8,128)S(1)}) custom-call(f32[8]{0:T(128)} %rates_ref.1, bf16[32,32,128]{2,1,0:T(8,128)(2,1)S(1)} %all_to_all.10.got_ref, f32[16,128]{1,0:T(8,128)S(1)} %get-tuple-element.17.cls_ref, bf16[33,8,128]{2,1,0:T(8,128)(2,1)S(1)} %collective-permute-done.1.below_ref, ...), custom_call_target="tpu_custom_call", output_to_operand_aliasing={{1}: (6, {})} | custom-call | tf_op jit(solution)/shard_map/apply/pallas_call | solution.py:377
  40.5 17.2 %all_to_all.11.got_ref = f32[32,3,4,128]{3,2,1,0:T(4,128)S(1)} all-to-all(f32[32,3,4,128]{3,2,1,0:T(4,128)S(1)} %get-tuple-element.22), channel_id=1, replica_groups=mesh['member'=32,'row'=4,'col'=2] {'member'}, dimensions={0} | all-to-all | bytes 393216 | tf_op jit(solution)/shard_map/all_to_all | solution.py:391
  57.6 1.4 %unpack.1 = f32[1,3,2,16,512]{4,3,2,1,0:T(8,128)} custom-call(f32[32,3,4,128]{3,2,1,0:T(4,128)S(1)} %all_to_all.11.got_ref), custom_call_target="tpu_custom_call" | custom-call | tf_op jit(solution)/shard_map/unpack/pallas_call | solution.py:393
  (2 shorter events, 0.0 us)
Async XLA Ops:
  0.9 3.4 %collective-permute-start = (bf16[80,128]{1,0:T(8,128)(2,1)S(1)}, bf16[80,128]{1,0:T(8,128)(2,1)S(1)}, u32[]{:S(2)}, u32[]{:S(2)}) collective-permute-start(bf16[80,128]{1,0:T(8,128)(2,1)S(1)} %side.1), channel_id=1, source_target_pairs={{0,1},{1,0},{2,3},{3,2},{4,5},{5,4},{6,7},{7,6},{8,9},{9,8},{10,11... | collective-permute-start | bytes 61448 | tf_op jit(solution)/shard_map/ppermute | solution.py:334
  30.1 4.5 %collective-permute-start.1 = (bf16[33,8,128]{2,1,0:T(8,128)(2,1)S(1)}, bf16[33,8,128]{2,1,0:T(8,128)(2,1)S(1)}, u32[]{:S(2)}, u32[]{:S(2)}) collective-permute-start(bf16[33,8,128]{2,1,0:T(8,128)(2,1)S(1)} %get-tuple-element.18), channel_id=1, source_target_pairs={{0,6},{2,0},{4,2},{6,4},{1,7},{3,1},{5,3},{7,5},{8,14},{10,8},{12,... | collective-permute-start | bytes 202760 | tf_op jit(solution)/shard_map/ppermute | solution.py:364
  33.0 4.3 %collective-permute-start.2 = (bf16[33,8,128]{2,1,0:T(8,128)(2,1)S(1)}, bf16[33,8,128]{2,1,0:T(8,128)(2,1)S(1)}, u32[]{:S(2)}, u32[]{:S(2)}) collective-permute-start(bf16[33,8,128]{2,1,0:T(8,128)(2,1)S(1)} %get-tuple-element.19), channel_id=1, source_target_pairs={{0,2},{2,4},{4,6},{6,0},{1,3},{3,5},{5,7},{7,1},{8,10},{10,12},{12... | collective-permute-start | bytes 202760 | tf_op jit(solution)/shard_map/ppermute | solution.py:365

commit v6 on v5

--- a/solution.py
+++ b/solution.py
@@ -268,13 +268,19 @@
                 both[j].append(total[j])
         return tuple(both[0] + both[1])
 
+    turn = lax.axis_index("member") // LEV % (LANES // STRIP) * STRIP
+    slot = (lane - turn) & (LANES - 1)
+
+    def turned(x, dx):
+        return pltpu.roll(x, (turn + (-dx) % LANES) & (LANES - 1), 1)
+
     def store(pair, done):
         for p, a, b in ((pair[0], done[0], done[1]), (pair[1], done[2], done[3])):
-            first = jnp.where(lane < STRIP, lanes_by(a, HALO), lanes_by(a, HALO + 8))
-            first = jnp.where(lane < 2 * STRIP, first, lanes_by(a, HALO + 16))
-            first = jnp.where(lane < 3 * STRIP, first, lanes_by(b, HALO - 3 * STRIP))
-            rest = jnp.where(lane < STRIP, lanes_by(b, WIN + HALO), lanes_by(b, 2 * WIN + HALO - STRIP))
-            rest = jnp.where(lane < 2 * STRIP, rest, pltpu.roll(lanes_by(rest, 2 * STRIP), HALO, 0))
+            first = jnp.where(slot < STRIP, turned(a, HALO), turned(a, HALO + 8))
+            first = jnp.where(slot < 2 * STRIP, first, turned(a, HALO + 16))
+            first = jnp.where(slot < 3 * STRIP, first, turned(b, HALO - 3 * STRIP))
+            rest = jnp.where(slot < STRIP, turned(b, WIN + HALO), turned(b, 2 * WIN + HALO - STRIP))
+            rest = jnp.where(slot < 2 * STRIP, rest, pltpu.roll(lanes_by(rest, 2 * STRIP), HALO, 0))
             out_ref[p, 0] = first[:HALO]
             out_ref[p, 1] = first[HALO:]
             out_ref[p, 2] = rest[:HALO]
@@ -287,27 +293,38 @@
     lax.fori_loop(0, members // 2, step, 0, unroll=4)
 
 
-def unpack_kernel(got_ref, out_ref):
-    lane = lax.broadcasted_iota(jnp.int32, (ROWS, LANES), 1)
+def unpack_kernel(got_ref, out_ref, tile_ref, sems):
     per = LANES // STRIP
-
-    def moved(x, shift):
-        shift %= LANES
-        return pltpu.roll(x, shift, 1) if shift else x
-
+    blocks = COLS // LANES
+    slots = [lax.broadcasted_iota(jnp.int32, (rows, LANES), 1) // STRIP for rows in (HALO, 8)]
+
+    def joined(parts, first):
+        slot = slots[0] if parts[0].shape[0] == HALO else slots[1]
+        acc = parts[0]
+        for q in range(1, per):
+            acc = jnp.where(slot == (first + q) % per, parts[q], acc)
+        return pltpu.roll(acc, (-first * STRIP) % LANES, 1) if first % per else acc
+
+    copies = []
     for l in range(LEV):
-        for at in range(COLS // LANES):
-            acc = [None] * VARS
-            for q in range(per):
-                got = got_ref[(at * per + q) * LEV + l]
-                top = jnp.concatenate([got[0], got[1]], axis=0)
-                low = jnp.concatenate([got[2], moved(got[2], 2 * STRIP)], axis=0)
-                for v in range(VARS):
-                    under = moved(top, STRIP * (q - VARS)) if v == 0 else moved(low, STRIP * (q - v + 1))
-                    piece = jnp.concatenate([moved(top, STRIP * (q - v)), under], axis=0)
-                    acc[v] = piece if acc[v] is None else jnp.where(lane >= STRIP * q, piece, acc[v])
+        for at in range(blocks):
+            got = [got_ref[(at * per + q) * LEV + l] for q in range(per)]
+            top = [jnp.concatenate([g[0], g[1]], axis=0) for g in got]
+            low = [g[2] for g in got]
+            span = slice(at * LANES, (at + 1) * LANES)
             for v in range(VARS):
-                out_ref[0, v, l, :, at * LANES : (at + 1) * LANES] = acc[v]
+                tile_ref[v, l, :8, span] = joined(top, v)
+                if v == 0:
+                    tile_ref[v, l, 8:, span] = joined(top, VARS)
+                else:
+                    tile_ref[v, l, 8 : 8 + HALO, span] = joined(low, v - 1)
+                    tile_ref[v, l, 8 + HALO :, span] = joined(low, v + 1)
+        for v in range(VARS):
+            copy = pltpu.make_async_copy(tile_ref.at[v, l], out_ref.at[0, v, l], sems.at[v * LEV + l])
+            copy.start()
+            copies.append(copy)
+    for copy in copies:
+        copy.wait()
 
 
 def body(pert, probes, diff_class, class_rate):
@@ -393,8 +410,12 @@
     return pl.pallas_call(
         unpack_kernel,
         in_specs=[vmem],
-        out_specs=vmem,
+        out_specs=pl.BlockSpec(memory_space=pl.ANY),
         out_shape=jax.ShapeDtypeStruct((1, VARS, LEV, ROWS, COLS), F32),
+        scratch_shapes=[
+            pltpu.VMEM((VARS, LEV, ROWS, COLS), F32),
+            pltpu.SemaphoreType.DMA((VARS * LEV,)),
+        ],
         name="unpack",
     )(near(back))
 

time: 59.3 us -> 58.7 us (0.990)
  no operation moved by 1% of the time
where the time goes in v6:
time: 58.7 us; the launch traced here: 58.5 us
  blocking collectives  42.9 us (73%)
  Pallas kernels  7.91 us (13%)
  starting transfers between devices  4.93 us (8%)
  waiting for transfers between devices  2.67 us (5%)
    all_to_all x1, blocking collectives, body(): got = lax.all_to_all(chunks, 'member', 0, 0, tiled=True)  25.7 us
    all_to_all x1, blocking collectives, body(): back = lax.all_to_all(part, 'member', 0, 0, tiled=True)  17.2 us
    pallas_call x1, Pallas kernels, body(): pl.pallas_call(functools.partial(apply_kernel, n_row), in_specs=[smem] +...  3.17 us
    ppermute x1, starting transfers between devices, body(): lax.ppermute(up, 'row', [(i, (i - 1) % n_row) for i in range(n_row)])  2.81 us
    ppermute x1, waiting for transfers between devices, body(): lax.ppermute(dn, 'row', [(i, (i + 1) % n_row) for i in range(n_row)])  2.66 us
    ppermute x1, starting transfers between devices, body(): beside = lax.ppermute(side, 'col', [(0, 1), (1, 0)])  2.12 us
    pallas_call x1, Pallas kernels, body(): pl.pallas_call(own_kernel, in_specs=[vmem], out_specs=[vmem] * 2, out_sha...  1.66 us
    pallas_call x1, Pallas kernels, body(): pl.pallas_call(pack_kernel, in_specs=[vmem] * 3, out_specs=[vmem] * 2, ou...  1.3 us
  transfers between devices with their start and end apart: 3, of which 1 were waited for; matrix products, arithmetic and copies ran while one was open for 0% of the time, Pallas kernels for 5%

profile of v6, /device:TPU:1, one launch (start us, length us, event | category | flops | bytes accessed | tf_op | source)
XLA Modules:
  0.0 58.5 jit_solution(1065455104405289635)
XLA Ops:
  0.0 0.9 %side.1 = bf16[80,128]{1,0:T(8,128)(2,1)S(1)} custom-call(bf16[1,3,2,16,512]{4,3,2,1,0:T(8,128)(2,1)} %pert_ref.1, bf16[1,3,2,16,512]{4,3,2,1,0:T(8,128)(2,1)} %pert_ref.1, bf16[1,3,2,16,512]{4,3,2,1,0:T(8,128)(2,1)} %prob_ref.1, bf16[1,3,2,16,512]{4,3,2,1,0:T(8,128)(2,1)} %prob_ref.1, s32[16,512]{1,0:T(8,128)} %cls_ref.1, s32[16,512]{1,0:T(8,128)} %cls_ref.1), custom_call_target="tpu_custom_call" | custom-call | tf_op jit(solution)/shard_map/side/pallas_call | solution.py:343
  0.9 2.1 %collective-permute-start = (bf16[80,128]{1,0:T(8,128)(2,1)S(1)}, bf16[80,128]{1,0:T(8,128)(2,1)S(1)}, u32[]{:S(2)}, u32[]{:S(2)}) collective-permute-start(bf16[80,128]{1,0:T(8,128)(2,1)S(1)} %side.1), channel_id=1, source_target_pairs={{0,1},{1,0},{2,3},{3,2},{4,5},{5,4},{6,7},{7,6},{8,9},{9,8},{10,11... | collective-permute-start | bytes 61448 | tf_op jit(solution)/shard_map/ppermute | solution.py:351
  3.0 1.3 %pack.1 = (bf16[32,32,128]{2,1,0:T(8,128)(2,1)S(1)}, f32[16,128]{1,0:T(8,128)S(1)}) custom-call(bf16[1,3,2,16,512]{4,3,2,1,0:T(8,128)(2,1)} %pert_ref.1, bf16[1,3,2,16,512]{4,3,2,1,0:T(8,128)(2,1)} %prob_ref.1, s32[16,512]{1,0:T(8,128)} %cls_ref.1), custom_call_target="tpu_custom_call" | custom-call | tf_op jit(solution)/shard_map/pack/pallas_call | solution.py:354
  4.3 0.0 collective-permute-done.side_ref
  4.4 25.7 %all_to_all.10.got_ref = bf16[32,32,128]{2,1,0:T(8,128)(2,1)S(1)} all-to-all(bf16[32,32,128]{2,1,0:T(8,128)(2,1)S(1)} %get-tuple-element.16), channel_id=1, replica_groups=mesh['member'=32,'row'=4,'col'=2] {'member'}, dimensions={0} | all-to-all | bytes 524288 | tf_op jit(solution)/shard_map/all_to_all | solution.py:371
  30.1 2.8 %collective-permute-start.1 = (bf16[33,8,128]{2,1,0:T(8,128)(2,1)S(1)}, bf16[33,8,128]{2,1,0:T(8,128)(2,1)S(1)}, u32[]{:S(2)}, u32[]{:S(2)}) collective-permute-start(bf16[33,8,128]{2,1,0:T(8,128)(2,1)S(1)} %get-tuple-element.18), channel_id=1, source_target_pairs={{0,6},{2,0},{4,2},{6,4},{1,7},{3,1},{5,3},{7,5},{8,14},{10,8},{12,... | collective-permute-start | bytes 202760 | tf_op jit(solution)/shard_map/ppermute | solution.py:381
  33.0 0.0 collective-permute-start.2
  33.0 1.7 %own.1 = (f32[21,16,128]{2,1,0:T(8,128)S(1)}, f32[32,32,128]{2,1,0:T(8,128)S(1)}) custom-call(bf16[32,32,128]{2,1,0:T(8,128)(2,1)S(1)} %all_to_all.10.got_ref), custom_call_target="tpu_custom_call" | custom-call | tf_op jit(solution)/shard_map/own/pallas_call | solution.py:385
  34.6 0.0 collective-permute-done.1.below_ref
  34.6 2.7 %collective-permute-done.2.above_ref = bf16[33,8,128]{2,1,0:T(8,128)(2,1)S(1)} collective-permute-done((bf16[33,8,128]{2,1,0:T(8,128)(2,1)S(1)}, bf16[33,8,128]{2,1,0:T(8,128)(2,1)S(1)}, u32[]{:S(2)}, u32[]{:S(2)}) %collective-permute-start.2) | collective-permute-done | bytes 67616 | tf_op jit(solution)/shard_map/ppermute | solution.py:382
  37.3 3.2 %apply.1 = (f32[32,3,4,128]{3,2,1,0:T(4,128)S(1)}, f32[32,32,128]{2,1,0:T(8,128)S(1)}) custom-call(f32[8]{0:T(128)} %rates_ref.1, bf16[32,32,128]{2,1,0:T(8,128)(2,1)S(1)} %all_to_all.10.got_ref, f32[16,128]{1,0:T(8,128)S(1)} %get-tuple-element.17.cls_ref, bf16[33,8,128]{2,1,0:T(8,128)(2,1)S(1)} %collective-permute-done.1.below_ref, ...), custom_call_target="tpu_custom_call", output_to_operand_aliasing={{1}: (6, {})} | custom-call | tf_op jit(solution)/shard_map/apply/pallas_call | solution.py:394
  40.5 17.2 %all_to_all.11.got_ref = f32[32,3,4,128]{3,2,1,0:T(4,128)S(1)} all-to-all(f32[32,3,4,128]{3,2,1,0:T(4,128)S(1)} %get-tuple-element.22), channel_id=1, replica_groups=mesh['member'=32,'row'=4,'col'=2] {'member'}, dimensions={0} | all-to-all | bytes 393216 | tf_op jit(solution)/shard_map/all_to_all | solution.py:408
  57.6 0.8 %unpack.1 = f32[1,3,2,16,512]{4,3,2,1,0:T(8,128)} custom-call(f32[32,3,4,128]{3,2,1,0:T(4,128)S(1)} %all_to_all.11.got_ref), custom_call_target="tpu_custom_call" | custom-call | tf_op jit(solution)/shard_map/unpack/pallas_call | solution.py:410
  (2 shorter events, 0.0 us)
Async XLA Ops:
  0.9 3.4 %collective-permute-start = (bf16[80,128]{1,0:T(8,128)(2,1)S(1)}, bf16[80,128]{1,0:T(8,128)(2,1)S(1)}, u32[]{:S(2)}, u32[]{:S(2)}) collective-permute-start(bf16[80,128]{1,0:T(8,128)(2,1)S(1)} %side.1), channel_id=1, source_target_pairs={{0,1},{1,0},{2,3},{3,2},{4,5},{5,4},{6,7},{7,6},{8,9},{9,8},{10,11... | collective-permute-start | bytes 61448 | tf_op jit(solution)/shard_map/ppermute | solution.py:351
  30.1 4.5 %collective-permute-start.1 = (bf16[33,8,128]{2,1,0:T(8,128)(2,1)S(1)}, bf16[33,8,128]{2,1,0:T(8,128)(2,1)S(1)}, u32[]{:S(2)}, u32[]{:S(2)}) collective-permute-start(bf16[33,8,128]{2,1,0:T(8,128)(2,1)S(1)} %get-tuple-element.18), channel_id=1, source_target_pairs={{0,6},{2,0},{4,2},{6,4},{1,7},{3,1},{5,3},{7,5},{8,14},{10,8},{12,... | collective-permute-start | bytes 202760 | tf_op jit(solution)/shard_map/ppermute | solution.py:381
  33.0 4.3 %collective-permute-start.2 = (bf16[33,8,128]{2,1,0:T(8,128)(2,1)S(1)}, bf16[33,8,128]{2,1,0:T(8,128)(2,1)S(1)}, u32[]{:S(2)}, u32[]{:S(2)}) collective-permute-start(bf16[33,8,128]{2,1,0:T(8,128)(2,1)S(1)} %get-tuple-element.19), channel_id=1, source_target_pairs={{0,2},{2,4},{4,6},{6,0},{1,3},{3,5},{5,7},{7,1},{8,10},{10,12},{12... | collective-permute-start | bytes 202760 | tf_op jit(solution)/shard_map/ppermute | solution.py:382

commit v7 on v6

--- a/solution.py
+++ b/solution.py
@@ -57,9 +57,11 @@
     side_ref[LEV * 2 * ROWS :] = placed([cls] * VARS).astype(BF16)
 
 
-def pack_kernel(pert_ref, prob_ref, cls_ref, out_ref, cls_out_ref, wide_ref):
+def pack_kernel(rates_ref, pert_ref, prob_ref, cls_ref, out_ref, cls_out_ref, rates_out_ref, wide_ref):
     lane = lax.broadcasted_iota(jnp.int32, (ROWS, LANES), 1)
     blocks = COLS // LANES
+    for k in range(rates_ref.shape[0]):
+        rates_out_ref[k : k + 1] = jnp.full((1, LANES), rates_ref[k], F32)
 
     def block(ref, v, l, at, shift):
         got = ref[0, v, l, :, at * LANES : (at + 1) * LANES].astype(F32)
@@ -135,7 +137,58 @@
     return pltpu.roll(x, (-dx) % LANES, 1) if dx else x
 
 
-def own_kernel(got_ref, gram_ref, prob_ref, pert_ref):
+def rates_of(cls, rates_ref):
+    rate = jnp.zeros(cls.shape, F32)
+    for k in range(rates_ref.shape[0]):
+        rate = jnp.where(cls == float(k + 1), rates_ref[k : k + 1], rate)
+    return rate
+
+
+def entries(rows_at):
+    steps = ((0, 1), (0, -1), (1, 0), (-1, 0))
+    near = {dy: rows_at(dy) for dy in range(-HALO + 1, HALO)}
+    at = {(dy, dx): lanes_by(near[dy], dx) for dy, dx in EVERY if abs(dy) + abs(dx) < HALO}
+    coef = {(0, 0): 1.0 - 4.0 * at[(0, 0)]}
+    for e in steps:
+        coef[e] = at[(0, 0)]
+    for sweep in range(1, SWEEPS):
+        flow = {d: c * at[d] for d, c in coef.items()}
+        to = {(d[0] + e[0], d[1] + e[1]) for d in flow for e in steps}
+        new = {}
+        for d in EVERY:
+            if d not in to:
+                continue
+            terms = [flow[(d[0] - e[0], d[1] - e[1])] for e in steps if (d[0] - e[0], d[1] - e[1]) in flow]
+            if d in coef:
+                terms.append(coef[d] - 4.0 * flow[d])
+            total = terms[0]
+            for t in terms[1:]:
+                total = total + t
+            new[d] = total
+        coef = new
+    return coef
+
+
+def set_weights(weight_ref, coef, gram_at, scale):
+    for i, (dy, dx) in enumerate(FORWARD):
+        weight_ref[AT[(dy, dx)]] = lanes_by(coef[(dy, dx)] * scale * gram_at(i, dy), -dx)
+        if (dy, dx) != (0, 0):
+            weight_ref[AT[(-dy, -dx)]] = lanes_by(coef[(-dy, -dx)] * scale, dx) * gram_at(i, 0)
+
+
+def weighted(weight_ref, rows):
+    total = None
+    for dx in range(-HALO, HALO + 1):
+        part = None
+        for dy in range(-HALO + abs(dx), HALO - abs(dx) + 1):
+            term = weight_ref[AT[(dy, dx)]] * rows[dy + HALO]
+            part = term if part is None else part + term
+        part = lanes_by(part, dx)
+        total = part if total is None else total + part
+    return total
+
+
+def own_kernel(rates_ref, got_ref, cls_ref, gram_ref, prob_ref, mid_ref, pert_ref, weight_ref, rate_ref):
     members = got_ref.shape[0]
     blank = jnp.zeros((TOP, LANES), F32)
 
@@ -162,9 +215,20 @@
         for i, a in enumerate(acc):
             gram_ref[i, 8 * b : 8 * b + 8] = a
 
+    rate_ref[...] = rates_of(cls_ref[...], rates_ref)
+    coef = entries(lambda dy: rate_ref[HALO + dy : HALO + dy + 8])
+    set_weights(weight_ref, coef, lambda i, dy: gram_ref[i, HALO + dy : HALO + dy + 8], 1.0 / (members - 1))
+
+    def one_probe(p, _):
+        start = TOP + HALO
+        mid_ref[p] = weighted(weight_ref, [prob_ref[p, start + dy : start + dy + 8] for dy in range(-HALO, HALO + 1)])
+        return 0
+
+    lax.fori_loop(0, members, one_probe, 0, unroll=8)
+
 
 def apply_kernel(
-    n_row, rates_ref, got_ref, cls_ref, below_ref, above_ref, own_ref, part_ref, out_ref,
+    n_row, rates_ref, got_ref, cls_ref, below_ref, above_ref, own_ref, mid_ref, part_ref, out_ref,
     prob_ref, gram_ref, weight_ref, rate_ref,
 ):
     members = got_ref.shape[0]
@@ -209,64 +273,16 @@
         ],
         axis=0,
     )
-    rate = jnp.zeros((TALL, LANES), F32)
-    for k in range(rates_ref.shape[0]):
-        rate = jnp.where(cls == float(k + 1), rates_ref[k], rate)
-    rate_ref[...] = rate
-
-    steps = ((0, 1), (0, -1), (1, 0), (-1, 0))
-    scale = 1.0 / (members - 1)
-    for b in range(2):
-        at = {
-            (dy, dx): lanes_by(rate_ref[TOP + 8 * b + dy : TOP + 8 * b + dy + 8], dx)
-            for dy, dx in EVERY
-            if abs(dy) + abs(dx) < HALO
-        }
-        coef = {(0, 0): 1.0 - 4.0 * at[(0, 0)]}
-        for e in steps:
-            coef[e] = at[(0, 0)]
-        for sweep in range(1, SWEEPS):
-            flow = {d: c * at[d] for d, c in coef.items()}
-            to = {(d[0] + e[0], d[1] + e[1]) for d in flow for e in steps}
-            new = {}
-            for d in EVERY:
-                if d not in to:
-                    continue
-                terms = [flow[(d[0] - e[0], d[1] - e[1])] for e in steps if (d[0] - e[0], d[1] - e[1]) in flow]
-                if d in coef:
-                    terms.append(coef[d] - 4.0 * flow[d])
-                total = terms[0]
-                for t in terms[1:]:
-                    total = total + t
-                new[d] = total
-            coef = new
-        rows = slice(8 * b, 8 * b + 8)
-        for i, (dy, dx) in enumerate(FORWARD):
-            gram = gram_ref[i, 8 * b + dy : 8 * b + dy + 8]
-            weight_ref[AT[(dy, dx)], rows] = lanes_by(coef[(dy, dx)] * scale * gram, -dx)
-            if (dy, dx) != (0, 0):
-                weight_ref[AT[(-dy, -dx)], rows] = lanes_by(coef[(-dy, -dx)] * scale, dx) * gram_ref[i, rows]
-
-    def sums(pair):
-        both = [[], []]
-        for b in range(2):
-            rows = [
-                [prob_ref[p, TOP + 8 * b + dy : TOP + 8 * b + dy + 8] for dy in range(-HALO, HALO + 1)] for p in pair
-            ]
-            total = [None, None]
-            for dx in range(-HALO, HALO + 1):
-                part = [None, None]
-                for dy in range(-HALO + abs(dx), HALO - abs(dx) + 1):
-                    weight = weight_ref[AT[(dy, dx)], 8 * b : 8 * b + 8]
-                    for j in range(2):
-                        term = weight * rows[j][dy + HALO]
-                        part[j] = term if part[j] is None else part[j] + term
-                for j in range(2):
-                    moved = lanes_by(part[j], dx)
-                    total[j] = moved if total[j] is None else total[j] + moved
-            for j in range(2):
-                both[j].append(total[j])
-        return tuple(both[0] + both[1])
+    rate_ref[...] = rates_of(cls, rates_ref)
+    coef = entries(
+        lambda dy: jnp.where(upper, rate_ref[TOP + dy : TOP + dy + 8], rate_ref[TOP + 8 + dy : TOP + dy + 16])
+    )
+    set_weights(
+        weight_ref,
+        coef,
+        lambda i, dy: jnp.where(upper, gram_ref[i, dy : dy + 8], gram_ref[i, 8 + dy : dy + 16]),
+        1.0 / (members - 1),
+    )
 
     turn = lax.axis_index("member") // LEV % (LANES // STRIP) * STRIP
     slot = (lane - turn) & (LANES - 1)
@@ -274,23 +290,23 @@
     def turned(x, dx):
         return pltpu.roll(x, (turn + (-dx) % LANES) & (LANES - 1), 1)
 
-    def store(pair, done):
-        for p, a, b in ((pair[0], done[0], done[1]), (pair[1], done[2], done[3])):
-            first = jnp.where(slot < STRIP, turned(a, HALO), turned(a, HALO + 8))
-            first = jnp.where(slot < 2 * STRIP, first, turned(a, HALO + 16))
-            first = jnp.where(slot < 3 * STRIP, first, turned(b, HALO - 3 * STRIP))
-            rest = jnp.where(slot < STRIP, turned(b, WIN + HALO), turned(b, 2 * WIN + HALO - STRIP))
-            rest = jnp.where(slot < 2 * STRIP, rest, pltpu.roll(lanes_by(rest, 2 * STRIP), HALO, 0))
-            out_ref[p, 0] = first[:HALO]
-            out_ref[p, 1] = first[HALO:]
-            out_ref[p, 2] = rest[:HALO]
-
-    def step(i, _):
-        pair = (2 * i, 2 * i + 1)
-        store(pair, sums(pair))
+    def one_probe(p, _):
+        rows = [
+            jnp.where(upper, prob_ref[p, TOP + dy : TOP + dy + 8], prob_ref[p, TOP + 8 + dy : TOP + dy + 16])
+            for dy in range(-HALO, HALO + 1)
+        ]
+        a, b = weighted(weight_ref, rows), mid_ref[p]
+        first = jnp.where(slot < STRIP, turned(a, HALO), turned(a, HALO + 8))
+        first = jnp.where(slot < 2 * STRIP, first, turned(a, HALO + 16))
+        first = jnp.where(slot < 3 * STRIP, first, turned(b, HALO - 3 * STRIP))
+        rest = jnp.where(slot < STRIP, turned(b, WIN + HALO), turned(b, 2 * WIN + HALO - STRIP))
+        rest = jnp.where(slot < 2 * STRIP, rest, pltpu.roll(lanes_by(rest, 2 * STRIP), HALO, 0))
+        out_ref[p, 0] = first[:HALO]
+        out_ref[p, 1] = first[HALO:]
+        out_ref[p, 2] = rest[:HALO]
         return 0
 
-    lax.fori_loop(0, members // 2, step, 0, unroll=4)
+    lax.fori_loop(0, members, one_probe, 0, unroll=8)
 
 
 def unpack_kernel(got_ref, out_ref, tile_ref, sems):
@@ -313,12 +329,14 @@
             low = [g[2] for g in got]
             span = slice(at * LANES, (at + 1) * LANES)
             for v in range(VARS):
-                tile_ref[v, l, :8, span] = joined(top, v)
+                ends = joined(top, v)
+                tile_ref[v, l, :HALO, span] = ends[:HALO]
+                tile_ref[v, l, ROWS - HALO :, span] = ends[HALO:]
                 if v == 0:
-                    tile_ref[v, l, 8:, span] = joined(top, VARS)
+                    tile_ref[v, l, HALO : HALO + 8, span] = joined(top, VARS)
                 else:
-                    tile_ref[v, l, 8 : 8 + HALO, span] = joined(low, v - 1)
-                    tile_ref[v, l, 8 + HALO :, span] = joined(low, v + 1)
+                    tile_ref[v, l, HALO : 2 * HALO, span] = joined(low, v - 1)
+                    tile_ref[v, l, 2 * HALO : 3 * HALO, span] = joined(low, v + 1)
         for v in range(VARS):
             copy = pltpu.make_async_copy(tile_ref.at[v, l], out_ref.at[0, v, l], sems.at[v * LEV + l])
             copy.start()
@@ -351,14 +369,14 @@
     beside = lax.ppermute(side, "col", [(0, 1), (1, 0)])
 
     chunk, classes = shape((members, 2 * ROWS, LANES), BF16), shape((ROWS, LANES), F32)
-    inner, cls = pl.pallas_call(
+    inner, cls, rates = pl.pallas_call(
         pack_kernel,
-        in_specs=[vmem] * 3,
-        out_specs=[vmem] * 2,
-        out_shape=[chunk, classes],
+        in_specs=[smem] + [vmem] * 3,
+        out_specs=[vmem] * 3,
+        out_shape=[chunk, classes, shape((class_rate.shape[0], LANES), F32)],
         scratch_shapes=[pltpu.VMEM((ROWS, COLS + 2 * LANES), BF16)],
         name="pack",
-    )(pert, probes, diff_class)
+    )(class_rate, pert, probes, diff_class)
     chunks, cls = pl.pallas_call(
         patch_kernel,
         in_specs=[vmem] * 3,
@@ -382,28 +400,33 @@
     above = lax.ppermute(dn, "row", [(i, (i + 1) % n_row) for i in range(n_row)])
 
     tall = shape((members, TALL, LANES), F32)
-    own, spread = pl.pallas_call(
+    weights = pltpu.VMEM((len(EVERY), 8, LANES), F32)
+    own, spread, mid = pl.pallas_call(
         own_kernel,
-        in_specs=[vmem],
-        out_specs=[vmem] * 2,
-        out_shape=[shape((len(FORWARD), ROWS, LANES), F32), tall],
-        scratch_shapes=[pltpu.VMEM((members, TOP + ROWS, LANES), F32)],
+        in_specs=[vmem] * 3,
+        out_specs=[vmem] * 3,
+        out_shape=[shape((len(FORWARD), ROWS, LANES), F32), tall, shape((members, 8, LANES), F32)],
+        scratch_shapes=[
+            pltpu.VMEM((members, TOP + ROWS, LANES), F32),
+            weights,
+            pltpu.VMEM((ROWS, LANES), F32),
+        ],
         name="own",
-    )(near(got))
+    )(near(rates), near(got), near(cls))
 
     part, spread = pl.pallas_call(
         functools.partial(apply_kernel, n_row),
-        in_specs=[smem] + [vmem] * 6,
+        in_specs=[vmem] * 8,
         out_specs=[vmem] * 2,
         out_shape=[shape((members, VARS, HALO, LANES), F32), tall],
-        input_output_aliases={6: 1},
+        input_output_aliases={7: 1},
         scratch_shapes=[
             pltpu.VMEM((len(FORWARD), 24, LANES), F32),
-            pltpu.VMEM((len(EVERY), ROWS, LANES), F32),
+            weights,
             pltpu.VMEM((TALL, LANES), F32),
         ],
         name="apply",
-    )(class_rate, near(got), near(cls), near(below), near(above), near(own), near(spread))
+    )(near(rates), near(got), near(cls), near(below), near(above), near(own), near(mid), near(spread))
 
     back = lax.all_to_all(part, "member", 0, 0, tiled=True)
 

time: 58.7 us -> 57.7 us (0.983)
  waiting for transfers between devices: 2.67 us -> 1.87 us
    ppermute x1, waiting for transfers between devices: 2.66 us -> 1.86 us  [body(): lax.ppermute(dn, 'row', [(i, (i + 1) % n_row) for i in range(n_row)])]
  transfers between devices with their start and end apart: 3 -> 3, of which waited for: 1 -> 1; matrix products, arithmetic and copies ran while one was open for 0% -> 0% of each run, Pallas kernels for 5% -> 7%
where the time goes in v7:
time: 57.7 us; the launch traced here: 57.5 us
  blocking collectives  42.9 us (74%)
  Pallas kernels  7.74 us (13%)
  starting transfers between devices  4.93 us (9%)
  waiting for transfers between devices  1.87 us (3%)
    all_to_all x1, blocking collectives, body(): got = lax.all_to_all(chunks, 'member', 0, 0, tiled=True)  25.7 us
    all_to_all x1, blocking collectives, body(): back = lax.all_to_all(part, 'member', 0, 0, tiled=True)  17.2 us
    ppermute x1, starting transfers between devices, body(): lax.ppermute(up, 'row', [(i, (i - 1) % n_row) for i in range(n_row)])  2.81 us
    pallas_call x1, Pallas kernels, body(): pl.pallas_call(own_kernel, in_specs=[vmem] * 3, out_specs=[vmem] * 3, out...  2.46 us
    pallas_call x1, Pallas kernels, body(): pl.pallas_call(functools.partial(apply_kernel, n_row), in_specs=[vmem] *...  2.19 us
    ppermute x1, starting transfers between devices, body(): beside = lax.ppermute(side, 'col', [(0, 1), (1, 0)])  2.12 us
    ppermute x1, waiting for transfers between devices, body(): lax.ppermute(dn, 'row', [(i, (i + 1) % n_row) for i in range(n_row)])  1.86 us
    pallas_call x1, Pallas kernels, body(): pl.pallas_call(pack_kernel, in_specs=[smem] + [vmem] * 3, out_specs=[vmem...  1.31 us
  transfers between devices with their start and end apart: 3, of which 1 were waited for; matrix products, arithmetic and copies ran while one was open for 0% of the time, Pallas kernels for 7%

profile of v7, /device:TPU:1, one launch (start us, length us, event | category | flops | bytes accessed | tf_op | source)
XLA Modules:
  0.0 57.5 jit_solution(3254811177825805195)
XLA Ops:
  0.0 0.9 %side.1 = bf16[80,128]{1,0:T(8,128)(2,1)S(1)} custom-call(bf16[1,3,2,16,512]{4,3,2,1,0:T(8,128)(2,1)} %pert1_ref.1, bf16[1,3,2,16,512]{4,3,2,1,0:T(8,128)(2,1)} %pert1_ref.1, bf16[1,3,2,16,512]{4,3,2,1,0:T(8,128)(2,1)} %prob1_ref.1, bf16[1,3,2,16,512]{4,3,2,1,0:T(8,128)(2,1)} %prob1_ref.1, s32[16,512]{1,0:T(8,128)} %cls1_ref.1, s32[16,512]{1,0:T(8,128)} %cls1_ref.1), custom_call_target="tpu_custom_call" | custom-call | tf_op jit(solution)/shard_map/side/pallas_call | solution.py:361
  0.9 2.1 %collective-permute-start = (bf16[80,128]{1,0:T(8,128)(2,1)S(1)}, bf16[80,128]{1,0:T(8,128)(2,1)S(1)}, u32[]{:S(2)}, u32[]{:S(2)}) collective-permute-start(bf16[80,128]{1,0:T(8,128)(2,1)S(1)} %side.1), channel_id=1, source_target_pairs={{0,1},{1,0},{2,3},{3,2},{4,5},{5,4},{6,7},{7,6},{8,9},{9,8},{10,11... | collective-permute-start | bytes 61448 | tf_op jit(solution)/shard_map/ppermute | solution.py:369
  3.0 1.3 %pack.1 = (bf16[32,32,128]{2,1,0:T(8,128)(2,1)S(1)}, f32[16,128]{1,0:T(8,128)S(1)}, f32[8,128]{1,0:T(8,128)S(1)}) custom-call(f32[8]{0:T(128)} %rates_ref.1, bf16[1,3,2,16,512]{4,3,2,1,0:T(8,128)(2,1)} %pert1_ref.1, bf16[1,3,2,16,512]{4,3,2,1,0:T(8,128)(2,1)} %prob1_ref.1, s32[16,512]{1,0:T(8,128)} %cls1_ref.1), custom_call_target="tpu_custom_call" | custom-call | tf_op jit(solution)/shard_map/pack/pallas_call | solution.py:372
  4.4 0.0 collective-permute-done.side_ref
  4.4 25.7 %all_to_all.10.got_ref = bf16[32,32,128]{2,1,0:T(8,128)(2,1)S(1)} all-to-all(bf16[32,32,128]{2,1,0:T(8,128)(2,1)S(1)} %get-tuple-element.19), channel_id=1, replica_groups=mesh['member'=32,'row'=4,'col'=2] {'member'}, dimensions={0} | all-to-all | bytes 524288 | tf_op jit(solution)/shard_map/all_to_all | solution.py:389
  30.1 2.8 %collective-permute-start.1 = (bf16[33,8,128]{2,1,0:T(8,128)(2,1)S(1)}, bf16[33,8,128]{2,1,0:T(8,128)(2,1)S(1)}, u32[]{:S(2)}, u32[]{:S(2)}) collective-permute-start(bf16[33,8,128]{2,1,0:T(8,128)(2,1)S(1)} %get-tuple-element.21), channel_id=1, source_target_pairs={{0,6},{2,0},{4,2},{6,4},{1,7},{3,1},{5,3},{7,5},{8,14},{10,8},{12,... | collective-permute-start | bytes 202760 | tf_op jit(solution)/shard_map/ppermute | solution.py:399
  33.0 0.0 collective-permute-start.2
  33.0 2.5 %own.1 = (f32[21,16,128]{2,1,0:T(8,128)S(1)}, f32[32,32,128]{2,1,0:T(8,128)S(1)}, f32[32,8,128]{2,1,0:T(8,128)S(1)}) custom-call(f32[8,128]{1,0:T(8,128)S(1)} %get-tuple-element.16.rates_ref, bf16[32,32,128]{2,1,0:T(8,128)(2,1)S(1)} %all_to_all.10.got_ref, f32[16,128]{1,0:T(8,128)S(1)} %get-tuple-element.20.cls_ref), custom_call_target="tpu_custom_call" | custom-call | tf_op jit(solution)/shard_map/own/pallas_call | solution.py:404
  35.4 0.0 collective-permute-done.1.below_ref
  35.4 1.9 %collective-permute-done.2.above_ref = bf16[33,8,128]{2,1,0:T(8,128)(2,1)S(1)} collective-permute-done((bf16[33,8,128]{2,1,0:T(8,128)(2,1)S(1)}, bf16[33,8,128]{2,1,0:T(8,128)(2,1)S(1)}, u32[]{:S(2)}, u32[]{:S(2)}) %collective-permute-start.2) | collective-permute-done | bytes 67616 | tf_op jit(solution)/shard_map/ppermute | solution.py:400
  37.3 2.2 %apply.1 = (f32[32,3,4,128]{3,2,1,0:T(4,128)S(1)}, f32[32,32,128]{2,1,0:T(8,128)S(1)}) custom-call(f32[8,128]{1,0:T(8,128)S(1)} %get-tuple-element.16.rates_ref, bf16[32,32,128]{2,1,0:T(8,128)(2,1)S(1)} %all_to_all.10.got_ref, f32[16,128]{1,0:T(8,128)S(1)} %get-tuple-element.20.cls_ref, ...), custom_call_target="tpu_custom_call", output_to_operand_aliasing={{1}: (7, {})} | custom-call | tf_op jit(solution)/shard_map/apply/pallas_call | solution.py:417
  39.5 17.2 %all_to_all.11.got_ref = f32[32,3,4,128]{3,2,1,0:T(4,128)S(1)} all-to-all(f32[32,3,4,128]{3,2,1,0:T(4,128)S(1)} %get-tuple-element.26), channel_id=1, replica_groups=mesh['member'=32,'row'=4,'col'=2] {'member'}, dimensions={0} | all-to-all | bytes 393216 | tf_op jit(solution)/shard_map/all_to_all | solution.py:431
  56.7 0.8 %unpack.1 = f32[1,3,2,16,512]{4,3,2,1,0:T(8,128)} custom-call(f32[32,3,4,128]{3,2,1,0:T(4,128)S(1)} %all_to_all.11.got_ref), custom_call_target="tpu_custom_call" | custom-call | tf_op jit(solution)/shard_map/unpack/pallas_call | solution.py:433
  (2 shorter events, 0.0 us)
Async XLA Ops:
  0.9 3.4 %collective-permute-start = (bf16[80,128]{1,0:T(8,128)(2,1)S(1)}, bf16[80,128]{1,0:T(8,128)(2,1)S(1)}, u32[]{:S(2)}, u32[]{:S(2)}) collective-permute-start(bf16[80,128]{1,0:T(8,128)(2,1)S(1)} %side.1), channel_id=1, source_target_pairs={{0,1},{1,0},{2,3},{3,2},{4,5},{5,4},{6,7},{7,6},{8,9},{9,8},{10,11... | collective-permute-start | bytes 61448 | tf_op jit(solution)/shard_map/ppermute | solution.py:369
  30.1 5.3 %collective-permute-start.1 = (bf16[33,8,128]{2,1,0:T(8,128)(2,1)S(1)}, bf16[33,8,128]{2,1,0:T(8,128)(2,1)S(1)}, u32[]{:S(2)}, u32[]{:S(2)}) collective-permute-start(bf16[33,8,128]{2,1,0:T(8,128)(2,1)S(1)} %get-tuple-element.21), channel_id=1, source_target_pairs={{0,6},{2,0},{4,2},{6,4},{1,7},{3,1},{5,3},{7,5},{8,14},{10,8},{12,... | collective-permute-start | bytes 202760 | tf_op jit(solution)/shard_map/ppermute | solution.py:399
  33.0 4.3 %collective-permute-start.2 = (bf16[33,8,128]{2,1,0:T(8,128)(2,1)S(1)}, bf16[33,8,128]{2,1,0:T(8,128)(2,1)S(1)}, u32[]{:S(2)}, u32[]{:S(2)}) collective-permute-start(bf16[33,8,128]{2,1,0:T(8,128)(2,1)S(1)} %get-tuple-element.22), channel_id=1, source_target_pairs={{0,2},{2,4},{4,6},{6,0},{1,3},{3,5},{5,7},{7,1},{8,10},{10,12},{12... | collective-permute-start | bytes 202760 | tf_op jit(solution)/shard_map/ppermute | solution.py:400

commit v8 on v7

--- a/solution.py
+++ b/solution.py
@@ -31,30 +31,33 @@
     return jnp.concatenate(groups, axis=0).astype(BF16)
 
 
-def side_kernel(pert0_ref, pert1_ref, prob0_ref, prob1_ref, cls0_ref, cls1_ref, side_ref):
+def side_kernel(pert_ref, prob_ref, cls_ref, side_ref, pert_end, prob_end, cls_end, sems):
     last = lax.axis_index("col") == 0
+    at = pl.ds(pl.multiple_of(jnp.where(last, COLS - LANES, 0), LANES), LANES)
+    copies = [
+        pltpu.make_async_copy(pert_ref.at[0, :, :, :, at], pert_end, sems.at[0]),
+        pltpu.make_async_copy(prob_ref.at[0, :, :, :, at], prob_end, sems.at[1]),
+        pltpu.make_async_copy(cls_ref.at[:, at], cls_end, sems.at[2]),
+    ]
+    for copy in copies:
+        copy.start()
     lane = lax.broadcasted_iota(jnp.int32, (ROWS, LANES), 1)
-    use = [
-        (lane >= WIN * v + jnp.where(last, 0, WIN - HALO)) & (lane < WIN * v + jnp.where(last, HALO, WIN))
-        for v in range(VARS)
-    ]
-
-    def placed(blocks):
+    low = jnp.where(last, 0, WIN - HALO)
+    use = [(lane >= WIN * v + low) & (lane < WIN * v + low + HALO) for v in range(VARS)]
+    for copy in copies:
+        copy.wait()
+
+    def placed(planes):
         acc = jnp.zeros((ROWS, LANES), F32)
-        for v, (head, tail) in enumerate(blocks):
-            tail = pltpu.roll(tail, (WIN * v + HALO) % LANES, 1)
-            head = pltpu.roll(head, (WIN * v + WIN - HALO) % LANES, 1)
-            acc = jnp.where(use[v], jnp.where(last, tail, head), acc)
+        for v, plane in enumerate(planes):
+            shift = jnp.where(last, WIN * v + HALO, WIN * v + WIN - HALO)
+            acc = jnp.where(use[v], pltpu.roll(plane, shift, 1), acc)
         return acc
 
     for l in range(LEV):
-        a, b = (
-            placed([(head[0, v, l].astype(F32), tail[0, v, l].astype(F32)) for v in range(VARS)])
-            for head, tail in ((pert0_ref, pert1_ref), (prob0_ref, prob1_ref))
-        )
+        a, b = (placed([end[v, l].astype(F32) for v in range(VARS)]) for end in (pert_end, prob_end))
         side_ref[l * 2 * ROWS : (l + 1) * 2 * ROWS] = grouped(a, b)
-    cls = ((cls0_ref[...] + 1).astype(F32), (cls1_ref[...] + 1).astype(F32))
-    side_ref[LEV * 2 * ROWS :] = placed([cls] * VARS).astype(BF16)
+    side_ref[LEV * 2 * ROWS :] = placed([(cls_end[...] + 1).astype(F32)] * VARS).astype(BF16)
 
 
 def pack_kernel(rates_ref, pert_ref, prob_ref, cls_ref, out_ref, cls_out_ref, rates_out_ref, wide_ref):
@@ -188,7 +191,17 @@
     return total
 
 
-def own_kernel(rates_ref, got_ref, cls_ref, gram_ref, prob_ref, mid_ref, pert_ref, weight_ref, rate_ref):
+def turning(rows):
+    turn = lax.axis_index("member") // LEV % (LANES // STRIP) * STRIP
+    slot = (lax.broadcasted_iota(jnp.int32, (rows, LANES), 1) - turn) & (LANES - 1)
+
+    def turned(x, dx):
+        return pltpu.roll(x, (turn + (-dx) % LANES) & (LANES - 1), 1)
+
+    return slot, turned
+
+
+def own_kernel(rates_ref, got_ref, cls_ref, gram_ref, prob_ref, mid_ref, out_ref, pert_ref, weight_ref, rate_ref):
     members = got_ref.shape[0]
     blank = jnp.zeros((TOP, LANES), F32)
 
@@ -211,7 +224,7 @@
             return tuple(a + high[dy] * near[dx] for a, (dy, dx) in zip(acc, FORWARD))
 
         acc = tuple(jnp.zeros((8, LANES), F32) for _ in FORWARD)
-        acc = lax.fori_loop(0, members, products, acc, unroll=4)
+        acc = lax.fori_loop(0, members, products, acc, unroll=16)
         for i, a in enumerate(acc):
             gram_ref[i, 8 * b : 8 * b + 8] = a
 
@@ -219,16 +232,22 @@
     coef = entries(lambda dy: rate_ref[HALO + dy : HALO + dy + 8])
     set_weights(weight_ref, coef, lambda i, dy: gram_ref[i, HALO + dy : HALO + dy + 8], 1.0 / (members - 1))
 
+    slot, turned = turning(8)
+
     def one_probe(p, _):
         start = TOP + HALO
-        mid_ref[p] = weighted(weight_ref, [prob_ref[p, start + dy : start + dy + 8] for dy in range(-HALO, HALO + 1)])
+        b = weighted(weight_ref, [prob_ref[p, start + dy : start + dy + 8] for dy in range(-HALO, HALO + 1)])
+        mid_ref[p] = turned(b, HALO - 3 * STRIP)
+        rest = jnp.where(slot < STRIP, turned(b, WIN + HALO), turned(b, 2 * WIN + HALO - STRIP))
+        rest = jnp.where(slot < 2 * STRIP, rest, pltpu.roll(lanes_by(rest, 2 * STRIP), HALO, 0))
+        out_ref[p, 2] = rest[:HALO]
         return 0
 
-    lax.fori_loop(0, members, one_probe, 0, unroll=8)
+    lax.fori_loop(0, members, one_probe, 0, unroll=16)
 
 
 def apply_kernel(
-    n_row, rates_ref, got_ref, cls_ref, below_ref, above_ref, own_ref, mid_ref, part_ref, out_ref,
+    n_row, rates_ref, got_ref, cls_ref, below_ref, above_ref, own_ref, mid_ref, part_ref, third_ref, out_ref,
     prob_ref, gram_ref, weight_ref, rate_ref,
 ):
     members = got_ref.shape[0]
@@ -236,7 +255,6 @@
     has_above = lax.axis_index("row") != 0
     blank = jnp.zeros((HALO, LANES), F32)
     sub = lax.broadcasted_iota(jnp.int32, (8, LANES), 0)
-    lane = lax.broadcasted_iota(jnp.int32, (8, LANES), 1)
     upper = sub < HALO
     crossing = [d for d in FORWARD if d[0] > 0]
 
@@ -284,26 +302,19 @@
         1.0 / (members - 1),
     )
 
-    turn = lax.axis_index("member") // LEV % (LANES // STRIP) * STRIP
-    slot = (lane - turn) & (LANES - 1)
-
-    def turned(x, dx):
-        return pltpu.roll(x, (turn + (-dx) % LANES) & (LANES - 1), 1)
+    slot, turned = turning(8)
 
     def one_probe(p, _):
         rows = [
             jnp.where(upper, prob_ref[p, TOP + dy : TOP + dy + 8], prob_ref[p, TOP + 8 + dy : TOP + dy + 16])
             for dy in range(-HALO, HALO + 1)
         ]
-        a, b = weighted(weight_ref, rows), mid_ref[p]
+        a = weighted(weight_ref, rows)
         first = jnp.where(slot < STRIP, turned(a, HALO), turned(a, HALO + 8))
         first = jnp.where(slot < 2 * STRIP, first, turned(a, HALO + 16))
-        first = jnp.where(slot < 3 * STRIP, first, turned(b, HALO - 3 * STRIP))
-        rest = jnp.where(slot < STRIP, turned(b, WIN + HALO), turned(b, 2 * WIN + HALO - STRIP))
-        rest = jnp.where(slot < 2 * STRIP, rest, pltpu.roll(lanes_by(rest, 2 * STRIP), HALO, 0))
+        first = jnp.where(slot < 3 * STRIP, first, mid_ref[p])
         out_ref[p, 0] = first[:HALO]
         out_ref[p, 1] = first[HALO:]
-        out_ref[p, 2] = rest[:HALO]
         return 0
 
     lax.fori_loop(0, members, one_probe, 0, unroll=8)
@@ -355,17 +366,15 @@
     def near(x):
         return pltpu.with_memory_space_constraint(x, pltpu.VMEM)
 
-    ends = (0, COLS // LANES - 1)
-    tile = [pl.BlockSpec((1, VARS, LEV, ROWS, LANES), functools.partial(lambda at, i: (0, 0, 0, 0, at), at)) for at in ends]
-    plane = [pl.BlockSpec((ROWS, LANES), functools.partial(lambda at, i: (0, at), at)) for at in ends]
+    end = pltpu.VMEM((VARS, LEV, ROWS, LANES), BF16)
     side = pl.pallas_call(
         side_kernel,
-        grid=(1,),
-        in_specs=tile + tile + plane,
+        in_specs=[pl.BlockSpec(memory_space=pl.ANY)] * 3,
         out_specs=vmem,
         out_shape=shape(((2 * LEV + 1) * ROWS, LANES), BF16),
+        scratch_shapes=[end, end, pltpu.VMEM((ROWS, LANES), jnp.int32), pltpu.SemaphoreType.DMA((3,))],
         name="side",
-    )(pert, pert, probes, probes, diff_class, diff_class)
+    )(pert, probes, diff_class)
     beside = lax.ppermute(side, "col", [(0, 1), (1, 0)])
 
     chunk, classes = shape((members, 2 * ROWS, LANES), BF16), shape((ROWS, LANES), F32)
@@ -401,11 +410,12 @@
 
     tall = shape((members, TALL, LANES), F32)
     weights = pltpu.VMEM((len(EVERY), 8, LANES), F32)
-    own, spread, mid = pl.pallas_call(
+    third = shape((members, VARS, HALO, LANES), F32)
+    own, spread, mid, part = pl.pallas_call(
         own_kernel,
         in_specs=[vmem] * 3,
-        out_specs=[vmem] * 3,
-        out_shape=[shape((len(FORWARD), ROWS, LANES), F32), tall, shape((members, 8, LANES), F32)],
+        out_specs=[vmem] * 4,
+        out_shape=[shape((len(FORWARD), ROWS, LANES), F32), tall, shape((members, 8, LANES), F32), third],
         scratch_shapes=[
             pltpu.VMEM((members, TOP + ROWS, LANES), F32),
             weights,
@@ -416,17 +426,17 @@
 
     part, spread = pl.pallas_call(
         functools.partial(apply_kernel, n_row),
-        in_specs=[vmem] * 8,
+        in_specs=[vmem] * 9,
         out_specs=[vmem] * 2,
-        out_shape=[shape((members, VARS, HALO, LANES), F32), tall],
-        input_output_aliases={7: 1},
+        out_shape=[third, tall],
+        input_output_aliases={7: 1, 8: 0},
         scratch_shapes=[
             pltpu.VMEM((len(FORWARD), 24, LANES), F32),
             weights,
             pltpu.VMEM((TALL, LANES), F32),
         ],
         name="apply",
-    )(near(rates), near(got), near(cls), near(below), near(above), near(own), near(mid), near(spread))
+    )(near(rates), near(got), near(cls), near(below), near(above), near(own), near(mid), near(spread), near(part))
 
     back = lax.all_to_all(part, "member", 0, 0, tiled=True)
 

time: 57.7 us -> 57.5 us (level)
  Pallas kernels: 7.74 us -> 6.99 us
  transfers between devices with their start and end apart: 3 -> 3, of which waited for: 1 -> 1; matrix products, arithmetic and copies ran while one was open for 0% -> 0% of each run, Pallas kernels for 7% -> 6%
where the time goes in v8:
time: 57.5 us; the launch traced here: 57.2 us
  blocking collectives  42.9 us (75%)
  Pallas kernels  6.99 us (12%)
  starting transfers between devices  4.93 us (9%)
  waiting for transfers between devices  2.37 us (4%)
    all_to_all x1, blocking collectives, body(): got = lax.all_to_all(chunks, 'member', 0, 0, tiled=True)  25.7 us
    all_to_all x1, blocking collectives, body(): back = lax.all_to_all(part, 'member', 0, 0, tiled=True)  17.2 us
    ppermute x1, starting transfers between devices, body(): lax.ppermute(up, 'row', [(i, (i - 1) % n_row) for i in range(n_row)])  2.81 us
    ppermute x1, waiting for transfers between devices, body(): lax.ppermute(dn, 'row', [(i, (i + 1) % n_row) for i in range(n_row)])  2.36 us
    ppermute x1, starting transfers between devices, body(): beside = lax.ppermute(side, 'col', [(0, 1), (1, 0)])  2.12 us
    pallas_call x1, Pallas kernels, body(): pl.pallas_call(functools.partial(apply_kernel, n_row), in_specs=[vmem] *...  1.97 us
    pallas_call x1, Pallas kernels, body(): pl.pallas_call(own_kernel, in_specs=[vmem] * 3, out_specs=[vmem] * 4, out...  1.96 us
    pallas_call x1, Pallas kernels, body(): pl.pallas_call(pack_kernel, in_specs=[smem] + [vmem] * 3, out_specs=[vmem...  1.31 us
  transfers between devices with their start and end apart: 3, of which 1 were waited for; matrix products, arithmetic and copies ran while one was open for 0% of the time, Pallas kernels for 6%

profile of v8, /device:TPU:1, one launch (start us, length us, event | category | flops | bytes accessed | tf_op | source)
XLA Modules:
  0.0 57.2 jit_solution(16557685197472157364)
XLA Ops:
  0.0 0.9 %side.1 = bf16[80,128]{1,0:T(8,128)(2,1)S(1)} custom-call(bf16[1,3,2,16,512]{4,3,2,1,0:T(8,128)(2,1)} %pert_ref.3, bf16[1,3,2,16,512]{4,3,2,1,0:T(8,128)(2,1)} %prob_ref.3, s32[16,512]{1,0:T(8,128)} %cls_ref.3), custom_call_target="tpu_custom_call" | custom-call | tf_op jit(solution)/shard_map/side/pallas_call | solution.py:370
  0.9 2.1 %collective-permute-start = (bf16[80,128]{1,0:T(8,128)(2,1)S(1)}, bf16[80,128]{1,0:T(8,128)(2,1)S(1)}, u32[]{:S(2)}, u32[]{:S(2)}) collective-permute-start(bf16[80,128]{1,0:T(8,128)(2,1)S(1)} %side.1), channel_id=1, source_target_pairs={{0,1},{1,0},{2,3},{3,2},{4,5},{5,4},{6,7},{7,6},{8,9},{9,8},{10,11... | collective-permute-start | bytes 61448 | tf_op jit(solution)/shard_map/ppermute | solution.py:378
  3.0 1.3 %pack.1 = (bf16[32,32,128]{2,1,0:T(8,128)(2,1)S(1)}, f32[16,128]{1,0:T(8,128)S(1)}, f32[8,128]{1,0:T(8,128)S(1)}) custom-call(f32[8]{0:T(128)} %rates_ref.1, bf16[1,3,2,16,512]{4,3,2,1,0:T(8,128)(2,1)} %pert_ref.3, bf16[1,3,2,16,512]{4,3,2,1,0:T(8,128)(2,1)} %prob_ref.3, s32[16,512]{1,0:T(8,128)} %cls_ref.3), custom_call_target="tpu_custom_call" | custom-call | tf_op jit(solution)/shard_map/pack/pallas_call | solution.py:381
  4.3 0.0 collective-permute-done.side_ref
  4.4 25.7 %all_to_all.10.got_ref = bf16[32,32,128]{2,1,0:T(8,128)(2,1)S(1)} all-to-all(bf16[32,32,128]{2,1,0:T(8,128)(2,1)S(1)} %get-tuple-element.20), channel_id=1, replica_groups=mesh['member'=32,'row'=4,'col'=2] {'member'}, dimensions={0} | all-to-all | bytes 524288 | tf_op jit(solution)/shard_map/all_to_all | solution.py:398
  30.1 2.8 %collective-permute-start.1 = (bf16[33,8,128]{2,1,0:T(8,128)(2,1)S(1)}, bf16[33,8,128]{2,1,0:T(8,128)(2,1)S(1)}, u32[]{:S(2)}, u32[]{:S(2)}) collective-permute-start(bf16[33,8,128]{2,1,0:T(8,128)(2,1)S(1)} %get-tuple-element.22), channel_id=1, source_target_pairs={{0,6},{2,0},{4,2},{6,4},{1,7},{3,1},{5,3},{7,5},{8,14},{10,8},{12,... | collective-permute-start | bytes 202760 | tf_op jit(solution)/shard_map/ppermute | solution.py:408
  32.9 0.0 collective-permute-start.2
  32.9 2.0 %own.1 = (f32[21,16,128]{2,1,0:T(8,128)S(1)}, f32[32,32,128]{2,1,0:T(8,128)S(1)}, f32[32,8,128]{2,1,0:T(8,128)S(1)}, f32[32,3,4,128]{3,2,1,0:T(4,128)S(1)}) custom-call(f32[8,128]{1,0:T(8,128)S(1)} %get-tuple-element.17.rates_ref, bf16[32,32,128]{2,1,0:T(8,128)(2,1)S(1)} %all_to_all.10.got_ref, f32[16,128]{1,0:T(8,128)S(1)} %get-tuple-element.21.cls_ref), custom_call_target="tpu_custom_call" | custom-call | tf_op jit(solution)/shard_map/own/pallas_call | solution.py:414
  34.9 0.0 collective-permute-done.1.below_ref
  34.9 2.4 %collective-permute-done.2.above_ref = bf16[33,8,128]{2,1,0:T(8,128)(2,1)S(1)} collective-permute-done((bf16[33,8,128]{2,1,0:T(8,128)(2,1)S(1)}, bf16[33,8,128]{2,1,0:T(8,128)(2,1)S(1)}, u32[]{:S(2)}, u32[]{:S(2)}) %collective-permute-start.2) | collective-permute-done | bytes 67616 | tf_op jit(solution)/shard_map/ppermute | solution.py:409
  37.3 2.0 %apply.1 = (f32[32,3,4,128]{3,2,1,0:T(4,128)S(1)}, f32[32,32,128]{2,1,0:T(8,128)S(1)}) custom-call(f32[8,128]{1,0:T(8,128)S(1)} %get-tuple-element.17.rates_ref, bf16[32,32,128]{2,1,0:T(8,128)(2,1)S(1)} %all_to_all.10.got_ref, f32[16,128]{1,0:T(8,128)S(1)} %get-tuple-element.21.cls_ref, ...), custom_call_target="tpu_custom_call", output_to_operand_aliasing={{1}: (7, {}), {0}: (8, {})} | custom-call | tf_op jit(solution)/shard_map/apply/pallas_call | solution.py:427
  39.2 17.2 %all_to_all.11.got_ref = f32[32,3,4,128]{3,2,1,0:T(4,128)S(1)} all-to-all(f32[32,3,4,128]{3,2,1,0:T(4,128)S(1)} %get-tuple-element.28), channel_id=1, replica_groups=mesh['member'=32,'row'=4,'col'=2] {'member'}, dimensions={0} | all-to-all | bytes 393216 | tf_op jit(solution)/shard_map/all_to_all | solution.py:441
  56.4 0.8 %unpack.1 = f32[1,3,2,16,512]{4,3,2,1,0:T(8,128)} custom-call(f32[32,3,4,128]{3,2,1,0:T(4,128)S(1)} %all_to_all.11.got_ref), custom_call_target="tpu_custom_call" | custom-call | tf_op jit(solution)/shard_map/unpack/pallas_call | solution.py:443
  (2 shorter events, 0.0 us)
Async XLA Ops:
  0.9 3.4 %collective-permute-start = (bf16[80,128]{1,0:T(8,128)(2,1)S(1)}, bf16[80,128]{1,0:T(8,128)(2,1)S(1)}, u32[]{:S(2)}, u32[]{:S(2)}) collective-permute-start(bf16[80,128]{1,0:T(8,128)(2,1)S(1)} %side.1), channel_id=1, source_target_pairs={{0,1},{1,0},{2,3},{3,2},{4,5},{5,4},{6,7},{7,6},{8,9},{9,8},{10,11... | collective-permute-start | bytes 61448 | tf_op jit(solution)/shard_map/ppermute | solution.py:378
  30.1 4.8 %collective-permute-start.1 = (bf16[33,8,128]{2,1,0:T(8,128)(2,1)S(1)}, bf16[33,8,128]{2,1,0:T(8,128)(2,1)S(1)}, u32[]{:S(2)}, u32[]{:S(2)}) collective-permute-start(bf16[33,8,128]{2,1,0:T(8,128)(2,1)S(1)} %get-tuple-element.22), channel_id=1, source_target_pairs={{0,6},{2,0},{4,2},{6,4},{1,7},{3,1},{5,3},{7,5},{8,14},{10,8},{12,... | collective-permute-start | bytes 202760 | tf_op jit(solution)/shard_map/ppermute | solution.py:408
  32.9 4.3 %collective-permute-start.2 = (bf16[33,8,128]{2,1,0:T(8,128)(2,1)S(1)}, bf16[33,8,128]{2,1,0:T(8,128)(2,1)S(1)}, u32[]{:S(2)}, u32[]{:S(2)}) collective-permute-start(bf16[33,8,128]{2,1,0:T(8,128)(2,1)S(1)} %get-tuple-element.23), channel_id=1, source_target_pairs={{0,2},{2,4},{4,6},{6,0},{1,3},{3,5},{5,7},{7,1},{8,10},{10,12},{12... | collective-permute-start | bytes 202760 | tf_op jit(solution)/shard_map/ppermute | solution.py:409

commit v9 on v8

--- a/solution.py
+++ b/solution.py
@@ -201,12 +201,16 @@
     return slot, turned
 
 
-def own_kernel(rates_ref, got_ref, cls_ref, gram_ref, prob_ref, mid_ref, out_ref, pert_ref, weight_ref, rate_ref):
+def own_kernel(
+    rates_ref, got_ref, cls_ref, gram_ref, prob_ref, mid_ref, out_ref, ends_ref, pert_ref, weight_ref, rate_ref
+):
     members = got_ref.shape[0]
     blank = jnp.zeros((TOP, LANES), F32)
+    upper = lax.broadcasted_iota(jnp.int32, (8, LANES), 0) < HALO
 
     def spread(m, _):
         tile = got_ref[m].astype(F32)
+        ends_ref[m] = jnp.where(upper, tile[0:8], pltpu.roll(tile[8:16], HALO, 0))
         pert_ref[m, 0:TOP] = blank
         for group, to in enumerate((0, 12, 4, 8)):
             pert_ref[m, TOP + to : TOP + to + HALO] = tile[8 * group : 8 * group + HALO]
@@ -247,10 +251,10 @@
 
 
 def apply_kernel(
-    n_row, rates_ref, got_ref, cls_ref, below_ref, above_ref, own_ref, mid_ref, part_ref, third_ref, out_ref,
+    n_row, rates_ref, ends_ref, cls_ref, below_ref, above_ref, own_ref, mid_ref, part_ref, third_ref, out_ref,
     prob_ref, gram_ref, weight_ref, rate_ref,
 ):
-    members = got_ref.shape[0]
+    members = ends_ref.shape[0]
     has_below = lax.axis_index("row") != n_row - 1
     has_above = lax.axis_index("row") != 0
     blank = jnp.zeros((HALO, LANES), F32)
@@ -259,12 +263,12 @@
     crossing = [d for d in FORWARD if d[0] > 0]
 
     def spread(m, acc):
-        tile = got_ref[m, :ROWS].astype(F32)
+        ends = ends_ref[m]
         below, above = below_ref[m].astype(F32), above_ref[m].astype(F32)
         prob_ref[m, TOP - HALO : TOP] = above[HALO:]
         prob_ref[m, TOP + ROWS : TOP + ROWS + HALO] = below[HALO:]
-        low = jnp.where(upper, tile[0:8], pltpu.roll(below, HALO, 0))
-        high = jnp.where(upper, above, pltpu.roll(tile[8:16], HALO, 0))
+        low = jnp.where(upper, ends, pltpu.roll(below, HALO, 0))
+        high = jnp.where(upper, above, ends)
         high = {dy: pltpu.roll(high, HALO + dy, 0) if dy < HALO else high for dy in range(1, HALO + 1)}
         near = {dx: lanes_by(low, dx) for dx in range(-HALO + 1, HALO)}
         return tuple(a + high[dy] * near[dx] for a, (dy, dx) in zip(acc, crossing))
@@ -304,20 +308,35 @@
 
     slot, turned = turning(8)
 
-    def one_probe(p, _):
+    def some_probes(i, _):
+        some = [2 * i + j for j in range(2)]
         rows = [
-            jnp.where(upper, prob_ref[p, TOP + dy : TOP + dy + 8], prob_ref[p, TOP + 8 + dy : TOP + dy + 16])
-            for dy in range(-HALO, HALO + 1)
+            [
+                jnp.where(upper, prob_ref[p, TOP + dy : TOP + dy + 8], prob_ref[p, TOP + 8 + dy : TOP + dy + 16])
+                for dy in range(-HALO, HALO + 1)
+            ]
+            for p in some
         ]
-        a = weighted(weight_ref, rows)
-        first = jnp.where(slot < STRIP, turned(a, HALO), turned(a, HALO + 8))
-        first = jnp.where(slot < 2 * STRIP, first, turned(a, HALO + 16))
-        first = jnp.where(slot < 3 * STRIP, first, mid_ref[p])
-        out_ref[p, 0] = first[:HALO]
-        out_ref[p, 1] = first[HALO:]
+        total = [None for p in some]
+        for dx in range(-HALO, HALO + 1):
+            part = [None for p in some]
+            for dy in range(-HALO + abs(dx), HALO - abs(dx) + 1):
+                weight = weight_ref[AT[(dy, dx)]]
+                for j in range(2):
+                    term = weight * rows[j][dy + HALO]
+                    part[j] = term if part[j] is None else part[j] + term
+            for j in range(2):
+                moved = lanes_by(part[j], dx)
+                total[j] = moved if total[j] is None else total[j] + moved
+        for p, a in zip(some, total):
+            first = jnp.where(slot < STRIP, turned(a, HALO), turned(a, HALO + 8))
+            first = jnp.where(slot < 2 * STRIP, first, turned(a, HALO + 16))
+            first = jnp.where(slot < 3 * STRIP, first, mid_ref[p])
+            out_ref[p, 0] = first[:HALO]
+            out_ref[p, 1] = first[HALO:]
         return 0
 
-    lax.fori_loop(0, members, one_probe, 0, unroll=8)
+    lax.fori_loop(0, members // 2, some_probes, 0, unroll=8)
 
 
 def unpack_kernel(got_ref, out_ref, tile_ref, sems):
@@ -411,11 +430,12 @@
     tall = shape((members, TALL, LANES), F32)
     weights = pltpu.VMEM((len(EVERY), 8, LANES), F32)
     third = shape((members, VARS, HALO, LANES), F32)
-    own, spread, mid, part = pl.pallas_call(
+    eight = shape((members, 8, LANES), F32)
+    own, spread, mid, part, ends = pl.pallas_call(
         own_kernel,
         in_specs=[vmem] * 3,
-        out_specs=[vmem] * 4,
-        out_shape=[shape((len(FORWARD), ROWS, LANES), F32), tall, shape((members, 8, LANES), F32), third],
+        out_specs=[vmem] * 5,
+        out_shape=[shape((len(FORWARD), ROWS, LANES), F32), tall, eight, third, eight],
         scratch_shapes=[
             pltpu.VMEM((members, TOP + ROWS, LANES), F32),
             weights,
@@ -436,7 +456,7 @@
             pltpu.VMEM((TALL, LANES), F32),
         ],
         name="apply",
-    )(near(rates), near(got), near(cls), near(below), near(above), near(own), near(mid), near(spread), near(part))
+    )(near(rates), near(ends), near(cls), near(below), near(above), near(own), near(mid), near(spread), near(part))
 
     back = lax.all_to_all(part, "member", 0, 0, tiled=True)
 

time: 57.5 us -> 57.3 us (level)
  no operation moved by 1% of the time
where the time goes in v9:
time: 57.3 us; the launch traced here: 57 us
  blocking collectives  42.9 us (75%)
  Pallas kernels  6.81 us (12%)
  starting transfers between devices  4.93 us (9%)
  waiting for transfers between devices  2.35 us (4%)
    all_to_all x1, blocking collectives, body(): got = lax.all_to_all(chunks, 'member', 0, 0, tiled=True)  25.7 us
    all_to_all x1, blocking collectives, body(): back = lax.all_to_all(part, 'member', 0, 0, tiled=True)  17.2 us
    ppermute x1, starting transfers between devices, body(): lax.ppermute(up, 'row', [(i, (i - 1) % n_row) for i in range(n_row)])  2.81 us
    ppermute x1, waiting for transfers between devices, body(): lax.ppermute(dn, 'row', [(i, (i + 1) % n_row) for i in range(n_row)])  2.35 us
    ppermute x1, starting transfers between devices, body(): beside = lax.ppermute(side, 'col', [(0, 1), (1, 0)])  2.12 us
    pallas_call x1, Pallas kernels, body(): pl.pallas_call(own_kernel, in_specs=[vmem] * 3, out_specs=[vmem] * 5, out...  1.98 us
    pallas_call x1, Pallas kernels, body(): pl.pallas_call(functools.partial(apply_kernel, n_row), in_specs=[vmem] *...  1.78 us
    pallas_call x1, Pallas kernels, body(): pl.pallas_call(pack_kernel, in_specs=[smem] + [vmem] * 3, out_specs=[vmem...  1.31 us
  transfers between devices with their start and end apart: 3, of which 1 were waited for; matrix products, arithmetic and copies ran while one was open for 0% of the time, Pallas kernels for 6%

profile of v9, /device:TPU:1, one launch (start us, length us, event | category | flops | bytes accessed | tf_op | source)
XLA Modules:
  0.0 57.0 jit_solution(15542327158715024937)
XLA Ops:
  0.0 0.9 %side.1 = bf16[80,128]{1,0:T(8,128)(2,1)S(1)} custom-call(bf16[1,3,2,16,512]{4,3,2,1,0:T(8,128)(2,1)} %pert_ref.3, bf16[1,3,2,16,512]{4,3,2,1,0:T(8,128)(2,1)} %prob_ref.3, s32[16,512]{1,0:T(8,128)} %cls_ref.3), custom_call_target="tpu_custom_call" | custom-call | tf_op jit(solution)/shard_map/side/pallas_call | solution.py:389
  0.9 2.1 %collective-permute-start = (bf16[80,128]{1,0:T(8,128)(2,1)S(1)}, bf16[80,128]{1,0:T(8,128)(2,1)S(1)}, u32[]{:S(2)}, u32[]{:S(2)}) collective-permute-start(bf16[80,128]{1,0:T(8,128)(2,1)S(1)} %side.1), channel_id=1, source_target_pairs={{0,1},{1,0},{2,3},{3,2},{4,5},{5,4},{6,7},{7,6},{8,9},{9,8},{10,11... | collective-permute-start | bytes 61448 | tf_op jit(solution)/shard_map/ppermute | solution.py:397
  3.0 1.3 %pack.1 = (bf16[32,32,128]{2,1,0:T(8,128)(2,1)S(1)}, f32[16,128]{1,0:T(8,128)S(1)}, f32[8,128]{1,0:T(8,128)S(1)}) custom-call(f32[8]{0:T(128)} %rates_ref.1, bf16[1,3,2,16,512]{4,3,2,1,0:T(8,128)(2,1)} %pert_ref.3, bf16[1,3,2,16,512]{4,3,2,1,0:T(8,128)(2,1)} %prob_ref.3, s32[16,512]{1,0:T(8,128)} %cls_ref.3), custom_call_target="tpu_custom_call" | custom-call | tf_op jit(solution)/shard_map/pack/pallas_call | solution.py:400
  4.3 0.0 collective-permute-done.side_ref
  4.4 25.7 %all_to_all.10.got_ref = bf16[32,32,128]{2,1,0:T(8,128)(2,1)S(1)} all-to-all(bf16[32,32,128]{2,1,0:T(8,128)(2,1)S(1)} %get-tuple-element.21), channel_id=1, replica_groups=mesh['member'=32,'row'=4,'col'=2] {'member'}, dimensions={0} | all-to-all | bytes 524288 | tf_op jit(solution)/shard_map/all_to_all | solution.py:417
  30.1 2.8 %collective-permute-start.1 = (bf16[33,8,128]{2,1,0:T(8,128)(2,1)S(1)}, bf16[33,8,128]{2,1,0:T(8,128)(2,1)S(1)}, u32[]{:S(2)}, u32[]{:S(2)}) collective-permute-start(bf16[33,8,128]{2,1,0:T(8,128)(2,1)S(1)} %get-tuple-element.24), channel_id=1, source_target_pairs={{0,6},{2,0},{4,2},{6,4},{1,7},{3,1},{5,3},{7,5},{8,14},{10,8},{12,... | collective-permute-start | bytes 202760 | tf_op jit(solution)/shard_map/ppermute | solution.py:427
  32.9 0.0 collective-permute-start.2
  32.9 2.0 %own.1 = (f32[21,16,128]{2,1,0:T(8,128)S(1)}, f32[32,32,128]{2,1,0:T(8,128)S(1)}, f32[32,8,128]{2,1,0:T(8,128)S(1)}, f32[32,3,4,128]{3,2,1,0:T(4,128)S(1)}, f32[32,8,128]{2,1,0:T(8,128)S(1)}) custom-call(f32[8,128]{1,0:T(8,128)S(1)} %get-tuple-element.18.rates_ref, bf16[32,32,128]{2,1,0:T(8,128)(2,1)S(1)} %all_to_all.10.got_ref, ...), custom_call_target="tpu_custom_call" | custom-call | tf_op jit(solution)/shard_map/own/pallas_call | solution.py:434
  34.9 0.0 collective-permute-done.1.below_ref
  34.9 2.3 %collective-permute-done.2.above_ref = bf16[33,8,128]{2,1,0:T(8,128)(2,1)S(1)} collective-permute-done((bf16[33,8,128]{2,1,0:T(8,128)(2,1)S(1)}, bf16[33,8,128]{2,1,0:T(8,128)(2,1)S(1)}, u32[]{:S(2)}, u32[]{:S(2)}) %collective-permute-start.2) | collective-permute-done | bytes 67616 | tf_op jit(solution)/shard_map/ppermute | solution.py:428
  37.3 1.8 %apply.1 = (f32[32,3,4,128]{3,2,1,0:T(4,128)S(1)}, f32[32,32,128]{2,1,0:T(8,128)S(1)}) custom-call(f32[8,128]{1,0:T(8,128)S(1)} %get-tuple-element.18.rates_ref, f32[32,8,128]{2,1,0:T(8,128)S(1)} %get-tuple-element.23.ends_ref, f32[16,128]{1,0:T(8,128)S(1)} %get-tuple-element.22.cls_ref, ...), custom_call_target="tpu_custom_call", output_to_operand_aliasing={{1}: (7, {}), {0}: (8, {})} | custom-call | tf_op jit(solution)/shard_map/apply/pallas_call | solution.py:447
  39.1 17.2 %all_to_all.11.got_ref = f32[32,3,4,128]{3,2,1,0:T(4,128)S(1)} all-to-all(f32[32,3,4,128]{3,2,1,0:T(4,128)S(1)} %get-tuple-element.30), channel_id=1, replica_groups=mesh['member'=32,'row'=4,'col'=2] {'member'}, dimensions={0} | all-to-all | bytes 393216 | tf_op jit(solution)/shard_map/all_to_all | solution.py:461
  56.2 0.8 %unpack.1 = f32[1,3,2,16,512]{4,3,2,1,0:T(8,128)} custom-call(f32[32,3,4,128]{3,2,1,0:T(4,128)S(1)} %all_to_all.11.got_ref), custom_call_target="tpu_custom_call" | custom-call | tf_op jit(solution)/shard_map/unpack/pallas_call | solution.py:463
  (2 shorter events, 0.0 us)
Async XLA Ops:
  0.9 3.4 %collective-permute-start = (bf16[80,128]{1,0:T(8,128)(2,1)S(1)}, bf16[80,128]{1,0:T(8,128)(2,1)S(1)}, u32[]{:S(2)}, u32[]{:S(2)}) collective-permute-start(bf16[80,128]{1,0:T(8,128)(2,1)S(1)} %side.1), channel_id=1, source_target_pairs={{0,1},{1,0},{2,3},{3,2},{4,5},{5,4},{6,7},{7,6},{8,9},{9,8},{10,11... | collective-permute-start | bytes 61448 | tf_op jit(solution)/shard_map/ppermute | solution.py:397
  30.1 4.8 %collective-permute-start.1 = (bf16[33,8,128]{2,1,0:T(8,128)(2,1)S(1)}, bf16[33,8,128]{2,1,0:T(8,128)(2,1)S(1)}, u32[]{:S(2)}, u32[]{:S(2)}) collective-permute-start(bf16[33,8,128]{2,1,0:T(8,128)(2,1)S(1)} %get-tuple-element.24), channel_id=1, source_target_pairs={{0,6},{2,0},{4,2},{6,4},{1,7},{3,1},{5,3},{7,5},{8,14},{10,8},{12,... | collective-permute-start | bytes 202760 | tf_op jit(solution)/shard_map/ppermute | solution.py:427
  32.9 4.3 %collective-permute-start.2 = (bf16[33,8,128]{2,1,0:T(8,128)(2,1)S(1)}, bf16[33,8,128]{2,1,0:T(8,128)(2,1)S(1)}, u32[]{:S(2)}, u32[]{:S(2)}) collective-permute-start(bf16[33,8,128]{2,1,0:T(8,128)(2,1)S(1)} %get-tuple-element.25), channel_id=1, source_target_pairs={{0,2},{2,4},{4,6},{6,0},{1,3},{3,5},{5,7},{7,1},{8,10},{10,12},{12... | collective-permute-start | bytes 202760 | tf_op jit(solution)/shard_map/ppermute | solution.py:428

commit v10 on v9

--- a/solution.py
+++ b/solution.py
@@ -201,16 +201,12 @@
     return slot, turned
 
 
-def own_kernel(
-    rates_ref, got_ref, cls_ref, gram_ref, prob_ref, mid_ref, out_ref, ends_ref, pert_ref, weight_ref, rate_ref
-):
+def own_kernel(rates_ref, got_ref, cls_ref, gram_ref, prob_ref, mid_ref, out_ref, pert_ref, weight_ref, rate_ref):
     members = got_ref.shape[0]
     blank = jnp.zeros((TOP, LANES), F32)
-    upper = lax.broadcasted_iota(jnp.int32, (8, LANES), 0) < HALO
 
     def spread(m, _):
         tile = got_ref[m].astype(F32)
-        ends_ref[m] = jnp.where(upper, tile[0:8], pltpu.roll(tile[8:16], HALO, 0))
         pert_ref[m, 0:TOP] = blank
         for group, to in enumerate((0, 12, 4, 8)):
             pert_ref[m, TOP + to : TOP + to + HALO] = tile[8 * group : 8 * group + HALO]
@@ -251,10 +247,10 @@
 
 
 def apply_kernel(
-    n_row, rates_ref, ends_ref, cls_ref, below_ref, above_ref, own_ref, mid_ref, part_ref, third_ref, out_ref,
+    n_row, rates_ref, got_ref, cls_ref, below_ref, above_ref, own_ref, mid_ref, part_ref, third_ref, out_ref,
     prob_ref, gram_ref, weight_ref, rate_ref,
 ):
-    members = ends_ref.shape[0]
+    members = got_ref.shape[0]
     has_below = lax.axis_index("row") != n_row - 1
     has_above = lax.axis_index("row") != 0
     blank = jnp.zeros((HALO, LANES), F32)
@@ -263,12 +259,12 @@
     crossing = [d for d in FORWARD if d[0] > 0]
 
     def spread(m, acc):
-        ends = ends_ref[m]
+        tile = got_ref[m, :ROWS].astype(F32)
         below, above = below_ref[m].astype(F32), above_ref[m].astype(F32)
         prob_ref[m, TOP - HALO : TOP] = above[HALO:]
         prob_ref[m, TOP + ROWS : TOP + ROWS + HALO] = below[HALO:]
-        low = jnp.where(upper, ends, pltpu.roll(below, HALO, 0))
-        high = jnp.where(upper, above, ends)
+        low = jnp.where(upper, tile[0:8], pltpu.roll(below, HALO, 0))
+        high = jnp.where(upper, above, pltpu.roll(tile[8:16], HALO, 0))
         high = {dy: pltpu.roll(high, HALO + dy, 0) if dy < HALO else high for dy in range(1, HALO + 1)}
         near = {dx: lanes_by(low, dx) for dx in range(-HALO + 1, HALO)}
         return tuple(a + high[dy] * near[dx] for a, (dy, dx) in zip(acc, crossing))
@@ -430,12 +426,11 @@
     tall = shape((members, TALL, LANES), F32)
     weights = pltpu.VMEM((len(EVERY), 8, LANES), F32)
     third = shape((members, VARS, HALO, LANES), F32)
-    eight = shape((members, 8, LANES), F32)
-    own, spread, mid, part, ends = pl.pallas_call(
+    own, spread, mid, part = pl.pallas_call(
         own_kernel,
         in_specs=[vmem] * 3,
-        out_specs=[vmem] * 5,
-        out_shape=[shape((len(FORWARD), ROWS, LANES), F32), tall, eight, third, eight],
+        out_specs=[vmem] * 4,
+        out_shape=[shape((len(FORWARD), ROWS, LANES), F32), tall, shape((members, 8, LANES), F32), third],
         scratch_shapes=[
             pltpu.VMEM((members, TOP + ROWS, LANES), F32),
             weights,
@@ -456,7 +451,7 @@
             pltpu.VMEM((TALL, LANES), F32),
         ],
         name="apply",
-    )(near(rates), near(ends), near(cls), near(below), near(above), near(own), near(mid), near(spread), near(part))
+    )(near(rates), near(got), near(cls), near(below), near(above), near(own), near(mid), near(spread), near(part))
 
     back = lax.all_to_all(part, "member", 0, 0, tiled=True)
 

time: 57.3 us -> 57.2 us (level)
  no operation moved by 1% of the time
where the time goes in v10:
time: 57.2 us; the launch traced here: 57 us
  blocking collectives  42.9 us (75%)
  Pallas kernels  6.75 us (12%)
  starting transfers between devices  4.93 us (9%)
  waiting for transfers between devices  2.37 us (4%)
    all_to_all x1, blocking collectives, body(): got = lax.all_to_all(chunks, 'member', 0, 0, tiled=True)  25.7 us
    all_to_all x1, blocking collectives, body(): back = lax.all_to_all(part, 'member', 0, 0, tiled=True)  17.2 us
    ppermute x1, starting transfers between devices, body(): lax.ppermute(up, 'row', [(i, (i - 1) % n_row) for i in range(n_row)])  2.81 us
    ppermute x1, waiting for transfers between devices, body(): lax.ppermute(dn, 'row', [(i, (i + 1) % n_row) for i in range(n_row)])  2.36 us
    ppermute x1, starting transfers between devices, body(): beside = lax.ppermute(side, 'col', [(0, 1), (1, 0)])  2.12 us
    pallas_call x1, Pallas kernels, body(): pl.pallas_call(own_kernel, in_specs=[vmem] * 3, out_specs=[vmem] * 4, out...  1.96 us
    pallas_call x1, Pallas kernels, body(): pl.pallas_call(functools.partial(apply_kernel, n_row), in_specs=[vmem] *...  1.73 us
    pallas_call x1, Pallas kernels, body(): pl.pallas_call(pack_kernel, in_specs=[smem] + [vmem] * 3, out_specs=[vmem...  1.31 us
  transfers between devices with their start and end apart: 3, of which 1 were waited for; matrix products, arithmetic and copies ran while one was open for 0% of the time, Pallas kernels for 6%

profile of v10, /device:TPU:1, one launch (start us, length us, event | category | flops | bytes accessed | tf_op | source)
XLA Modules:
  0.0 57.0 jit_solution(12474240378839241062)
XLA Ops:
  0.0 0.9 %side.1 = bf16[80,128]{1,0:T(8,128)(2,1)S(1)} custom-call(bf16[1,3,2,16,512]{4,3,2,1,0:T(8,128)(2,1)} %pert_ref.3, bf16[1,3,2,16,512]{4,3,2,1,0:T(8,128)(2,1)} %prob_ref.3, s32[16,512]{1,0:T(8,128)} %cls_ref.3), custom_call_target="tpu_custom_call" | custom-call | tf_op jit(solution)/shard_map/side/pallas_call | solution.py:385
  0.9 2.1 %collective-permute-start = (bf16[80,128]{1,0:T(8,128)(2,1)S(1)}, bf16[80,128]{1,0:T(8,128)(2,1)S(1)}, u32[]{:S(2)}, u32[]{:S(2)}) collective-permute-start(bf16[80,128]{1,0:T(8,128)(2,1)S(1)} %side.1), channel_id=1, source_target_pairs={{0,1},{1,0},{2,3},{3,2},{4,5},{5,4},{6,7},{7,6},{8,9},{9,8},{10,11... | collective-permute-start | bytes 61448 | tf_op jit(solution)/shard_map/ppermute | solution.py:393
  3.0 1.3 %pack.1 = (bf16[32,32,128]{2,1,0:T(8,128)(2,1)S(1)}, f32[16,128]{1,0:T(8,128)S(1)}, f32[8,128]{1,0:T(8,128)S(1)}) custom-call(f32[8]{0:T(128)} %rates_ref.1, bf16[1,3,2,16,512]{4,3,2,1,0:T(8,128)(2,1)} %pert_ref.3, bf16[1,3,2,16,512]{4,3,2,1,0:T(8,128)(2,1)} %prob_ref.3, s32[16,512]{1,0:T(8,128)} %cls_ref.3), custom_call_target="tpu_custom_call" | custom-call | tf_op jit(solution)/shard_map/pack/pallas_call | solution.py:396
  4.3 0.0 collective-permute-done.side_ref
  4.4 25.7 %all_to_all.10.got_ref = bf16[32,32,128]{2,1,0:T(8,128)(2,1)S(1)} all-to-all(bf16[32,32,128]{2,1,0:T(8,128)(2,1)S(1)} %get-tuple-element.20), channel_id=1, replica_groups=mesh['member'=32,'row'=4,'col'=2] {'member'}, dimensions={0} | all-to-all | bytes 524288 | tf_op jit(solution)/shard_map/all_to_all | solution.py:413
  30.1 2.8 %collective-permute-start.1 = (bf16[33,8,128]{2,1,0:T(8,128)(2,1)S(1)}, bf16[33,8,128]{2,1,0:T(8,128)(2,1)S(1)}, u32[]{:S(2)}, u32[]{:S(2)}) collective-permute-start(bf16[33,8,128]{2,1,0:T(8,128)(2,1)S(1)} %get-tuple-element.22), channel_id=1, source_target_pairs={{0,6},{2,0},{4,2},{6,4},{1,7},{3,1},{5,3},{7,5},{8,14},{10,8},{12,... | collective-permute-start | bytes 202760 | tf_op jit(solution)/shard_map/ppermute | solution.py:423
  32.9 0.0 collective-permute-start.2
  32.9 2.0 %own.1 = (f32[21,16,128]{2,1,0:T(8,128)S(1)}, f32[32,32,128]{2,1,0:T(8,128)S(1)}, f32[32,8,128]{2,1,0:T(8,128)S(1)}, f32[32,3,4,128]{3,2,1,0:T(4,128)S(1)}) custom-call(f32[8,128]{1,0:T(8,128)S(1)} %get-tuple-element.17.rates_ref, bf16[32,32,128]{2,1,0:T(8,128)(2,1)S(1)} %all_to_all.10.got_ref, f32[16,128]{1,0:T(8,128)S(1)} %get-tuple-element.21.cls_ref), custom_call_target="tpu_custom_call" | custom-call | tf_op jit(solution)/shard_map/own/pallas_call | solution.py:429
  34.9 0.0 collective-permute-done.1.below_ref
  34.9 2.4 %collective-permute-done.2.above_ref = bf16[33,8,128]{2,1,0:T(8,128)(2,1)S(1)} collective-permute-done((bf16[33,8,128]{2,1,0:T(8,128)(2,1)S(1)}, bf16[33,8,128]{2,1,0:T(8,128)(2,1)S(1)}, u32[]{:S(2)}, u32[]{:S(2)}) %collective-permute-start.2) | collective-permute-done | bytes 67616 | tf_op jit(solution)/shard_map/ppermute | solution.py:424
  37.3 1.7 %apply.1 = (f32[32,3,4,128]{3,2,1,0:T(4,128)S(1)}, f32[32,32,128]{2,1,0:T(8,128)S(1)}) custom-call(f32[8,128]{1,0:T(8,128)S(1)} %get-tuple-element.17.rates_ref, bf16[32,32,128]{2,1,0:T(8,128)(2,1)S(1)} %all_to_all.10.got_ref, f32[16,128]{1,0:T(8,128)S(1)} %get-tuple-element.21.cls_ref, ...), custom_call_target="tpu_custom_call", output_to_operand_aliasing={{1}: (7, {}), {0}: (8, {})} | custom-call | tf_op jit(solution)/shard_map/apply/pallas_call | solution.py:442
  39.0 17.2 %all_to_all.11.got_ref = f32[32,3,4,128]{3,2,1,0:T(4,128)S(1)} all-to-all(f32[32,3,4,128]{3,2,1,0:T(4,128)S(1)} %get-tuple-element.28), channel_id=1, replica_groups=mesh['member'=32,'row'=4,'col'=2] {'member'}, dimensions={0} | all-to-all | bytes 393216 | tf_op jit(solution)/shard_map/all_to_all | solution.py:456
  56.2 0.8 %unpack.1 = f32[1,3,2,16,512]{4,3,2,1,0:T(8,128)} custom-call(f32[32,3,4,128]{3,2,1,0:T(4,128)S(1)} %all_to_all.11.got_ref), custom_call_target="tpu_custom_call" | custom-call | tf_op jit(solution)/shard_map/unpack/pallas_call | solution.py:458
  (2 shorter events, 0.0 us)
Async XLA Ops:
  0.9 3.4 %collective-permute-start = (bf16[80,128]{1,0:T(8,128)(2,1)S(1)}, bf16[80,128]{1,0:T(8,128)(2,1)S(1)}, u32[]{:S(2)}, u32[]{:S(2)}) collective-permute-start(bf16[80,128]{1,0:T(8,128)(2,1)S(1)} %side.1), channel_id=1, source_target_pairs={{0,1},{1,0},{2,3},{3,2},{4,5},{5,4},{6,7},{7,6},{8,9},{9,8},{10,11... | collective-permute-start | bytes 61448 | tf_op jit(solution)/shard_map/ppermute | solution.py:393
  30.1 4.8 %collective-permute-start.1 = (bf16[33,8,128]{2,1,0:T(8,128)(2,1)S(1)}, bf16[33,8,128]{2,1,0:T(8,128)(2,1)S(1)}, u32[]{:S(2)}, u32[]{:S(2)}) collective-permute-start(bf16[33,8,128]{2,1,0:T(8,128)(2,1)S(1)} %get-tuple-element.22), channel_id=1, source_target_pairs={{0,6},{2,0},{4,2},{6,4},{1,7},{3,1},{5,3},{7,5},{8,14},{10,8},{12,... | collective-permute-start | bytes 202760 | tf_op jit(solution)/shard_map/ppermute | solution.py:423
  32.9 4.3 %collective-permute-start.2 = (bf16[33,8,128]{2,1,0:T(8,128)(2,1)S(1)}, bf16[33,8,128]{2,1,0:T(8,128)(2,1)S(1)}, u32[]{:S(2)}, u32[]{:S(2)}) collective-permute-start(bf16[33,8,128]{2,1,0:T(8,128)(2,1)S(1)} %get-tuple-element.23), channel_id=1, source_target_pairs={{0,2},{2,4},{4,6},{6,0},{1,3},{3,5},{5,7},{7,1},{8,10},{10,12},{12... | collective-permute-start | bytes 202760 | tf_op jit(solution)/shard_map/ppermute | solution.py:424
